TPU v7x, 32 devices: a whole 2x2x4 slice. The times are simulated.
32 devices in a mesh: ctx: 8 (over z, y), head: 4 (over x, core).
Axes of the slice: x: 2, y: 2, z: 4, core: 2. Of those that a mesh axis runs over, the one named last changes fastest.
Arguments:
- queries: bfloat16 [4096, 16, 128], P('ctx', 'head'), may hold values from -16 to 16
- keys: bfloat16 [4096, 1, 128], P('ctx'), may hold values from -6 to 6
- values: bfloat16 [4096, 1, 128], P('ctx'), may hold values from -6 to 6
- d_out: bfloat16 [4096, 16, 128], P('ctx', 'head'), may hold values from -1.796875 to 1.796875
- block_pos: int32 [4, 8], replicated, may hold values from 0 to 7, each once within a row
- block_mask: int32 [4, 8, 8], replicated, may hold values 0 or 1
Outputs:
- d_queries: bfloat16 [4096, 16, 128], P('ctx', 'head')
- d_keys: bfloat16 [4096, 1, 128], P('ctx')
- d_values: bfloat16 [4096, 1, 128], P('ctx')
Inputs may be any that keep to these rules, and one draw needn't show every extreme that they name: `block_pos`: each row holds each of the 8 block numbers once. `block_mask`: only entries [s, i, i2] with i2 < i are read.
All inputs are finite; a program needn't handle non-finite values.
Results may differ from a plain program's by a relative error of at most 0.0075.
Values may be sent and summed in bfloat16 or wider, within the bound.
No kernel may reach another device: no remote copies, remote signals or barrier semaphores. Data moves between devices by JAX's collectives and lax.ppermute only.
A program may use at most 64 MiB of HBM per device.

v0:
```python
import jax
import jax.numpy as jnp
from jax import lax
from jax.sharding import PartitionSpec as P

GROUP = 16
BLK = 128
SEQS = 4
QB_DEV = 4


def shifted(value, axis, steps):
    count = lax.axis_size(axis)
    pairs = [(source, (source + steps) % count) for source in range(count)]
    return lax.ppermute(value, axis, pairs)


def contract_last(left, right):
    return lax.dot_general(
        left, right, (((1,), (1,)), ((), ())), preferred_element_type=jnp.float32
    )


def contract_first(left, right):
    return lax.dot_general(
        left, right, (((0,), (0,)), ((), ())), preferred_element_type=jnp.float32
    )


def pass_keys(key_pair):
    return shifted(key_pair, "ctx", SEQS)


def send_sums(key_sums):
    return shifted(key_sums, "ctx", SEQS)


def per_device(queries, keys, values, d_out, block_pos, block_mask):
    cycle_members = lax.axis_size("ctx") // SEQS
    head_dim = queries.shape[2]
    score_scale = head_dim ** (-0.5)
    shard_tokens = queries.shape[0]
    local_heads = queries.shape[1]
    kv_count = keys.shape[1]
    kv_index = lax.axis_index("head") * local_heads // GROUP
    key_local = lax.dynamic_index_in_dim(keys, kv_index, 1, keepdims=False)
    value_local = lax.dynamic_index_in_dim(values, kv_index, 1, keepdims=False)
    row_total = shard_tokens * local_heads
    query_rows = queries.reshape(row_total, head_dim)
    grad_rows = d_out.reshape(row_total, head_dim)
    own_pair = jnp.stack([key_local, value_local])
    ctx_index = lax.axis_index("ctx")
    seq_id = ctx_index % SEQS
    member = ctx_index // SEQS
    order_row = lax.dynamic_index_in_dim(block_pos, seq_id, 0, keepdims=False)
    mask_table = lax.dynamic_index_in_dim(block_mask, seq_id, 0, keepdims=False)

    def blocks_of(owner_member):
        return lax.dynamic_slice_in_dim(order_row, owner_member % cycle_members * QB_DEV, QB_DEV)

    query_blocks = blocks_of(member)
    query_offset = lax.broadcasted_iota(jnp.int32, (1, BLK, 1, 1, 1), 1)
    key_offset = lax.broadcasted_iota(jnp.int32, (1, 1, 1, 1, BLK), 4)
    causal = key_offset <= query_offset

    def hop_mask(owner_member):
        key_blocks = blocks_of(owner_member)
        query_ids = query_blocks[:, None]
        key_ids = key_blocks[None, :]
        entries = mask_table[query_ids, key_ids]
        earlier = jnp.logical_and(key_ids < query_ids, entries == 1)
        same = query_ids == key_ids
        allowed = jnp.logical_or(
            earlier[:, None, None, :, None], jnp.logical_and(same[:, None, None, :, None], causal)
        )
        allowed = jnp.broadcast_to(allowed, (QB_DEV, BLK, local_heads, QB_DEV, BLK))
        active = jnp.any(jnp.logical_or(earlier, same))
        return (allowed.reshape(row_total, shard_tokens), active)

    def masked_logits(key_pair, allowed):
        logits = contract_last(query_rows, key_pair[0]) * score_scale
        return jnp.where(allowed, logits, -jnp.inf)

    def add_stats(running, key_pair, owner_member):
        allowed, active = hop_mask(owner_member)

        def update(running):
            maxima, totals, weighted = running
            logits = masked_logits(key_pair, allowed)
            dprob_rows = contract_last(grad_rows, key_pair[1])
            new_max = jnp.maximum(maxima, jnp.max(logits, axis=1))
            factor = jnp.exp(maxima - new_max)
            exp_rows = jnp.exp(logits - new_max[:, None])
            return (
                new_max,
                totals * factor + jnp.sum(exp_rows, axis=1),
                weighted * factor + jnp.sum(exp_rows * dprob_rows, axis=1),
            )

        return lax.cond(active, update, lambda kept: kept, running)

    kept_pairs = None
    stats = (
        jnp.full((row_total,), -jnp.inf, jnp.float32),
        jnp.zeros((row_total,), jnp.float32),
        jnp.zeros((row_total,), jnp.float32),
    )
    stats = add_stats(stats, own_pair, member)

    def one_way(hop_index, loop_state):
        stats, key_pair, kept_pairs = loop_state
        key_pair = pass_keys(key_pair)
        stats = add_stats(stats, key_pair, member - hop_index - 1)
        return (stats, key_pair, kept_pairs)

    stats, last_pair, kept_pairs = lax.fori_loop(
        0, cycle_members - 1, one_way, (stats, own_pair, kept_pairs)
    )
    maxima, totals, weighted = stats
    log_sums = maxima + jnp.log(totals)
    deltas = weighted / totals

    def add_grads(running, key_pair, owner_member):
        allowed, active = hop_mask(owner_member)

        def update(running):
            query_grad, key_sums = running
            logits = masked_logits(key_pair, allowed)
            prob_rows = jnp.exp(logits - log_sums[:, None])
            dprob_rows = contract_last(grad_rows, key_pair[1])
            dscore = (prob_rows * (dprob_rows - deltas[:, None])).astype(jnp.bfloat16)
            query_grad = query_grad + jnp.dot(
                dscore, key_pair[0], preferred_element_type=jnp.float32
            )
            key_add = contract_first(dscore, query_rows)
            value_add = contract_first(prob_rows.astype(jnp.bfloat16), grad_rows)
            return (query_grad, key_sums + jnp.stack([key_add, value_add]))

        return lax.cond(active, update, lambda kept: kept, running)

    query_grad = jnp.zeros((row_total, head_dim), jnp.float32)
    key_sums = jnp.zeros((2, shard_tokens, head_dim), jnp.float32)

    def resend_step(hop_index, loop_state):
        query_grad, key_sums, key_pair = loop_state
        query_grad, key_sums = add_grads((query_grad, key_sums), key_pair, member - hop_index)
        return (query_grad, send_sums(key_sums), pass_keys(key_pair))

    query_grad, key_sums, key_pair = lax.fori_loop(
        0, cycle_members - 1, resend_step, (query_grad, key_sums, own_pair)
    )
    query_grad, key_sums = add_grads((query_grad, key_sums), key_pair, member - (cycle_members - 1))
    key_sums = send_sums(key_sums)
    d_queries = (
        (query_grad * score_scale).reshape(shard_tokens, local_heads, head_dim).astype(jnp.bfloat16)
    )
    slot_weight = (lax.broadcasted_iota(jnp.int32, (kv_count,), 0) == kv_index).astype(jnp.float32)
    scaled = jnp.stack([key_sums[0] * score_scale, key_sums[1]])
    spread = scaled[:, :, None, :] * slot_weight[None, None, :, None]
    summed = lax.psum(spread, "head")
    return (d_queries, summed[0].astype(jnp.bfloat16), summed[1].astype(jnp.bfloat16))


def solution(mesh):
    placed = (
        P("ctx", "head", None),
        P("ctx", None, None),
        P("ctx", None, None),
        P("ctx", "head", None),
        P(),
        P(),
    )
    return jax.shard_map(
        per_device,
        mesh=mesh,
        in_specs=placed,
        out_specs=(P("ctx", "head", None), P("ctx", None, None), P("ctx", None, None)),
        check_vma=False,
    )
```

profile of v0, /device:TPU:0, one launch (start us, length us, event | category | flops | bytes accessed | tf_op | source)
XLA Modules:
  0.0 114.8 jit_solution(3894081865647388457)
XLA Ops:
  0.6 1.7 %pad_maximum_fusion = bf16[2,512,128]{2,1,0:T(8,128)(2,1)} fusion(bf16[1,512,128]{2,1,0:T(8,128)(2,1)} %bitcast.102, bf16[1,512,128]{2,1,0:T(8,128)(2,1)} %bitcast.104), kind=kLoop, calls=%fused_computation.57 | loop fusion | flops 131072 | bytes 524288 | tf_op jit(solution)/shard_map/stack | solution.py:51
  2.3 4.1 %collective-permute-start = (bf16[2,512,128]{2,1,0:T(8,128)(2,1)}, bf16[2,512,128]{2,1,0:T(8,128)(2,1)S(1)}, u32[]{:S(2)}, u32[]{:S(2)}) collective-permute-start(bf16[2,512,128]{2,1,0:T(8,128)(2,1)} %pad_maximum_fusion), channel_id=1, source_target_pairs={{0,16},{4,20},{8,24},{12,28},{16,0},{20,4},{24,8},{28,12},{1,17},{... | collective-permute-start | bytes 786440 | tf_op jit(solution)/shard_map/while/body/eval_jaxpr/ppermute | solution.py:15
  6.5 0.8 fusion.38
  13.7 1.5 %copy.18 = pred[256,8,4,128]{3,1,2,0:T(8,128)(4,1)} copy(pred[256,8,4,128]{3,2,1,0:T(4,128)(4,1)S(1)} %bitcast.98) | data formatting | bytes 2097152
  15.2 0.8 broadcast_in_dim.133
  16.1 8.1 %conditional.4 = (f32[2048]{0:T(1024)}, f32[2048]{0:T(1024)}, f32[2048]{0:T(1024)}) conditional(s32[]{:T(128)} %convert_element_type.57, () %tuple.63, (bf16[2048,128]{1,0:T(8,128)(2,1)S(1)}, bf16[512,128]{1,0:T(8,128)(2,1)S(1)}, pred[2048,512]{1,0:T(8,128)(4,1)}, bf16[2048,128]{1,0:T(8,128)(2,1)S(1)}, bf16[512,128]{1,0:T(8,128)(2,1)S(1)}) %tuple.130), branch_computations={%region_2.3_spmd, %region_3.7_spmd} | conditional | flops 545261568 | bytes 17121304 | solution.py:100
  16.1 2.4 %copy.11 = pred[2048,512]{0,1:T(32,128)(4,1)S(1)} copy(pred[2048,512]{1,0:T(8,128)(4,1)} %get-tuple-element.285) | data formatting | bytes 2097152 | tf_op jit(solution)/shard_map
  18.5 1.5 %fusion.39 = (f32[2048]{0:T(1024)}, f32[2048,512]{0,1:T(8,128)S(1)}) fusion(pred[2048,512]{0,1:T(32,128)(4,1)S(1)} %copy.11, bf16[2048,128]{1,0:T(8,128)(2,1)S(1)} %get-tuple-element.200, bf16[512,128]{1,0:T(8,128)(2,1)S(1)} %get-tuple-element.201), kind=kOutput, calls=%fused_computation.85 | convolution fusion | flops 271579136 | bytes 5906432 | tf_op jit(solution)/shard_map/cond/branch_1_fun/dot_general | solution.py:19
  20.0 1.3 %fusion = f32[2048]{0:T(1024)S(1)} fusion(f32[2048,512]{0,1:T(8,128)S(1)} %get-tuple-element.308, f32[2048]{0:T(1024)} %get-tuple-element.333), kind=kLoop, calls=%fused_computation.5 | loop fusion | flops 2095104 | bytes 4210688 | tf_op jit(solution)/shard_map/cond/branch_1_fun/reduce_sum | solution.py:96
  21.3 1.6 %multiply_reduce_fusion = f32[2048]{0:T(1024)S(1)} fusion(f32[2048,512]{0,1:T(8,128)S(1)} %get-tuple-element.308, bf16[2048,128]{1,0:T(8,128)(2,1)S(1)} %get-tuple-element.202, bf16[512,128]{1,0:T(8,128)(2,1)S(1)} %get-tuple-element.203, f32[2048]{0:T(1024)} %get-tuple-element.333), kind=kOutput, calls=%fused_computation.2 | convolution fusion | flops 271579136 | bytes 4866048 | tf_op jit(solution)/shard_map/cond/branch_1_fun/dot_general | solution.py:19
  22.8 1.3 %fusion.1 = (f32[2048]{0:T(1024)}, f32[2048]{0:T(1024)}) fusion(f32[2048]{0:T(1024)S(1)} %multiply_reduce_fusion, f32[2048]{0:T(1024)} %get-tuple-element.333, f32[2048]{0:T(1024)S(1)} %fusion), kind=kLoop, calls=%fused_computation.7 | loop fusion | flops 8192 | bytes 40960 | tf_op jit(solution)/shard_map/cond/branch_1_fun/add | solution.py:97
  24.1 6.2 %conditional.5 = ((f32[2048]{0:T(1024)}, f32[2048]{0:T(1024)}, f32[2048]{0:T(1024)})) conditional(s32[]{:T(128)} %convert_element_type.56, (f32[2048]{0:T(1024)}, f32[2048]{0:T(1024)}, f32[2048]{0:T(1024)}) %conditional.4, (bf16[2,512,128]{2,1,0:T(8,128)(2,1)S(1)}, bf16[2048,128]{1,0:T(8,128)(2,1)S(1)}, pred[2048,512]{1,0:T(8,128)(4,1)S(1)}, ...), branch_computations={%region_7.8_spmd.clone, %region_8.12_spmd.clone} | conditional | flops 545265664 | bytes 17186848 | solution.py:100
  24.1 1.2 %copy.12 = pred[2048,512]{0,1:T(32,128)(4,1)S(1)} copy(pred[2048,512]{1,0:T(8,128)(4,1)S(1)} %get-tuple-element.290) | data formatting | bytes 2097152 | tf_op jit(solution)/shard_map
  25.3 0.9 fusion.40
  26.9 0.9 multiply_reduce_fusion.1
  28.4 1.3 %multiply_add_fusion = (f32[2048]{0:T(1024)}, f32[2048]{0:T(1024)}) fusion(f32[2048]{0:T(1024)S(1)} %multiply_reduce_fusion.1, f32[2048]{0:T(1024)} %get-tuple-element.266, f32[2048]{0:T(1024)} %get-tuple-element.261, f32[2048]{0:T(1024)S(1)} %max.5, f32[2048]{0:T(1024)S(1)} %fusion.25, f32[2048]{0:T(1024)} %get-tuple-element.265), kind=kLoop, calls=%fused_computation.45 | loop fusion | flops 10240 | bytes 65536 | tf_op jit(solution)/shard_map/while/body/eval_jaxpr/cond/branch_1_fun/add | solution.py:97
  31.1 9.3 %conditional.6 = ((f32[2048,128]{1,0:T(8,128)S(1)}, f32[2,512,128]{2,1,0:T(8,128)})) conditional(s32[]{:T(128)} %convert_element_type.57, (f32[2048,128]{1,0:T(8,128)S(1)}, f32[2,512,128]{2,1,0:T(8,128)}) %tuple.62, (bf16[2,512,128]{2,1,0:T(8,128)(2,1)}, bf16[2048,128]{1,0:T(8,128)(2,1)S(1)}, pred[2048,512]{1,0:T(8,128)(4,1)}, ...), branch_computations={%region_12.13_spmd, %region_13.14_spmd} | conditional | flops 1350041600 | bytes 26624024 | solution.py:139
  31.3 2.4 %subtract_exponential_fusion.1 = f32[2048,512]{1,0:T(8,128)S(1)} fusion(pred[2048,512]{1,0:T(8,128)(4,1)} %get-tuple-element.212, bf16[2048,128]{1,0:T(8,128)(2,1)S(1)} %get-tuple-element.213, f32[2048]{0:T(1024)S(1)} %get-tuple-element.215, bf16[2,512,128]{2,1,0:T(8,128)(2,1)} %get-tuple-element.214), kind=kOutput, calls=%fused_computation.10 | convolution fusion | flops 271581184 | bytes 5906432 | tf_op jit(solution)/shard_map/while/body/eval_jaxpr/cond/branch_1_fun/dot_general | solution.py:19
  33.7 0.8 fusion.5
  34.5 1.6 %multiply_convert_fusion = bf16[2048,512]{1,0:T(8,128)(2,1)S(1)} fusion(f32[2048,512]{1,0:T(8,128)S(1)} %subtract_exponential_fusion.1, bf16[2048,128]{1,0:T(8,128)(2,1)S(1)} %get-tuple-element.216, f32[2048]{0:T(1024)S(1)} %get-tuple-element.217, bf16[2,512,128]{2,1,0:T(8,128)(2,1)} %get-tuple-element.214), kind=kOutput, calls=%fused_computation.9 | convolution fusion | flops 271581184 | bytes 6955008 | tf_op jit(solution)/shard_map/while/body/eval_jaxpr/cond/branch_1_fun/dot_general | solution.py:19
  36.1 1.7 %convolution_add_fusion = f32[2048,128]{1,0:T(8,128)S(1)} fusion(f32[2048,128]{1,0:T(8,128)S(1)} %get-tuple-element.211, bf16[2048,512]{1,0:T(8,128)(2,1)S(1)} %multiply_convert_fusion, bf16[2,512,128]{2,1,0:T(8,128)(2,1)} %get-tuple-element.214), kind=kOutput, calls=%fused_computation.11 | convolution fusion | flops 268697600 | bytes 4325376 | tf_op jit(solution)/shard_map/while/body/eval_jaxpr/cond/branch_1_fun/dot_general | solution.py:132
  37.8 0.7 convolution_bitcast_fusion
  38.5 1.9 %maximum_add_fusion = f32[2,512,128]{2,1,0:T(8,128)} fusion(f32[2,512,128]{2,1,0:T(8,128)} %get-tuple-element.218, f32[1,512,128]{2,1,0:T(8,128)S(1)} %fusion.5, f32[1,512,128]{2,1,0:T(8,128)S(1)} %convolution_bitcast_fusion), kind=kLoop, calls=%fused_computation.16 | loop fusion | flops 262144 | bytes 1572864 | tf_op jit(solution)/shard_map/while/body/eval_jaxpr/cond/branch_1_fun/add | solution.py:137
  40.4 25.8 %collective-permute-done.1 = f32[2,512,128]{2,1,0:T(8,128)} collective-permute-done((f32[2,512,128]{2,1,0:T(8,128)}, f32[2,512,128]{2,1,0:T(8,128)}, u32[]{:S(2)}, u32[]{:S(2)}) %collective-permute-start.1) | collective-permute-done | bytes 524320 | tf_op jit(solution)/shard_map/while/body/eval_jaxpr/ppermute | solution.py:15
  66.3 6.0 %conditional.7 = ((f32[2048,128]{1,0:T(8,128)S(1)}, f32[2,512,128]{2,1,0:T(8,128)})) conditional(s32[]{:T(128)} %convert_element_type.56, (f32[2048,128]{1,0:T(8,128)S(1)}, f32[2,512,128]{2,1,0:T(8,128)}) %tuple.67, (bf16[2,512,128]{2,1,0:T(8,128)(2,1)S(1)}, bf16[2048,128]{1,0:T(8,128)(2,1)S(1)}, pred[2048,512]{1,0:T(8,128)(4,1)S(1)}, ...), branch_computations={%region_14.15_spmd, %region_15.16_spmd} | conditional | flops 1350041600 | bytes 26624024 | solution.py:139
  66.3 1.1 subtract_exponential_fusion.2
  67.4 0.8 fusion.16
  69.6 0.7 convolution_bitcast_fusion.1
  70.3 1.9 %maximum_add_fusion.1 = f32[2,512,128]{2,1,0:T(8,128)} fusion(f32[2,512,128]{2,1,0:T(8,128)} %get-tuple-element.226, f32[1,512,128]{2,1,0:T(8,128)S(1)} %fusion.16, f32[1,512,128]{2,1,0:T(8,128)S(1)} %convolution_bitcast_fusion.1), kind=kLoop, calls=%fused_computation.30 | loop fusion | flops 262144 | bytes 1572864 | tf_op jit(solution)/shard_map/cond/branch_1_fun/add | solution.py:137
  72.2 0.9 multiply_convert_fusion.2
  73.1 23.9 %collective-permute-done.2 = f32[2,512,128]{2,1,0:T(8,128)S(1)} collective-permute-done((f32[2,512,128]{2,1,0:T(8,128)}, f32[2,512,128]{2,1,0:T(8,128)S(1)}, u32[]{:S(2)}, u32[]{:S(2)}) %collective-permute-start.2) | collective-permute-done | bytes 524320 | tf_op jit(solution)/shard_map/ppermute | solution.py:15
  97.1 17.0 %all-reduce.1 = bf16[2,512,1,128]{3,1,2,0:T(8,128)(2,1)S(1)} all-reduce(f32[2,512,1,128]{3,1,2,0:T(8,128)S(1)} %maximum_multiply_fusion), channel_id=1, replica_groups=mesh['ctx'=8,'head'=4] {'head'}, use_global_device_ids=true, to_apply=%region_16.17 | all-reduce | flops 131072 | bytes 786432 | tf_op jit(solution)/shard_map/psum | solution.py:160
  (40 shorter events, 10.0 us)
Async XLA Ops:
  0.6 6.9 %copy-start = (s32[4,8,8]{2,1,0:T(8,128)S(1)}, s32[4,8,8]{2,1,0:T(8,128)}, u32[]{:S(2)}) copy-start(s32[4,8,8]{2,1,0:T(8,128)} %param.19) | copy-start | bytes 3076
  2.3 21.8 %collective-permute-start = (bf16[2,512,128]{2,1,0:T(8,128)(2,1)}, bf16[2,512,128]{2,1,0:T(8,128)(2,1)S(1)}, u32[]{:S(2)}, u32[]{:S(2)}) collective-permute-start(bf16[2,512,128]{2,1,0:T(8,128)(2,1)} %pad_maximum_fusion), channel_id=1, source_target_pairs={{0,16},{4,20},{8,24},{12,28},{16,0},{20,4},{24,8},{28,12},{1,17},{... | collective-permute-start | bytes 786440 | tf_op jit(solution)/shard_map/while/body/eval_jaxpr/ppermute | solution.py:15
  11.7 4.3 %copy-start.1 = (bf16[512,4,128]{2,1,0:T(4,128)(2,1)S(1)}, bf16[512,4,128]{2,1,0:T(4,128)(2,1)}, u32[]{:S(2)}) copy-start(bf16[512,4,128]{2,1,0:T(4,128)(2,1)} %param.17) | copy-start | bytes 1572868
  11.8 4.3 %copy-start.2 = (bf16[512,4,128]{2,1,0:T(4,128)(2,1)S(1)}, bf16[512,4,128]{2,1,0:T(4,128)(2,1)}, u32[]{:S(2)}) copy-start(bf16[512,4,128]{2,1,0:T(4,128)(2,1)} %param.14) | copy-start | bytes 1572868
  11.8 4.3 %copy-start.3 = (bf16[512,1,128]{2,0,1:T(8,128)(2,1)S(1)}, bf16[512,1,128]{2,0,1:T(8,128)(2,1)}, u32[]{:S(2)}) copy-start(bf16[512,1,128]{2,0,1:T(8,128)(2,1)} %param.16) | copy-start | bytes 393220
  11.8 4.3 %copy-start.4 = (bf16[512,1,128]{2,0,1:T(8,128)(2,1)S(1)}, bf16[512,1,128]{2,0,1:T(8,128)(2,1)}, u32[]{:S(2)}) copy-start(bf16[512,1,128]{2,0,1:T(8,128)(2,1)} %param.15) | copy-start | bytes 393220
  40.4 25.9 %collective-permute-start.1 = (f32[2,512,128]{2,1,0:T(8,128)}, f32[2,512,128]{2,1,0:T(8,128)}, u32[]{:S(2)}, u32[]{:S(2)}) collective-permute-start(f32[2,512,128]{2,1,0:T(8,128)} %get-tuple-element.247), channel_id=1, source_target_pairs={{0,16},{4,20},{8,24},{12,28},{16,0},{20,4},{24,8},{28,12},{1,17},{... | collective-permute-start | bytes 1572872 | tf_op jit(solution)/shard_map/while/body/eval_jaxpr/ppermute | solution.py:15
  72.2 24.7 %collective-permute-start.2 = (f32[2,512,128]{2,1,0:T(8,128)}, f32[2,512,128]{2,1,0:T(8,128)S(1)}, u32[]{:S(2)}, u32[]{:S(2)}) collective-permute-start(f32[2,512,128]{2,1,0:T(8,128)} %get-tuple-element.249), channel_id=1, source_target_pairs={{0,16},{4,20},{8,24},{12,28},{16,0},{20,4},{24,8},{28,12},{1,17},{... | collective-permute-start | bytes 1572872 | tf_op jit(solution)/shard_map/ppermute | solution.py:15
where the time goes:
time: 115 us
  waiting for transfers between devices  49.7 us (43%)
  blocking collectives  17 us (15%)
  matrix products  16.1 us (14%)
  other arithmetic  14.8 us (13%)
  local copies, waits for them, and re-layouts  10.7 us (9%)
  starting transfers between devices  4.07 us (4%)
  between operations  2.1 us (2%)
    ppermute x3, waiting for transfers between devices, shifted(): return lax.ppermute(value, axis, pairs)  49.7 us
    psum x1, blocking collectives, per_device(): summed = lax.psum(spread, 'head')  17 us
    dot_general x8, matrix products, contract_last(): lax.dot_general(left, right, (((1,), (1,)), ((), ())), preferred_element_...  10.7 us
    ppermute x3, starting transfers between devices, shifted(): return lax.ppermute(value, axis, pairs)  4.07 us
    add x2, other arithmetic, update(): return (query_grad, key_sums + jnp.stack([key_add, value_add]))  3.78 us
    another operation x2, local copies, waits for them, and re-layouts  3.52 us
    dot_general x4, matrix products, contract_first(): lax.dot_general(left, right, (((0,), (0,)), ((), ())), preferred_element_...  2.98 us
    add x2, other arithmetic, update(): weighted * factor + jnp.sum(exp_rows * dprob_rows, axis=1)  2.66 us
  transfers between devices with their start and end apart: 3, of which 2 were waited for; matrix products, arithmetic and copies ran while one was open for 15% of the time, Pallas kernels for 0%

commit v1 on v0

v1 whole, which is shorter than its diff:
```python
import functools

import jax
import jax.numpy as jnp
from jax import lax
from jax.experimental import pallas as pl
from jax.experimental.pallas import tpu as pltpu
from jax.sharding import PartitionSpec as P

GROUP = 16
BLK = 128
SEQS = 4
LOG2E = 1.4426950408889634
MASKED = -1e30
SUB = 8


def dot_nt(left, right):
    return lax.dot_general(
        left, right, (((1,), (1,)), ((), ())), preferred_element_type=jnp.float32
    )


def dot_nn(left, right):
    return lax.dot_general(
        left, right, (((1,), (0,)), ((), ())), preferred_element_type=jnp.float32
    )


def by_sublane(value):
    return value.reshape(value.shape[0] // SUB, SUB, value.shape[1])


def shifted(value, axis, steps):
    count = lax.axis_size(axis)
    return lax.ppermute(value, axis, [(i, (i + steps) % count) for i in range(count)])


def swapped(value, axis, bit):
    count = lax.axis_size(axis)
    return lax.ppermute(value, axis, [(i, i ^ bit) for i in range(count)])


class Shape:
    def __init__(self, tokens, heads, depth, members):
        self.tokens = tokens
        self.heads = heads
        self.depth = depth
        self.members = members
        self.blocks = tokens // BLK
        self.rows = BLK * heads
        self.scale = depth**-0.5


def place(dims):
    ctx = lax.axis_index("ctx")
    return ctx % SEQS, ctx // SEQS


def seen(dims, pos_ref, mask_ref, query_slot, hop, key_slot):
    seq, member = place(dims)
    owner = (member - hop + dims.members) % dims.members
    query_id = pos_ref[seq, member * dims.blocks + query_slot]
    key_id = pos_ref[seq, owner * dims.blocks + key_slot]
    return jnp.logical_and(key_id < query_id, mask_ref[seq, query_id, key_id] == 1)


def causal_logits(dims, logits):
    key_token = lax.broadcasted_iota(jnp.int32, logits.shape, 0)
    query_token = lax.broadcasted_iota(jnp.int32, logits.shape, 1) // dims.heads
    return jnp.where(key_token <= query_token, logits, MASKED)


def stats_of(logits, dprob):
    parts = by_sublane(logits)
    top = jnp.max(parts, axis=0)
    exps = jnp.exp2(parts - top[None])
    return top, jnp.sum(exps, axis=0), jnp.sum(exps * by_sublane(dprob), axis=0)


def merged(first, second):
    top = jnp.maximum(first[0], second[0])
    one, two = jnp.exp2(first[0] - top), jnp.exp2(second[0] - top)
    return top, first[1] * one + second[1] * two, first[2] * one + second[2] * two


def load_stats(ref, slot):
    return ref[slot, 0], ref[slot, 1], ref[slot, 2]


def store_stats(ref, slot, stats):
    for index in range(3):
        ref[slot, index] = stats[index]


def rows_of(ref, slot, count):
    return ref[pl.ds(pl.multiple_of(slot * count, count), count), :]


def own_stats_kernel(dims, pos_ref, mask_ref, q_ref, g_ref, k_ref, v_ref, stats_ref):
    factor = dims.scale * LOG2E

    @pl.loop(0, dims.blocks)
    def _(slot):
        query = rows_of(q_ref, slot, dims.rows)
        grad = rows_of(g_ref, slot, dims.rows)

        def tile(key_slot, mask):
            logits = dot_nt(rows_of(k_ref, key_slot, BLK), query) * factor
            if mask:
                logits = causal_logits(dims, logits)
            return stats_of(logits, dot_nt(rows_of(v_ref, key_slot, BLK), grad))

        store_stats(stats_ref, slot, tile(slot, True))

        @pl.loop(0, dims.blocks)
        def _(key_slot):
            @pl.when(seen(dims, pos_ref, mask_ref, slot, 0, key_slot))
            def _():
                store_stats(stats_ref, slot, merged(load_stats(stats_ref, slot), tile(key_slot, False)))


def far_kernel(
    dims, pos_ref, mask_ref, q_ref, g_ref, near_ref, swap_ref, stats_ref,
    final_ref, dq_ref, keep_ref, send_ref,
    k_all, v_all, kt_all, run, logit_all, dprob_all, dk_all, dv_all,
):
    factor = dims.scale * LOG2E
    first_core = lax.axis_index("head") % 2 == 0
    far_blocks = (dims.members - 1) * dims.blocks

    @pl.when(first_core)
    def _():
        k_all[...] = near_ref[...]
        v_all[...] = swap_ref[...]

    @pl.when(jnp.logical_not(first_core))
    def _():
        k_all[...] = swap_ref[...]
        v_all[...] = near_ref[...]

    for index in range(far_blocks):
        kt_all[index] = k_all[index * BLK:(index + 1) * BLK, :].T

    dk_all[...] = jnp.zeros_like(dk_all)
    dv_all[...] = jnp.zeros_like(dv_all)
    run[...] = stats_ref[...]

    @pl.loop(0, dims.blocks)
    def _(slot):
        dq_ref[slot] = jnp.zeros(dq_ref.shape[1:], jnp.float32)

        def visible(index):
            return seen(dims, pos_ref, mask_ref, slot, index // dims.blocks + 1, index % dims.blocks)

        @pl.loop(0, far_blocks)
        def _(index):
            @pl.when(visible(index))
            def _():
                logits = dot_nt(rows_of(k_all, index, BLK), rows_of(q_ref, slot, dims.rows)) * factor
                dprob = dot_nt(rows_of(v_all, index, BLK), rows_of(g_ref, slot, dims.rows))
                logit_all[index] = logits
                dprob_all[index] = dprob
                store_stats(run, slot, merged(load_stats(run, slot), stats_of(logits, dprob)))

        tops, totals, weighted = load_stats(run, slot)
        top = jnp.max(tops, axis=0, keepdims=True)
        factors = jnp.exp2(tops - top)
        total = jnp.sum(totals * factors, axis=0, keepdims=True)
        log_sum = top + jnp.log2(total)
        delta = jnp.sum(weighted * factors, axis=0, keepdims=True) / total
        final_ref[slot, 0] = jnp.broadcast_to(log_sum, tops.shape)
        final_ref[slot, 1] = jnp.broadcast_to(delta, tops.shape)

        @pl.loop(0, far_blocks)
        def _(index):
            @pl.when(visible(index))
            def _():
                probs = jnp.exp2(by_sublane(logit_all[index]) - final_ref[slot, 0][None])
                dscore = probs * (by_sublane(dprob_all[index]) - final_ref[slot, 1][None])
                probs = probs.reshape(BLK, dims.rows).astype(jnp.bfloat16)
                dscore = dscore.reshape(BLK, dims.rows).astype(jnp.bfloat16)
                dk_all[index] += dot_nn(dscore, rows_of(q_ref, slot, dims.rows))
                dv_all[index] += dot_nn(probs, rows_of(g_ref, slot, dims.rows))
                dq_ref[slot] += dot_nn(kt_all[index], dscore)

    share_out(dims, first_core, dk_all, dv_all, keep_ref, send_ref)


def share_out(dims, first_core, dk_all, dv_all, keep_ref, send_ref):
    shape = keep_ref.shape

    @pl.when(first_core)
    def _():
        keep_ref[...] = (dk_all[...] * dims.scale).reshape(shape)
        send_ref[...] = dv_all[...].reshape(shape).astype(send_ref.dtype)

    @pl.when(jnp.logical_not(first_core))
    def _():
        keep_ref[...] = dv_all[...].reshape(shape)
        send_ref[...] = (dk_all[...] * dims.scale).reshape(shape).astype(send_ref.dtype)


def own_grads_kernel(
    dims, pos_ref, mask_ref, q_ref, g_ref, k_ref, v_ref, final_ref, dq_far_ref,
    dq_ref, keep_ref, send_ref,
    kt_all, dq_sum, dk_all, dv_all,
):
    factor = dims.scale * LOG2E
    first_core = lax.axis_index("head") % 2 == 0
    for index in range(dims.blocks):
        kt_all[index] = k_ref[index * BLK:(index + 1) * BLK, :].T
    dk_all[...] = jnp.zeros_like(dk_all)
    dv_all[...] = jnp.zeros_like(dv_all)

    @pl.loop(0, dims.blocks)
    def _(slot):
        query = rows_of(q_ref, slot, dims.rows)
        grad = rows_of(g_ref, slot, dims.rows)

        def tile(key_slot, mask):
            logits = dot_nt(rows_of(k_ref, key_slot, BLK), query) * factor
            if mask:
                logits = causal_logits(dims, logits)
            dprob = dot_nt(rows_of(v_ref, key_slot, BLK), grad)
            probs = jnp.exp2(by_sublane(logits) - final_ref[slot, 0][None])
            dscore = probs * (by_sublane(dprob) - final_ref[slot, 1][None])
            probs = probs.reshape(BLK, dims.rows).astype(jnp.bfloat16)
            dscore = dscore.reshape(BLK, dims.rows).astype(jnp.bfloat16)
            dk_all[key_slot] += dot_nn(dscore, query)
            dv_all[key_slot] += dot_nn(probs, grad)
            return dot_nn(kt_all[key_slot], dscore)

        dq_sum[...] = dq_far_ref[slot] + tile(slot, True)

        @pl.loop(0, dims.blocks)
        def _(key_slot):
            @pl.when(seen(dims, pos_ref, mask_ref, slot, 0, key_slot))
            def _():
                dq_sum[...] += tile(key_slot, False)

        start = pl.multiple_of(slot * dims.rows, dims.rows)
        dq_ref[pl.ds(start, dims.rows), :] = (dq_sum[...] * dims.scale).T.astype(dq_ref.dtype)

    share_out(dims, first_core, dk_all, dv_all, keep_ref, send_ref)


VMEM = pl.BlockSpec(memory_space=pltpu.VMEM)
SMEM = pl.BlockSpec(memory_space=pltpu.SMEM)


def per_device(queries, keys, values, d_out, block_pos, block_mask):
    tokens, heads, depth = queries.shape
    kv_count = keys.shape[1]
    members = lax.axis_size("ctx") // SEQS
    head_count = lax.axis_size("head")
    sharers = GROUP // heads
    dims = Shape(tokens, heads, depth, members)
    head_index = lax.axis_index("head")
    kv_index = head_index // sharers
    first_core = head_index % 2 == 0
    f32, bf16 = jnp.float32, jnp.bfloat16
    sds = jax.ShapeDtypeStruct

    key_own = lax.dynamic_index_in_dim(keys, kv_index, 1, keepdims=False) if kv_count > 1 else keys[:, 0]
    value_own = lax.dynamic_index_in_dim(values, kv_index, 1, keepdims=False) if kv_count > 1 else values[:, 0]
    query_rows = queries.reshape(tokens * heads, depth)
    grad_rows = d_out.reshape(tokens * heads, depth)

    passed = jnp.where(first_core, key_own, value_own)
    near, swap = [], []
    for _ in range(members - 1):
        passed = shifted(passed, "ctx", SEQS)
        near.append(passed)
        swap.append(swapped(passed, "head", 1))
    near = near[0] if members == 2 else jnp.concatenate(near)
    swap = swap[0] if members == 2 else jnp.concatenate(swap)

    params = pltpu.CompilerParams(vmem_limit_bytes=(12 + 4 * members) << 20)
    blocks, rows = dims.blocks, dims.rows
    tile_flops = 2 * BLK * rows * depth

    def cost(tiles, dots):
        return pl.CostEstimate(
            flops=tiles * dots * tile_flops,
            bytes_accessed=4 * tokens * heads * depth,
            transcendentals=tiles * BLK * rows,
        )

    stats = pl.pallas_call(
        functools.partial(own_stats_kernel, dims),
        out_shape=sds((blocks, 3, SUB, rows), f32),
        in_specs=[SMEM] * 2 + [VMEM] * 4,
        out_specs=VMEM,
        compiler_params=params,
        cost_estimate=cost(blocks * blocks, 2),
        name="own_stats",
    )(block_pos, block_mask, query_rows, grad_rows, key_own, value_own)

    far = (members - 1) * blocks
    final, dq_far, keep_far, send_far = pl.pallas_call(
        functools.partial(far_kernel, dims),
        out_shape=(
            sds((blocks, 2, SUB, rows), f32),
            sds((blocks, depth, rows), f32),
            sds(((members - 1) * tokens, depth), f32),
            sds(((members - 1) * tokens, depth), bf16),
        ),
        in_specs=[SMEM] * 2 + [VMEM] * 5,
        out_specs=(VMEM,) * 4,
        scratch_shapes=[
            pltpu.VMEM((far * BLK, depth), bf16),
            pltpu.VMEM((far * BLK, depth), bf16),
            pltpu.VMEM((far, depth, BLK), bf16),
            pltpu.VMEM((blocks, 3, SUB, rows), f32),
            pltpu.VMEM((far, BLK, rows), f32),
            pltpu.VMEM((far, BLK, rows), f32),
            pltpu.VMEM((far, BLK, depth), f32),
            pltpu.VMEM((far, BLK, depth), f32),
        ],
        compiler_params=params,
        cost_estimate=cost(blocks * far, 5),
        name="far_part",
    )(block_pos, block_mask, query_rows, grad_rows, near, swap, stats)

    dq, keep_own, send_own = pl.pallas_call(
        functools.partial(own_grads_kernel, dims),
        out_shape=(
            sds((tokens * heads, depth), bf16),
            sds((tokens, depth), f32),
            sds((tokens, depth), bf16),
        ),
        in_specs=[SMEM] * 2 + [VMEM] * 6,
        out_specs=(VMEM,) * 3,
        scratch_shapes=[
            pltpu.VMEM((blocks, depth, BLK), bf16),
            pltpu.VMEM((depth, rows), f32),
            pltpu.VMEM((blocks, BLK, depth), f32),
            pltpu.VMEM((blocks, BLK, depth), f32),
        ],
        compiler_params=params,
        cost_estimate=cost(blocks * blocks, 5),
        name="own_grads",
    )(block_pos, block_mask, query_rows, grad_rows, key_own, value_own, final, dq_far)

    travel = bf16 if members == 2 else f32
    pair_far = keep_far + swapped(send_far, "head", 1).astype(f32)
    total = pair_far[:tokens]
    for hop in range(1, members):
        moved = shifted(total.astype(travel), "ctx", SEQS).astype(f32)
        if hop < members - 1:
            total = moved + pair_far[hop * tokens:(hop + 1) * tokens]
    total = moved + (keep_own + swapped(send_own, "head", 1).astype(f32))
    bit = 2
    total = total.astype(bf16)
    while bit < sharers:
        total = (total.astype(f32) + swapped(total, "head", bit).astype(f32)).astype(bf16)
        bit *= 2
    other = swapped(total, "head", 1)
    d_keys = jnp.where(first_core, total, other)
    d_values = jnp.where(first_core, other, total)
    if kv_count > 1:
        groups = [[p + sharers * g for g in range(kv_count)] for p in range(sharers)]
        both = lax.all_gather(
            jnp.stack([d_keys, d_values]), "head", axis=2, axis_index_groups=groups
        )
        d_keys, d_values = both[0], both[1]
    else:
        d_keys, d_values = d_keys[:, None], d_values[:, None]
    return dq.reshape(tokens, heads, depth), d_keys, d_values


def solution(mesh):
    placed = (
        P("ctx", "head", None),
        P("ctx", None, None),
        P("ctx", None, None),
        P("ctx", "head", None),
        P(),
        P(),
    )
    return jax.shard_map(
        per_device,
        mesh=mesh,
        in_specs=placed,
        out_specs=(P("ctx", "head", None), P("ctx", None, None), P("ctx", None, None)),
        check_vma=False,
    )
```

time: 115 us -> 46.9 us (0.41)
  waiting for transfers between devices: 49.7 us -> 19.7 us
  blocking collectives: 17 us -> 0 us
  matrix products: 16.1 us -> 0 us
  Pallas kernels: 0 us -> 16 us
  other arithmetic: 14.8 us -> 1.86 us
  local copies, waits for them, and re-layouts: 10.7 us -> 2.75 us
  starting transfers between devices: 4.07 us -> 6.43 us
  between operations: 2.1 us -> 0.75 us
    ppermute x3 -> x7, waiting for transfers between devices: 49.7 us -> 19.7 us  [the longest x2 13.1 us: shifted(): lax.ppermute(value, axis, [(i, (i + steps) % count) for i in range(count)])]
    psum x1 -> x0, blocking collectives: 17 us -> none  [per_device(): summed = lax.psum(spread, 'head')]
    dot_general x14 -> x0, matrix products: 16.1 us -> none  [the longest x8 10.7 us: contract_last(): lax.dot_general(left, right, (((1,), (1,)), ((), ())), preferred_element_...]
    pallas_call x0 -> x3, Pallas kernels: none -> 16 us  [the longest x1 6.73 us: per_device(): pl.pallas_call(functools.partial(own_grads_kernel, dims), out_shape=(sds(...]
    add x4 -> x0, other arithmetic: 6.44 us -> none  [the longest x2 3.78 us: update(): return (query_grad, key_sums + jnp.stack([key_add, value_add]))]
    another operation x2 -> x0, local copies, waits for them, and re-layouts: 3.52 us -> none
    ppermute x3 -> x7, starting transfers between devices: 4.07 us -> 6.43 us  [the longest x2 4.2 us: shifted(): lax.ppermute(value, axis, [(i, (i + steps) % count) for i in range(count)])]
    broadcast_in_dim x4 -> x0, local copies, waits for them, and re-layouts: 2.25 us -> none  [the longest x2 1.35 us: hop_mask(): allowed = jnp.broadcast_to(allowed, (QB_DEV, BLK, local_heads, QB_DEV, BLK))]
  transfers between devices with their start and end apart: 3 -> 7, of which waited for: 2 -> 5; matrix products, arithmetic and copies ran while one was open for 15% -> 0% of each run, Pallas kernels for 0% -> 22%
where the time goes in v1:
time: 46.9 us; the launch traced here: 47.5 us
  waiting for transfers between devices  19.7 us (42%)
  Pallas kernels  16 us (34%)
  starting transfers between devices  6.43 us (14%)
  local copies, waits for them, and re-layouts  2.75 us (6%)
  other arithmetic  1.86 us (4%)
  between operations  0.75 us (2%)
    ppermute x2, waiting for transfers between devices, shifted(): lax.ppermute(value, axis, [(i, (i + steps) % count) for i in range(count)])  13.1 us
    pallas_call x1, Pallas kernels, per_device(): pl.pallas_call(functools.partial(own_grads_kernel, dims), out_shape=(sds(...  6.73 us
    ppermute x5, waiting for transfers between devices, swapped(): return lax.ppermute(value, axis, [(i, i ^ bit) for i in range(count)])  6.53 us
    pallas_call x1, Pallas kernels, per_device(): pl.pallas_call(functools.partial(far_kernel, dims), out_shape=(sds((block...  5.53 us
    ppermute x2, starting transfers between devices, shifted(): lax.ppermute(value, axis, [(i, (i + steps) % count) for i in range(count)])  4.2 us
    pallas_call x1, Pallas kernels, per_device(): pl.pallas_call(functools.partial(own_stats_kernel, dims), out_shape=sds((...  3.77 us
    unnamed x12, local copies, waits for them, and re-layouts  2.75 us
    ppermute x5, starting transfers between devices, swapped(): return lax.ppermute(value, axis, [(i, i ^ bit) for i in range(count)])  2.23 us
  transfers between devices with their start and end apart: 7, of which 5 were waited for; matrix products, arithmetic and copies ran while one was open for 0% of the time, Pallas kernels for 22%

profile of v1, /device:TPU:0, one launch (start us, length us, event | category | flops | bytes accessed | tf_op | source)
XLA Modules:
  0.0 47.5 jit_solution(3301447967558832827)
XLA Ops:
  0.6 0.0 copy-start
  0.7 0.0 copy-start.1
  0.7 0.0 copy-start.4
  0.7 1.0 %broadcast_select_fusion = bf16[512,128]{1,0:T(8,128)(2,1)S(1)} fusion(pred[]{:T(512)S(6)} %eq.5, bf16[512,1,128]{2,0,1:T(8,128)(2,1)} %param.8, bf16[512,1,128]{2,0,1:T(8,128)(2,1)} %param.7), kind=kLoop, calls=%fused_computation.5 | loop fusion | flops 65536 | bytes 393217 | tf_op jit(solution)/shard_map/jit(_where)/select_n | solution.py:270
  1.7 4.1 %collective-permute-start = (bf16[512,128]{1,0:T(8,128)(2,1)S(1)}, bf16[512,128]{1,0:T(8,128)(2,1)S(1)}, u32[]{:S(2)}, u32[]{:S(2)}) collective-permute-start(bf16[512,128]{1,0:T(8,128)(2,1)S(1)} %broadcast_select_fusion), channel_id=1, source_target_pairs={{0,16},{4,20},{8,24},{12,28},{16,0},{20,4},{24,8},{28,12},{1,17},{... | collective-permute-start | bytes 393224 | tf_op jit(solution)/shard_map/ppermute | solution.py:36
  5.8 6.3 %collective-permute-done.near_ref = bf16[512,128]{1,0:T(8,128)(2,1)S(1)} collective-permute-done((bf16[512,128]{1,0:T(8,128)(2,1)S(1)}, bf16[512,128]{1,0:T(8,128)(2,1)S(1)}, u32[]{:S(2)}, u32[]{:S(2)}) %collective-permute-start) | collective-permute-done | bytes 131104 | tf_op jit(solution)/shard_map/ppermute | solution.py:36
  12.1 0.0 collective-permute-start.1
  12.1 0.0 copy-start.5
  12.1 0.0 copy-done
  12.2 0.0 copy-done.1
  12.2 0.0 copy-done.4
  12.2 0.7 %copy-done.5 = s32[4,8]{1,0:T(4,128)S(1)} copy-done((s32[4,8]{1,0:T(4,128)S(1)}, s32[4,8]{1,0:T(4,128)}, u32[]{:S(2)}) %copy-start.5) | copy-done | bytes 152
  12.8 0.0 copy-start.2
  12.8 1.0 %copy-done.2 = bf16[512,4,128]{2,1,0:T(4,128)(2,1)S(1)} copy-done((bf16[512,4,128]{2,1,0:T(4,128)(2,1)S(1)}, bf16[512,4,128]{2,1,0:T(4,128)(2,1)}, u32[]{:S(2)}) %copy-start.2) | copy-done | bytes 524312
  13.9 0.0 copy-start.3
  13.9 1.0 %copy-done.3 = bf16[512,4,128]{2,1,0:T(4,128)(2,1)S(1)} copy-done((bf16[512,4,128]{2,1,0:T(4,128)(2,1)S(1)}, bf16[512,4,128]{2,1,0:T(4,128)(2,1)}, u32[]{:S(2)}) %copy-start.3) | copy-done | bytes 524312
  14.9 3.8 %own_stats.1.stats_ref = f32[4,3,8,512]{3,2,1,0:T(8,128)S(1)} custom-call(s32[4,8]{1,0:T(4,128)S(1)} %copy-done.5, s32[4,8,8]{2,1,0:T(8,128)S(1)} %copy-done.4, bf16[2048,128]{1,0:T(8,128)(2,1)S(1)} %bitcast.15, bf16[2048,128]{1,0:T(8,128)(2,1)S(1)} %bitcast.18, bf16[512,128]{1,0:T(8,128)(2,1)S(1)} %bitcast.11, bf16[512,128]{1,0:T(8,128)(2,1)S(1)} %bitcast.13), custom_call_target="tpu_custom_call" | custom-call | flops 536870912 | bytes 1048576 | tf_op jit(solution)/shard_map/own_stats/pallas_call | solution.py:290
  18.7 0.0 collective-permute-done.1.swap_ref
  18.7 5.5 %far_part.1 = (f32[4,2,8,512]{3,2,1,0:T(8,128)S(1)}, f32[4,128,512]{2,1,0:T(8,128)S(1)}, f32[512,128]{1,0:T(8,128)S(1)}, bf16[512,128]{1,0:T(8,128)(2,1)S(1)}) custom-call(s32[4,8]{1,0:T(4,128)S(1)} %copy-done.5, s32[4,8,8]{2,1,0:T(8,128)S(1)} %copy-done.4, bf16[2048,128]{1,0:T(8,128)(2,1)S(1)} %bitcast.16, bf16[2048,128]{1,0:T(8,128)(2,1)S(1)} %bitcast.19, ...), custom_call_target="tpu_custom_call" | custom-call | flops 1342177280 | bytes 1048576 | tf_op jit(solution)/shard_map/far_part/pallas_call | solution.py:301
  24.2 0.6 %collective-permute-start.2 = (bf16[512,128]{1,0:T(8,128)(2,1)S(1)}, bf16[512,128]{1,0:T(8,128)(2,1)S(1)}, u32[]{:S(2)}, u32[]{:S(2)}) collective-permute-start(bf16[512,128]{1,0:T(8,128)(2,1)S(1)} %get-tuple-element.14), channel_id=1, source_target_pairs={{0,1},{1,0},{2,3},{3,2},{4,5},{5,4},{6,7},{7,6},{8,9},{9,8},{10,11... | collective-permute-start | bytes 393224 | tf_op jit(solution)/shard_map/ppermute | solution.py:41
  24.8 6.7 %own_grads.1 = (bf16[2048,128]{1,0:T(8,128)(2,1)}, f32[512,128]{1,0:T(8,128)S(1)}, bf16[512,128]{1,0:T(8,128)(2,1)S(1)}) custom-call(s32[4,8]{1,0:T(4,128)S(1)} %copy-done.5, s32[4,8,8]{2,1,0:T(8,128)S(1)} %copy-done.4, bf16[2048,128]{1,0:T(8,128)(2,1)S(1)} %bitcast.17, bf16[2048,128]{1,0:T(8,128)(2,1)S(1)} %bitcast.20, bf16[512,128]{1,0:T(8,128)(2,1)S(1)} %bitcast.12, ...), custom_call_target="tpu_custom_call" | custom-call | flops 1342177280 | bytes 1048576 | tf_op jit(solution)/shard_map/own_grads/pallas_call | solution.py:326
  31.5 0.0 collective-permute-start.4
  31.6 0.0 collective-permute-done.2
  31.6 0.1 collective-permute-start.3
  31.7 1.2 %collective-permute-done.4 = bf16[512,128]{1,0:T(8,128)(2,1)S(1)} collective-permute-done((bf16[512,128]{1,0:T(8,128)(2,1)S(1)}, bf16[512,128]{1,0:T(8,128)(2,1)S(1)}, u32[]{:S(2)}, u32[]{:S(2)}) %collective-permute-start.4) | collective-permute-done | bytes 131104 | tf_op jit(solution)/shard_map/ppermute | solution.py:41
  32.9 6.8 %collective-permute-done.3 = bf16[512,128]{1,0:T(8,128)(2,1)S(1)} collective-permute-done((bf16[512,128]{1,0:T(8,128)(2,1)S(1)}, bf16[512,128]{1,0:T(8,128)(2,1)S(1)}, u32[]{:S(2)}, u32[]{:S(2)}) %collective-permute-start.3) | collective-permute-done | bytes 131104 | tf_op jit(solution)/shard_map/ppermute | solution.py:36
  39.8 1.6 %collective-permute-start.5 = (bf16[512,128]{1,0:T(8,128)(2,1)S(1)}, bf16[512,128]{1,0:T(8,128)(2,1)S(1)}, u32[]{:S(2)}, u32[]{:S(2)}) collective-permute-start(bf16[512,128]{1,0:T(8,128)(2,1)S(1)} %add_convert_fusion.1), channel_id=1, source_target_pairs={{0,2},{1,3},{2,0},{3,1},{4,6},{5,7},{6,4},{7,5},{8,10},{9,11},{10,... | collective-permute-start | bytes 393224 | tf_op jit(solution)/shard_map/ppermute | solution.py:41
  41.3 4.0 %collective-permute-done.5 = bf16[512,128]{1,0:T(8,128)(2,1)S(1)} collective-permute-done((bf16[512,128]{1,0:T(8,128)(2,1)S(1)}, bf16[512,128]{1,0:T(8,128)(2,1)S(1)}, u32[]{:S(2)}, u32[]{:S(2)}) %collective-permute-start.5) | collective-permute-done | bytes 131104 | tf_op jit(solution)/shard_map/ppermute | solution.py:41
  45.4 0.1 collective-permute-start.6
  45.4 1.3 %collective-permute-done.6 = bf16[512,128]{1,0:T(8,128)(2,1)S(1)} collective-permute-done((bf16[512,128]{1,0:T(8,128)(2,1)S(1)}, bf16[512,128]{1,0:T(8,128)(2,1)S(1)}, u32[]{:S(2)}, u32[]{:S(2)}) %collective-permute-start.6) | collective-permute-done | bytes 131104 | tf_op jit(solution)/shard_map/ppermute | solution.py:41
  46.8 0.7 %select_bitcast_fusion = (bf16[512,1,128]{2,0,1:T(8,128)(2,1)}, bf16[512,1,128]{2,0,1:T(8,128)(2,1)}) fusion(bf16[512,128]{1,0:T(8,128)(2,1)S(1)} %collective-permute-done.6, bf16[512,128]{1,0:T(8,128)(2,1)S(1)} %add_convert_fusion, pred[]{:T(512)S(6)} %eq.5), kind=kLoop, calls=%fused_computation.3 | loop fusion | flops 131072 | bytes 524289 | tf_op jit(solution)/shard_map/broadcast_in_dim | solution.py:369
  (3 shorter events, 0.1 us)
Async XLA Ops:
  0.6 11.5 %copy-start = (bf16[512,1,128]{2,0,1:T(8,128)(2,1)S(1)}, bf16[512,1,128]{2,0,1:T(8,128)(2,1)}, u32[]{:S(2)}) copy-start(bf16[512,1,128]{2,0,1:T(8,128)(2,1)} %param.7) | copy-start | bytes 393220
  0.7 11.5 %copy-start.1 = (bf16[512,1,128]{2,0,1:T(8,128)(2,1)S(1)}, bf16[512,1,128]{2,0,1:T(8,128)(2,1)}, u32[]{:S(2)}) copy-start(bf16[512,1,128]{2,0,1:T(8,128)(2,1)} %param.8) | copy-start | bytes 393220
  0.7 11.5 %copy-start.4 = (s32[4,8,8]{2,1,0:T(8,128)S(1)}, s32[4,8,8]{2,1,0:T(8,128)}, u32[]{:S(2)}) copy-start(s32[4,8,8]{2,1,0:T(8,128)} %mask_ref.5) | copy-start | bytes 3076
  1.7 10.4 %collective-permute-start = (bf16[512,128]{1,0:T(8,128)(2,1)S(1)}, bf16[512,128]{1,0:T(8,128)(2,1)S(1)}, u32[]{:S(2)}, u32[]{:S(2)}) collective-permute-start(bf16[512,128]{1,0:T(8,128)(2,1)S(1)} %broadcast_select_fusion), channel_id=1, source_target_pairs={{0,16},{4,20},{8,24},{12,28},{16,0},{20,4},{24,8},{28,12},{1,17},{... | collective-permute-start | bytes 393224 | tf_op jit(solution)/shard_map/ppermute | solution.py:36
  12.1 6.5 %collective-permute-start.1 = (bf16[512,128]{1,0:T(8,128)(2,1)S(1)}, bf16[512,128]{1,0:T(8,128)(2,1)S(1)}, u32[]{:S(2)}, u32[]{:S(2)}) collective-permute-start(bf16[512,128]{1,0:T(8,128)(2,1)S(1)} %collective-permute-done.near_ref), channel_id=1, source_target_pairs={{0,1},{1,0},{2,3},{3,2},{4,5},{5,4},{6,7},{7,6},{8,9},{9,8},{10,11... | collective-permute-start | bytes 393224 | tf_op jit(solution)/shard_map/ppermute | solution.py:41
  12.1 0.7 %copy-start.5 = (s32[4,8]{1,0:T(4,128)S(1)}, s32[4,8]{1,0:T(4,128)}, u32[]{:S(2)}) copy-start(s32[4,8]{1,0:T(4,128)} %pos_ref.5) | copy-start | bytes 388
  12.8 1.0 %copy-start.2 = (bf16[512,4,128]{2,1,0:T(4,128)(2,1)S(1)}, bf16[512,4,128]{2,1,0:T(4,128)(2,1)}, u32[]{:S(2)}) copy-start(bf16[512,4,128]{2,1,0:T(4,128)(2,1)} %param.6) | copy-start | bytes 1572868
  13.9 1.0 %copy-start.3 = (bf16[512,4,128]{2,1,0:T(4,128)(2,1)S(1)}, bf16[512,4,128]{2,1,0:T(4,128)(2,1)}, u32[]{:S(2)}) copy-start(bf16[512,4,128]{2,1,0:T(4,128)(2,1)} %param.9) | copy-start | bytes 1572868
  24.2 7.3 %collective-permute-start.2 = (bf16[512,128]{1,0:T(8,128)(2,1)S(1)}, bf16[512,128]{1,0:T(8,128)(2,1)S(1)}, u32[]{:S(2)}, u32[]{:S(2)}) collective-permute-start(bf16[512,128]{1,0:T(8,128)(2,1)S(1)} %get-tuple-element.14), channel_id=1, source_target_pairs={{0,1},{1,0},{2,3},{3,2},{4,5},{5,4},{6,7},{7,6},{8,9},{9,8},{10,11... | collective-permute-start | bytes 393224 | tf_op jit(solution)/shard_map/ppermute | solution.py:41
  31.5 1.3 %collective-permute-start.4 = (bf16[512,128]{1,0:T(8,128)(2,1)S(1)}, bf16[512,128]{1,0:T(8,128)(2,1)S(1)}, u32[]{:S(2)}, u32[]{:S(2)}) collective-permute-start(bf16[512,128]{1,0:T(8,128)(2,1)S(1)} %get-tuple-element.16), channel_id=1, source_target_pairs={{0,1},{1,0},{2,3},{3,2},{4,5},{5,4},{6,7},{7,6},{8,9},{9,8},{10,11... | collective-permute-start | bytes 393224 | tf_op jit(solution)/shard_map/ppermute | solution.py:41
  31.6 8.1 %collective-permute-start.3 = (bf16[512,128]{1,0:T(8,128)(2,1)S(1)}, bf16[512,128]{1,0:T(8,128)(2,1)S(1)}, u32[]{:S(2)}, u32[]{:S(2)}) collective-permute-start(bf16[512,128]{1,0:T(8,128)(2,1)S(1)} %add_convert_fusion.2), channel_id=1, source_target_pairs={{0,16},{4,20},{8,24},{12,28},{16,0},{20,4},{24,8},{28,12},{1,17},{... | collective-permute-start | bytes 393224 | tf_op jit(solution)/shard_map/ppermute | solution.py:36
  39.8 5.5 %collective-permute-start.5 = (bf16[512,128]{1,0:T(8,128)(2,1)S(1)}, bf16[512,128]{1,0:T(8,128)(2,1)S(1)}, u32[]{:S(2)}, u32[]{:S(2)}) collective-permute-start(bf16[512,128]{1,0:T(8,128)(2,1)S(1)} %add_convert_fusion.1), channel_id=1, source_target_pairs={{0,2},{1,3},{2,0},{3,1},{4,6},{5,7},{6,4},{7,5},{8,10},{9,11},{10,... | collective-permute-start | bytes 393224 | tf_op jit(solution)/shard_map/ppermute | solution.py:41
  45.4 1.4 %collective-permute-start.6 = (bf16[512,128]{1,0:T(8,128)(2,1)S(1)}, bf16[512,128]{1,0:T(8,128)(2,1)S(1)}, u32[]{:S(2)}, u32[]{:S(2)}) collective-permute-start(bf16[512,128]{1,0:T(8,128)(2,1)S(1)} %add_convert_fusion), channel_id=1, source_target_pairs={{0,1},{1,0},{2,3},{3,2},{4,5},{5,4},{6,7},{7,6},{8,9},{9,8},{10,11... | collective-permute-start | bytes 393224 | tf_op jit(solution)/shard_map/ppermute | solution.py:41

commit v2 on v1

--- a/solution.py
+++ b/solution.py
@@ -7,6 +7,7 @@
 from jax.experimental.pallas import tpu as pltpu
 from jax.sharding import PartitionSpec as P
 
+
 GROUP = 16
 BLK = 128
 SEQS = 4
@@ -43,22 +44,20 @@
 
 class Shape:
     def __init__(self, tokens, heads, depth, members):
-        self.tokens = tokens
         self.heads = heads
-        self.depth = depth
         self.members = members
         self.blocks = tokens // BLK
         self.rows = BLK * heads
         self.scale = depth**-0.5
 
 
-def place(dims):
+def place():
     ctx = lax.axis_index("ctx")
     return ctx % SEQS, ctx // SEQS
 
 
 def seen(dims, pos_ref, mask_ref, query_slot, hop, key_slot):
-    seq, member = place(dims)
+    seq, member = place()
     owner = (member - hop + dims.members) % dims.members
     query_id = pos_ref[seq, member * dims.blocks + query_slot]
     key_id = pos_ref[seq, owner * dims.blocks + key_slot]
@@ -253,7 +252,6 @@
     tokens, heads, depth = queries.shape
     kv_count = keys.shape[1]
     members = lax.axis_size("ctx") // SEQS
-    head_count = lax.axis_size("head")
     sharers = GROUP // heads
     dims = Shape(tokens, heads, depth, members)
     head_index = lax.axis_index("head")
@@ -347,7 +345,8 @@
     pair_far = keep_far + swapped(send_far, "head", 1).astype(f32)
     total = pair_far[:tokens]
     for hop in range(1, members):
-        moved = shifted(total.astype(travel), "ctx", SEQS).astype(f32)
+        moved = shifted(total.astype(travel), "ctx", SEQS)
+        moved = moved.astype(f32)
         if hop < members - 1:
             total = moved + pair_far[hop * tokens:(hop + 1) * tokens]
     total = moved + (keep_own + swapped(send_own, "head", 1).astype(f32))

time: 46.9 us -> 48.7 us (1.038); the launches traced: 47.5 us -> 48.4 us
  waiting for transfers between devices: 19.7 us -> 20.7 us
    ppermute x2, waiting for transfers between devices: 13.1 us -> 14.7 us  [shifted(): lax.ppermute(value, axis, [(i, (i + steps) % count) for i in range(count)])]
    pallas_call x1, Pallas kernels: 5.53 us -> 6.05 us  [per_device(): pl.pallas_call(functools.partial(far_kernel, dims), out_shape=(sds((block...]
  transfers between devices with their start and end apart: 7 -> 7, of which waited for: 5 -> 5; matrix products, arithmetic and copies ran while one was open for 0% -> 0% of each run, Pallas kernels for 22% -> 20%
where the time goes in v2:
time: 48.7 us; the launch traced here: 48.4 us
  waiting for transfers between devices  20.7 us (43%)
  Pallas kernels  15.9 us (33%)
  starting transfers between devices  6.47 us (13%)
  local copies, waits for them, and re-layouts  2.75 us (6%)
  other arithmetic  1.86 us (4%)
  between operations  0.75 us (2%)
    ppermute x2, waiting for transfers between devices, shifted(): lax.ppermute(value, axis, [(i, (i + steps) % count) for i in range(count)])  14.7 us
    pallas_call x1, Pallas kernels, per_device(): pl.pallas_call(functools.partial(own_grads_kernel, dims), out_shape=(sds(...  6.3 us
    pallas_call x1, Pallas kernels, per_device(): pl.pallas_call(functools.partial(far_kernel, dims), out_shape=(sds((block...  6.05 us
    ppermute x5, waiting for transfers between devices, swapped(): return lax.ppermute(value, axis, [(i, i ^ bit) for i in range(count)])  6.05 us
    ppermute x2, starting transfers between devices, shifted(): lax.ppermute(value, axis, [(i, (i + steps) % count) for i in range(count)])  4.2 us
    pallas_call x1, Pallas kernels, per_device(): pl.pallas_call(functools.partial(own_stats_kernel, dims), out_shape=sds((...  3.51 us
    unnamed x12, local copies, waits for them, and re-layouts  2.75 us
    ppermute x5, starting transfers between devices, swapped(): return lax.ppermute(value, axis, [(i, i ^ bit) for i in range(count)])  2.27 us
  transfers between devices with their start and end apart: 7, of which 5 were waited for; matrix products, arithmetic and copies ran while one was open for 0% of the time, Pallas kernels for 20%

profile of v2, /device:TPU:0, one launch (start us, length us, event | category | flops | bytes accessed | tf_op | source)
XLA Modules:
  0.0 48.4 jit_solution(3301447967558832827)
XLA Ops:
  0.6 0.0 copy-start
  0.7 0.0 copy-start.1
  0.7 0.0 copy-start.4
  0.7 1.0 %broadcast_select_fusion = bf16[512,128]{1,0:T(8,128)(2,1)S(1)} fusion(pred[]{:T(512)S(6)} %eq.5, bf16[512,1,128]{2,0,1:T(8,128)(2,1)} %param.8, bf16[512,1,128]{2,0,1:T(8,128)(2,1)} %param.7), kind=kLoop, calls=%fused_computation.5 | loop fusion | flops 65536 | bytes 393217 | tf_op jit(solution)/shard_map/jit(_where)/select_n | solution.py:268
  1.7 4.1 %collective-permute-start = (bf16[512,128]{1,0:T(8,128)(2,1)S(1)}, bf16[512,128]{1,0:T(8,128)(2,1)S(1)}, u32[]{:S(2)}, u32[]{:S(2)}) collective-permute-start(bf16[512,128]{1,0:T(8,128)(2,1)S(1)} %broadcast_select_fusion), channel_id=1, source_target_pairs={{0,16},{4,20},{8,24},{12,28},{16,0},{20,4},{24,8},{28,12},{1,17},{... | collective-permute-start | bytes 393224 | tf_op jit(solution)/shard_map/ppermute | solution.py:37
  5.8 6.3 %collective-permute-done.near_ref = bf16[512,128]{1,0:T(8,128)(2,1)S(1)} collective-permute-done((bf16[512,128]{1,0:T(8,128)(2,1)S(1)}, bf16[512,128]{1,0:T(8,128)(2,1)S(1)}, u32[]{:S(2)}, u32[]{:S(2)}) %collective-permute-start) | collective-permute-done | bytes 131104 | tf_op jit(solution)/shard_map/ppermute | solution.py:37
  12.1 0.0 collective-permute-start.1
  12.1 0.0 copy-start.5
  12.1 0.0 copy-done
  12.2 0.0 copy-done.1
  12.2 0.0 copy-done.4
  12.2 0.7 %copy-done.5 = s32[4,8]{1,0:T(4,128)S(1)} copy-done((s32[4,8]{1,0:T(4,128)S(1)}, s32[4,8]{1,0:T(4,128)}, u32[]{:S(2)}) %copy-start.5) | copy-done | bytes 152
  12.8 0.0 copy-start.2
  12.8 1.0 %copy-done.2 = bf16[512,4,128]{2,1,0:T(4,128)(2,1)S(1)} copy-done((bf16[512,4,128]{2,1,0:T(4,128)(2,1)S(1)}, bf16[512,4,128]{2,1,0:T(4,128)(2,1)}, u32[]{:S(2)}) %copy-start.2) | copy-done | bytes 524312
  13.9 0.0 copy-start.3
  13.9 1.0 %copy-done.3 = bf16[512,4,128]{2,1,0:T(4,128)(2,1)S(1)} copy-done((bf16[512,4,128]{2,1,0:T(4,128)(2,1)S(1)}, bf16[512,4,128]{2,1,0:T(4,128)(2,1)}, u32[]{:S(2)}) %copy-start.3) | copy-done | bytes 524312
  14.9 3.5 %own_stats.1.stats_ref = f32[4,3,8,512]{3,2,1,0:T(8,128)S(1)} custom-call(s32[4,8]{1,0:T(4,128)S(1)} %copy-done.5, s32[4,8,8]{2,1,0:T(8,128)S(1)} %copy-done.4, bf16[2048,128]{1,0:T(8,128)(2,1)S(1)} %bitcast.15, bf16[2048,128]{1,0:T(8,128)(2,1)S(1)} %bitcast.18, bf16[512,128]{1,0:T(8,128)(2,1)S(1)} %bitcast.11, bf16[512,128]{1,0:T(8,128)(2,1)S(1)} %bitcast.13), custom_call_target="tpu_custom_call" | custom-call | flops 536870912 | bytes 1048576 | tf_op jit(solution)/shard_map/own_stats/pallas_call | solution.py:288
  18.4 0.0 collective-permute-done.1.swap_ref
  18.4 6.1 %far_part.1 = (f32[4,2,8,512]{3,2,1,0:T(8,128)S(1)}, f32[4,128,512]{2,1,0:T(8,128)S(1)}, f32[512,128]{1,0:T(8,128)S(1)}, bf16[512,128]{1,0:T(8,128)(2,1)S(1)}) custom-call(s32[4,8]{1,0:T(4,128)S(1)} %copy-done.5, s32[4,8,8]{2,1,0:T(8,128)S(1)} %copy-done.4, bf16[2048,128]{1,0:T(8,128)(2,1)S(1)} %bitcast.16, bf16[2048,128]{1,0:T(8,128)(2,1)S(1)} %bitcast.19, ...), custom_call_target="tpu_custom_call" | custom-call | flops 1342177280 | bytes 1048576 | tf_op jit(solution)/shard_map/far_part/pallas_call | solution.py:299
  24.5 0.6 %collective-permute-start.2 = (bf16[512,128]{1,0:T(8,128)(2,1)S(1)}, bf16[512,128]{1,0:T(8,128)(2,1)S(1)}, u32[]{:S(2)}, u32[]{:S(2)}) collective-permute-start(bf16[512,128]{1,0:T(8,128)(2,1)S(1)} %get-tuple-element.14), channel_id=1, source_target_pairs={{0,1},{1,0},{2,3},{3,2},{4,5},{5,4},{6,7},{7,6},{8,9},{9,8},{10,11... | collective-permute-start | bytes 393224 | tf_op jit(solution)/shard_map/ppermute | solution.py:42
  25.1 6.3 %own_grads.1 = (bf16[2048,128]{1,0:T(8,128)(2,1)}, f32[512,128]{1,0:T(8,128)S(1)}, bf16[512,128]{1,0:T(8,128)(2,1)S(1)}) custom-call(s32[4,8]{1,0:T(4,128)S(1)} %copy-done.5, s32[4,8,8]{2,1,0:T(8,128)S(1)} %copy-done.4, bf16[2048,128]{1,0:T(8,128)(2,1)S(1)} %bitcast.17, bf16[2048,128]{1,0:T(8,128)(2,1)S(1)} %bitcast.20, bf16[512,128]{1,0:T(8,128)(2,1)S(1)} %bitcast.12, ...), custom_call_target="tpu_custom_call" | custom-call | flops 1342177280 | bytes 1048576 | tf_op jit(solution)/shard_map/own_grads/pallas_call | solution.py:324
  31.4 0.0 collective-permute-start.4
  31.4 0.0 collective-permute-done.2
  31.4 0.1 collective-permute-start.3
  31.5 1.2 %collective-permute-done.4 = bf16[512,128]{1,0:T(8,128)(2,1)S(1)} collective-permute-done((bf16[512,128]{1,0:T(8,128)(2,1)S(1)}, bf16[512,128]{1,0:T(8,128)(2,1)S(1)}, u32[]{:S(2)}, u32[]{:S(2)}) %collective-permute-start.4) | collective-permute-done | bytes 131104 | tf_op jit(solution)/shard_map/ppermute | solution.py:42
  32.7 8.4 %collective-permute-done.3 = bf16[512,128]{1,0:T(8,128)(2,1)S(1)} collective-permute-done((bf16[512,128]{1,0:T(8,128)(2,1)S(1)}, bf16[512,128]{1,0:T(8,128)(2,1)S(1)}, u32[]{:S(2)}, u32[]{:S(2)}) %collective-permute-start.3) | collective-permute-done | bytes 131104 | tf_op jit(solution)/shard_map/ppermute | solution.py:37
  41.1 1.6 %collective-permute-start.5 = (bf16[512,128]{1,0:T(8,128)(2,1)S(1)}, bf16[512,128]{1,0:T(8,128)(2,1)S(1)}, u32[]{:S(2)}, u32[]{:S(2)}) collective-permute-start(bf16[512,128]{1,0:T(8,128)(2,1)S(1)} %add_convert_fusion.1), channel_id=1, source_target_pairs={{0,2},{1,3},{2,0},{3,1},{4,6},{5,7},{6,4},{7,5},{8,10},{9,11},{10,... | collective-permute-start | bytes 393224 | tf_op jit(solution)/shard_map/ppermute | solution.py:42
  42.7 3.5 %collective-permute-done.5 = bf16[512,128]{1,0:T(8,128)(2,1)S(1)} collective-permute-done((bf16[512,128]{1,0:T(8,128)(2,1)S(1)}, bf16[512,128]{1,0:T(8,128)(2,1)S(1)}, u32[]{:S(2)}, u32[]{:S(2)}) %collective-permute-start.5) | collective-permute-done | bytes 131104 | tf_op jit(solution)/shard_map/ppermute | solution.py:42
  46.3 0.1 collective-permute-start.6
  46.4 1.3 %collective-permute-done.6 = bf16[512,128]{1,0:T(8,128)(2,1)S(1)} collective-permute-done((bf16[512,128]{1,0:T(8,128)(2,1)S(1)}, bf16[512,128]{1,0:T(8,128)(2,1)S(1)}, u32[]{:S(2)}, u32[]{:S(2)}) %collective-permute-start.6) | collective-permute-done | bytes 131104 | tf_op jit(solution)/shard_map/ppermute | solution.py:42
  47.7 0.7 %select_bitcast_fusion = (bf16[512,1,128]{2,0,1:T(8,128)(2,1)}, bf16[512,1,128]{2,0,1:T(8,128)(2,1)}) fusion(bf16[512,128]{1,0:T(8,128)(2,1)S(1)} %collective-permute-done.6, bf16[512,128]{1,0:T(8,128)(2,1)S(1)} %add_convert_fusion, pred[]{:T(512)S(6)} %eq.5), kind=kLoop, calls=%fused_computation.3 | loop fusion | flops 131072 | bytes 524289 | tf_op jit(solution)/shard_map/broadcast_in_dim | solution.py:368
  (3 shorter events, 0.1 us)
Async XLA Ops:
  0.6 11.5 %copy-start = (bf16[512,1,128]{2,0,1:T(8,128)(2,1)S(1)}, bf16[512,1,128]{2,0,1:T(8,128)(2,1)}, u32[]{:S(2)}) copy-start(bf16[512,1,128]{2,0,1:T(8,128)(2,1)} %param.7) | copy-start | bytes 393220
  0.7 11.5 %copy-start.1 = (bf16[512,1,128]{2,0,1:T(8,128)(2,1)S(1)}, bf16[512,1,128]{2,0,1:T(8,128)(2,1)}, u32[]{:S(2)}) copy-start(bf16[512,1,128]{2,0,1:T(8,128)(2,1)} %param.8) | copy-start | bytes 393220
  0.7 11.5 %copy-start.4 = (s32[4,8,8]{2,1,0:T(8,128)S(1)}, s32[4,8,8]{2,1,0:T(8,128)}, u32[]{:S(2)}) copy-start(s32[4,8,8]{2,1,0:T(8,128)} %mask_ref.5) | copy-start | bytes 3076
  1.7 10.4 %collective-permute-start = (bf16[512,128]{1,0:T(8,128)(2,1)S(1)}, bf16[512,128]{1,0:T(8,128)(2,1)S(1)}, u32[]{:S(2)}, u32[]{:S(2)}) collective-permute-start(bf16[512,128]{1,0:T(8,128)(2,1)S(1)} %broadcast_select_fusion), channel_id=1, source_target_pairs={{0,16},{4,20},{8,24},{12,28},{16,0},{20,4},{24,8},{28,12},{1,17},{... | collective-permute-start | bytes 393224 | tf_op jit(solution)/shard_map/ppermute | solution.py:37
  12.1 6.3 %collective-permute-start.1 = (bf16[512,128]{1,0:T(8,128)(2,1)S(1)}, bf16[512,128]{1,0:T(8,128)(2,1)S(1)}, u32[]{:S(2)}, u32[]{:S(2)}) collective-permute-start(bf16[512,128]{1,0:T(8,128)(2,1)S(1)} %collective-permute-done.near_ref), channel_id=1, source_target_pairs={{0,1},{1,0},{2,3},{3,2},{4,5},{5,4},{6,7},{7,6},{8,9},{9,8},{10,11... | collective-permute-start | bytes 393224 | tf_op jit(solution)/shard_map/ppermute | solution.py:42
  12.1 0.7 %copy-start.5 = (s32[4,8]{1,0:T(4,128)S(1)}, s32[4,8]{1,0:T(4,128)}, u32[]{:S(2)}) copy-start(s32[4,8]{1,0:T(4,128)} %pos_ref.5) | copy-start | bytes 388
  12.8 1.0 %copy-start.2 = (bf16[512,4,128]{2,1,0:T(4,128)(2,1)S(1)}, bf16[512,4,128]{2,1,0:T(4,128)(2,1)}, u32[]{:S(2)}) copy-start(bf16[512,4,128]{2,1,0:T(4,128)(2,1)} %param.6) | copy-start | bytes 1572868
  13.9 1.0 %copy-start.3 = (bf16[512,4,128]{2,1,0:T(4,128)(2,1)S(1)}, bf16[512,4,128]{2,1,0:T(4,128)(2,1)}, u32[]{:S(2)}) copy-start(bf16[512,4,128]{2,1,0:T(4,128)(2,1)} %param.9) | copy-start | bytes 1572868
  24.5 6.9 %collective-permute-start.2 = (bf16[512,128]{1,0:T(8,128)(2,1)S(1)}, bf16[512,128]{1,0:T(8,128)(2,1)S(1)}, u32[]{:S(2)}, u32[]{:S(2)}) collective-permute-start(bf16[512,128]{1,0:T(8,128)(2,1)S(1)} %get-tuple-element.14), channel_id=1, source_target_pairs={{0,1},{1,0},{2,3},{3,2},{4,5},{5,4},{6,7},{7,6},{8,9},{9,8},{10,11... | collective-permute-start | bytes 393224 | tf_op jit(solution)/shard_map/ppermute | solution.py:42
  31.4 1.3 %collective-permute-start.4 = (bf16[512,128]{1,0:T(8,128)(2,1)S(1)}, bf16[512,128]{1,0:T(8,128)(2,1)S(1)}, u32[]{:S(2)}, u32[]{:S(2)}) collective-permute-start(bf16[512,128]{1,0:T(8,128)(2,1)S(1)} %get-tuple-element.16), channel_id=1, source_target_pairs={{0,1},{1,0},{2,3},{3,2},{4,5},{5,4},{6,7},{7,6},{8,9},{9,8},{10,11... | collective-permute-start | bytes 393224 | tf_op jit(solution)/shard_map/ppermute | solution.py:42
  31.4 9.7 %collective-permute-start.3 = (bf16[512,128]{1,0:T(8,128)(2,1)S(1)}, bf16[512,128]{1,0:T(8,128)(2,1)S(1)}, u32[]{:S(2)}, u32[]{:S(2)}) collective-permute-start(bf16[512,128]{1,0:T(8,128)(2,1)S(1)} %add_convert_fusion.2), channel_id=1, source_target_pairs={{0,16},{4,20},{8,24},{12,28},{16,0},{20,4},{24,8},{28,12},{1,17},{... | collective-permute-start | bytes 393224 | tf_op jit(solution)/shard_map/ppermute | solution.py:37
  41.1 5.1 %collective-permute-start.5 = (bf16[512,128]{1,0:T(8,128)(2,1)S(1)}, bf16[512,128]{1,0:T(8,128)(2,1)S(1)}, u32[]{:S(2)}, u32[]{:S(2)}) collective-permute-start(bf16[512,128]{1,0:T(8,128)(2,1)S(1)} %add_convert_fusion.1), channel_id=1, source_target_pairs={{0,2},{1,3},{2,0},{3,1},{4,6},{5,7},{6,4},{7,5},{8,10},{9,11},{10,... | collective-permute-start | bytes 393224 | tf_op jit(solution)/shard_map/ppermute | solution.py:42
  46.3 1.4 %collective-permute-start.6 = (bf16[512,128]{1,0:T(8,128)(2,1)S(1)}, bf16[512,128]{1,0:T(8,128)(2,1)S(1)}, u32[]{:S(2)}, u32[]{:S(2)}) collective-permute-start(bf16[512,128]{1,0:T(8,128)(2,1)S(1)} %add_convert_fusion), channel_id=1, source_target_pairs={{0,1},{1,0},{2,3},{3,2},{4,5},{5,4},{6,7},{7,6},{8,9},{9,8},{10,11... | collective-permute-start | bytes 393224 | tf_op jit(solution)/shard_map/ppermute | solution.py:42

commit v3 on v2

v3 whole, which is shorter than its diff:
```python
import functools

import jax
import jax.numpy as jnp
from jax import lax
from jax.experimental import pallas as pl
from jax.experimental.pallas import tpu as pltpu
from jax.sharding import PartitionSpec as P


GROUP = 16
BLK = 128
SEQS = 4
LOG2E = 1.4426950408889634
MASKED = -1e30
SUB = 8


def dot_nt(left, right):
    return lax.dot_general(
        left, right, (((1,), (1,)), ((), ())), preferred_element_type=jnp.float32
    )


def dot_nn(left, right):
    return lax.dot_general(
        left, right, (((1,), (0,)), ((), ())), preferred_element_type=jnp.float32
    )


def by_sublane(value):
    return value.reshape(value.shape[0] // SUB, SUB, value.shape[1])


def shifted(value, axis, steps):
    count = lax.axis_size(axis)
    return lax.ppermute(value, axis, [(i, (i + steps) % count) for i in range(count)])


def swapped(value, axis, bit):
    count = lax.axis_size(axis)
    return lax.ppermute(value, axis, [(i, i ^ bit) for i in range(count)])


class Shape:
    def __init__(self, tokens, heads, depth, members):
        self.heads = heads
        self.members = members
        self.blocks = tokens // BLK
        self.far = (members - 1) * self.blocks
        self.rows = BLK * heads
        self.scale = depth**-0.5
        self.keep_tiles = self.blocks * self.far <= 32


FAR_Q, FAR_K, OWN_Q, OWN_K, COUNTS = range(5)
PLAN = (8, 128)


def causal_logits(dims, logits):
    key_token = lax.broadcasted_iota(jnp.int32, logits.shape, 0)
    query_token = lax.broadcasted_iota(jnp.int32, logits.shape, 1) // dims.heads
    return jnp.where(key_token <= query_token, logits, MASKED)


def stats_of(logits, dprob):
    parts = by_sublane(logits)
    top = jnp.max(parts, axis=0)
    exps = jnp.exp2(parts - top[None])
    return top, jnp.sum(exps, axis=0), jnp.sum(exps * by_sublane(dprob), axis=0)


def merged(first, second):
    top = jnp.maximum(first[0], second[0])
    one, two = jnp.exp2(first[0] - top), jnp.exp2(second[0] - top)
    return top, first[1] * one + second[1] * two, first[2] * one + second[2] * two


def load_stats(ref, slot):
    return ref[slot, 0], ref[slot, 1], ref[slot, 2]


def store_stats(ref, slot, stats):
    for index in range(3):
        ref[slot, index] = stats[index]


def rows_of(ref, slot, count):
    return ref[pl.ds(pl.multiple_of(slot * count, count), count), :]


def build_plan(dims, pos_ref, mask_ref, plan_ref):
    ctx = lax.axis_index("ctx")
    seq, member = lax.rem(ctx, SEQS), lax.div(ctx, SEQS)
    query_ids = [pos_ref[seq, member * dims.blocks + slot] for slot in range(dims.blocks)]

    def listed(row_q, row_k, row_count, hops):
        total = jnp.int32(0)
        for hop in hops:
            owner = member - hop
            owner = jnp.where(owner < 0, owner + dims.members, owner)
            key_ids = [pos_ref[seq, owner * dims.blocks + slot] for slot in range(dims.blocks)]
            for query_slot in range(dims.blocks):
                for key_slot in range(dims.blocks):
                    if hop == 0 and key_slot == query_slot:
                        continue
                    query_id, key_id = query_ids[query_slot], key_ids[key_slot]
                    seen = jnp.logical_and(key_id < query_id, mask_ref[seq, query_id, key_id] == 1)
                    plan_ref[row_q, total] = query_slot
                    plan_ref[row_k, total] = key_slot + max(hop - 1, 0) * dims.blocks
                    total = total + seen.astype(jnp.int32)
        plan_ref[row_q, total] = dims.blocks
        plan_ref[row_k, total] = dims.blocks if row_count else dims.far
        plan_ref[COUNTS, row_count] = lax.div(total + 1, 2)

    listed(OWN_Q, OWN_K, 1, range(1))
    listed(FAR_Q, FAR_K, 0, range(1, dims.members))


def two_at_once(count, front, back):
    def trip(step, carry):
        first, second = 2 * step, 2 * step + 1
        one, two = front(first), front(second)
        back(first, one)
        back(second, two)
        return carry

    lax.fori_loop(0, count, trip, 0)


def own_stats_kernel(
    dims, pos_hbm, mask_hbm, q_hbm, g_hbm, k_hbm, v_hbm,
    stats_ref, plan_ref, q_ref, g_ref, k_ref, v_ref,
    pos_ref, mask_ref, sums, whole_sems, slot_sems,
):
    factor = dims.scale * LOG2E
    whole = [
        pltpu.make_async_copy(source, target, whole_sems.at[index])
        for index, (source, target) in enumerate(
            ((pos_hbm, pos_ref), (mask_hbm, mask_ref), (k_hbm, k_ref), (v_hbm, v_ref))
        )
    ]
    slots = [
        [
            pltpu.make_async_copy(
                source.at[pl.ds(slot * dims.rows, dims.rows)],
                target.at[pl.ds(slot * dims.rows, dims.rows)],
                slot_sems.at[index, slot],
            )
            for index, (source, target) in enumerate(((q_hbm, q_ref), (g_hbm, g_ref)))
        ]
        for slot in range(dims.blocks)
    ]
    for copy in whole:
        copy.start()
    for pair in slots:
        for copy in pair:
            copy.start()
    whole[0].wait()
    whole[1].wait()
    build_plan(dims, pos_ref, mask_ref, plan_ref)
    whole[2].wait()
    whole[3].wait()

    def tile(query_slot, key_slot, mask):
        query_slot = jnp.minimum(query_slot, dims.blocks - 1)
        key_slot = jnp.minimum(key_slot, dims.blocks - 1)
        logits = dot_nt(rows_of(k_ref, key_slot, BLK), rows_of(q_ref, query_slot, dims.rows)) * factor
        dprob = dot_nt(rows_of(v_ref, key_slot, BLK), rows_of(g_ref, query_slot, dims.rows))
        return stats_of(causal_logits(dims, logits) if mask else logits, dprob)

    for slot in range(dims.blocks):
        slots[slot][0].wait()
        slots[slot][1].wait()
        store_stats(sums, slot, tile(slot, slot, True))

    def front(pair):
        return tile(plan_ref[OWN_Q, pair], plan_ref[OWN_K, pair], False)

    def back(pair, stats):
        slot = plan_ref[OWN_Q, pair]
        store_stats(sums, slot, merged(load_stats(sums, slot), stats))

    two_at_once(plan_ref[COUNTS, 1], front, back)
    stats_ref[...] = sums[0:dims.blocks]


def far_kernel(
    dims, plan_hbm, q_ref, g_ref, near_ref, swap_ref, stats_ref,
    final_ref, ds_ref, keep_ref, send_ref,
    plan_ref, plan_sem, k_all, v_all, run, logit_all, dprob_all, dk_all, dv_all,
):
    factor = dims.scale * LOG2E
    first_core = lax.rem(lax.axis_index("head"), 2) == 0
    load_plan = pltpu.make_async_copy(plan_hbm, plan_ref, plan_sem)
    load_plan.start()

    @pl.when(first_core)
    def _():
        k_all[...] = near_ref[...]
        v_all[...] = swap_ref[...]

    @pl.when(jnp.logical_not(first_core))
    def _():
        k_all[...] = swap_ref[...]
        v_all[...] = near_ref[...]

    dk_all[...] = jnp.zeros_like(dk_all)
    dv_all[...] = jnp.zeros_like(dv_all)
    run[0:dims.blocks] = stats_ref[...]
    load_plan.wait()
    count = plan_ref[COUNTS, 0]

    def places(pair):
        query_slot, key_slot = plan_ref[FAR_Q, pair], plan_ref[FAR_K, pair]
        return jnp.minimum(query_slot, dims.blocks - 1), jnp.minimum(key_slot, dims.far - 1)

    def tile(pair):
        query_slot, key_slot = places(pair)
        logits = dot_nt(rows_of(k_all, key_slot, BLK), rows_of(q_ref, query_slot, dims.rows)) * factor
        dprob = dot_nt(rows_of(v_all, key_slot, BLK), rows_of(g_ref, query_slot, dims.rows))
        return logits, dprob

    def stats_front(pair):
        logits, dprob = tile(pair)
        if dims.keep_tiles:
            logit_all[pair] = logits
            dprob_all[pair] = dprob
        return stats_of(logits, dprob)

    def stats_back(pair, stats):
        slot = plan_ref[FAR_Q, pair]
        store_stats(run, slot, merged(load_stats(run, slot), stats))

    two_at_once(count, stats_front, stats_back)

    for slot in range(dims.blocks):
        tops, totals, weighted = load_stats(run, slot)
        top = jnp.max(tops, axis=0, keepdims=True)
        factors = jnp.exp2(tops - top)
        total = jnp.sum(totals * factors, axis=0, keepdims=True)
        log_sum = top + jnp.log2(total)
        delta = jnp.sum(weighted * factors, axis=0, keepdims=True) / total
        final_ref[slot, 0] = jnp.broadcast_to(log_sum, tops.shape)
        final_ref[slot, 1] = jnp.broadcast_to(delta, tops.shape)

    def grads_front(pair):
        query_slot, _ = places(pair)
        logits, dprob = (logit_all[pair], dprob_all[pair]) if dims.keep_tiles else tile(pair)
        return gradient_tiles(dims, logits, dprob, final_ref, query_slot)

    def grads_back(pair, tiles):
        probs, dscore = tiles
        query_slot, _ = places(pair)
        key_slot = plan_ref[FAR_K, pair]
        ds_ref[pair] = dscore
        dk_all[key_slot] += dot_nn(dscore, rows_of(q_ref, query_slot, dims.rows))
        dv_all[key_slot] += dot_nn(probs, rows_of(g_ref, query_slot, dims.rows))

    two_at_once(count, grads_front, grads_back)
    share_out(dims, dims.far, first_core, dk_all, dv_all, keep_ref, send_ref)


def gradient_tiles(dims, logits, dprob, final_ref, slot):
    probs = jnp.exp2(by_sublane(logits) - final_ref[slot, 0][None])
    dscore = probs * (by_sublane(dprob) - final_ref[slot, 1][None])
    return (
        probs.reshape(BLK, dims.rows).astype(jnp.bfloat16),
        dscore.reshape(BLK, dims.rows).astype(jnp.bfloat16),
    )


def share_out(dims, count, first_core, dk_all, dv_all, keep_ref, send_ref):
    shape = keep_ref.shape

    @pl.when(first_core)
    def _():
        keep_ref[...] = (dk_all[0:count] * dims.scale).reshape(shape)
        send_ref[...] = dv_all[0:count].reshape(shape).astype(send_ref.dtype)

    @pl.when(jnp.logical_not(first_core))
    def _():
        keep_ref[...] = dv_all[0:count].reshape(shape)
        send_ref[...] = (dk_all[0:count] * dims.scale).reshape(shape).astype(send_ref.dtype)


def own_grads_kernel(
    dims, plan_hbm, q_ref, g_ref, k_ref, v_ref, near_ref, swap_ref, final_ref, ds_ref,
    dq_ref, keep_ref, send_ref,
    plan_ref, plan_sem, kt_own, kt_far, dq_all, dk_all, dv_all,
):
    factor = dims.scale * LOG2E
    first_core = lax.rem(lax.axis_index("head"), 2) == 0
    load_plan = pltpu.make_async_copy(plan_hbm, plan_ref, plan_sem)
    load_plan.start()
    for index in range(dims.blocks):
        kt_own[index] = k_ref[index * BLK:(index + 1) * BLK, :].T

    @pl.when(first_core)
    def _():
        for index in range(dims.far):
            kt_far[index] = near_ref[index * BLK:(index + 1) * BLK, :].T

    @pl.when(jnp.logical_not(first_core))
    def _():
        for index in range(dims.far):
            kt_far[index] = swap_ref[index * BLK:(index + 1) * BLK, :].T

    def tile(query_slot, key_slot, mask):
        logits = dot_nt(rows_of(k_ref, key_slot, BLK), rows_of(q_ref, query_slot, dims.rows)) * factor
        dprob = dot_nt(rows_of(v_ref, key_slot, BLK), rows_of(g_ref, query_slot, dims.rows))
        logits = causal_logits(dims, logits) if mask else logits
        return gradient_tiles(dims, logits, dprob, final_ref, query_slot)

    for slot in range(dims.blocks):
        probs, dscore = tile(slot, slot, True)
        dk_all[slot] = dot_nn(dscore, rows_of(q_ref, slot, dims.rows))
        dv_all[slot] = dot_nn(probs, rows_of(g_ref, slot, dims.rows))
        dq_all[slot] = dot_nn(kt_own[slot], dscore)
    load_plan.wait()

    def places(pair):
        query_slot, key_slot = plan_ref[OWN_Q, pair], plan_ref[OWN_K, pair]
        return jnp.minimum(query_slot, dims.blocks - 1), jnp.minimum(key_slot, dims.blocks - 1)

    def front(pair):
        return tile(*places(pair), False)

    def back(pair, tiles):
        probs, dscore = tiles
        query_slot, key_slot = places(pair)
        dk_all[plan_ref[OWN_K, pair]] += dot_nn(dscore, rows_of(q_ref, query_slot, dims.rows))
        dv_all[plan_ref[OWN_K, pair]] += dot_nn(probs, rows_of(g_ref, query_slot, dims.rows))
        dq_all[plan_ref[OWN_Q, pair]] += dot_nn(kt_own[key_slot], dscore)

    two_at_once(plan_ref[COUNTS, 1], front, back)

    def far_front(pair):
        key_slot = jnp.minimum(plan_ref[FAR_K, pair], dims.far - 1)
        return dot_nn(kt_far[key_slot], ds_ref[pair])

    def far_back(pair, part):
        dq_all[plan_ref[FAR_Q, pair]] += part

    two_at_once(plan_ref[COUNTS, 0], far_front, far_back)

    for slot in range(dims.blocks):
        start = slot * dims.rows
        dq_ref[start:start + dims.rows, :] = (dq_all[slot] * dims.scale).T.astype(dq_ref.dtype)

    share_out(dims, dims.blocks, first_core, dk_all, dv_all, keep_ref, send_ref)


VMEM = pl.BlockSpec(memory_space=pltpu.VMEM)
SMEM = pl.BlockSpec(memory_space=pltpu.SMEM)
HBM = pl.BlockSpec(memory_space=pltpu.HBM)


def per_device(queries, keys, values, d_out, block_pos, block_mask):
    tokens, heads, depth = queries.shape
    kv_count = keys.shape[1]
    members = lax.axis_size("ctx") // SEQS
    sharers = GROUP // heads
    dims = Shape(tokens, heads, depth, members)
    head_index = lax.axis_index("head")
    kv_index = head_index // sharers
    first_core = head_index % 2 == 0
    f32, bf16 = jnp.float32, jnp.bfloat16
    sds = jax.ShapeDtypeStruct

    key_own = lax.dynamic_index_in_dim(keys, kv_index, 1, keepdims=False) if kv_count > 1 else keys[:, 0]
    value_own = lax.dynamic_index_in_dim(values, kv_index, 1, keepdims=False) if kv_count > 1 else values[:, 0]
    query_rows = queries.reshape(tokens * heads, depth)
    grad_rows = d_out.reshape(tokens * heads, depth)

    passed = jnp.where(first_core, key_own, value_own)
    near, swap = [], []
    for _ in range(members - 1):
        passed = shifted(passed, "ctx", SEQS)
        near.append(passed)
        swap.append(swapped(passed, "head", 1))
    near = near[0] if members == 2 else jnp.concatenate(near)
    swap = swap[0] if members == 2 else jnp.concatenate(swap)

    params = pltpu.CompilerParams(vmem_limit_bytes=16 << 20)
    blocks, rows = dims.blocks, dims.rows
    tile_flops = 2 * BLK * rows * depth

    def cost(tiles, dots):
        return pl.CostEstimate(
            flops=tiles * dots * tile_flops,
            bytes_accessed=4 * tokens * heads * depth,
            transcendentals=tiles * BLK * rows,
        )

    stats, plan, query_rows, grad_rows, key_own, value_own = pl.pallas_call(
        functools.partial(own_stats_kernel, dims),
        out_shape=(
            sds((blocks, 3, SUB, rows), f32),
            sds(PLAN, jnp.int32),
            sds((tokens * heads, depth), bf16),
            sds((tokens * heads, depth), bf16),
            sds((tokens, depth), bf16),
            sds((tokens, depth), bf16),
        ),
        in_specs=[HBM] * 6,
        out_specs=(VMEM, SMEM) + (VMEM,) * 4,
        scratch_shapes=[
            pltpu.SMEM(block_pos.shape, jnp.int32),
            pltpu.SMEM(block_mask.shape, jnp.int32),
            pltpu.VMEM((blocks + 1, 3, SUB, rows), f32),
            pltpu.SemaphoreType.DMA((4,)),
            pltpu.SemaphoreType.DMA((2, blocks)),
        ],
        compiler_params=params,
        cost_estimate=cost(blocks * blocks, 2),
        name="own_stats",
    )(
        *(
            pltpu.with_memory_space_constraint(operand, pltpu.HBM)
            for operand in (block_pos, block_mask, query_rows, grad_rows, key_own, value_own)
        )
    )

    far = dims.far
    pairs = blocks * far + 2
    kept = pairs if dims.keep_tiles else 1
    final, far_scores, keep_far, send_far = pl.pallas_call(
        functools.partial(far_kernel, dims),
        out_shape=(
            sds((blocks, 2, SUB, rows), f32),
            sds((pairs, BLK, rows), bf16),
            sds((far * BLK, depth), f32),
            sds((far * BLK, depth), bf16),
        ),
        in_specs=[VMEM] * 6,
        out_specs=(VMEM,) * 4,
        scratch_shapes=[
            pltpu.SMEM(PLAN, jnp.int32),
            pltpu.SemaphoreType.DMA,
            pltpu.VMEM((far * BLK, depth), bf16),
            pltpu.VMEM((far * BLK, depth), bf16),
            pltpu.VMEM((blocks + 1, 3, SUB, rows), f32),
            pltpu.VMEM((kept, BLK, rows), f32),
            pltpu.VMEM((kept, BLK, rows), f32),
            pltpu.VMEM((far + 1, BLK, depth), f32),
            pltpu.VMEM((far + 1, BLK, depth), f32),
        ],
        compiler_params=params,
        cost_estimate=cost(blocks * far, 4),
        name="far_part",
    )(plan, query_rows, grad_rows, near, swap, stats)

    dq, keep_own, send_own = pl.pallas_call(
        functools.partial(own_grads_kernel, dims),
        out_shape=(
            sds((tokens * heads, depth), bf16),
            sds((tokens, depth), f32),
            sds((tokens, depth), bf16),
        ),
        in_specs=[VMEM] * 9,
        out_specs=(VMEM,) * 3,
        scratch_shapes=[
            pltpu.SMEM(PLAN, jnp.int32),
            pltpu.SemaphoreType.DMA,
            pltpu.VMEM((blocks, depth, BLK), bf16),
            pltpu.VMEM((far, depth, BLK), bf16),
            pltpu.VMEM((blocks + 1, depth, rows), f32),
            pltpu.VMEM((blocks + 1, BLK, depth), f32),
            pltpu.VMEM((blocks + 1, BLK, depth), f32),
        ],
        compiler_params=params,
        cost_estimate=cost(blocks * (blocks + far), 5),
        name="own_grads",
    )(plan, query_rows, grad_rows, key_own, value_own, near, swap, final, far_scores)

    travel = bf16 if members == 2 else f32
    pair_far = keep_far + swapped(send_far, "head", 1).astype(f32)
    total = pair_far[:tokens]
    for hop in range(1, members):
        moved = shifted(total.astype(travel), "ctx", SEQS)
        moved = moved.astype(f32)
        if hop < members - 1:
            total = moved + pair_far[hop * tokens:(hop + 1) * tokens]
    total = moved + (keep_own + swapped(send_own, "head", 1).astype(f32))
    bit = 2
    total = total.astype(bf16)
    while bit < sharers:
        total = (total.astype(f32) + swapped(total, "head", bit).astype(f32)).astype(bf16)
        bit *= 2
    other = swapped(total, "head", 1)
    d_keys = jnp.where(first_core, total, other)
    d_values = jnp.where(first_core, other, total)
    if kv_count > 1:
        groups = [[p + sharers * g for g in range(kv_count)] for p in range(sharers)]
        both = lax.all_gather(
            jnp.stack([d_keys, d_values]), "head", axis=2, axis_index_groups=groups
        )
        d_keys, d_values = both[0], both[1]
    else:
        d_keys, d_values = d_keys[:, None], d_values[:, None]
    return dq.reshape(tokens, heads, depth), d_keys, d_values


def solution(mesh):
    placed = (
        P("ctx", "head", None),
        P("ctx", None, None),
        P("ctx", None, None),
        P("ctx", "head", None),
        P(),
        P(),
    )
    return jax.shard_map(
        per_device,
        mesh=mesh,
        in_specs=placed,
        out_specs=(P("ctx", "head", None), P("ctx", None, None), P("ctx", None, None)),
        check_vma=False,
    )
```

time: 48.7 us -> 41.5 us (0.85)
  Pallas kernels: 15.9 us -> 11.6 us
  local copies, waits for them, and re-layouts: 2.75 us -> 0 us
    unnamed x12 -> x0, local copies, waits for them, and re-layouts: 2.75 us -> none
    pallas_call x1, Pallas kernels: 6.05 us -> 3.41 us  [per_device(): pl.pallas_call(functools.partial(far_kernel, dims), out_shape=(sds((block...]
    pallas_call x1, Pallas kernels: 6.3 us -> 4.47 us  [per_device(): pl.pallas_call(functools.partial(own_grads_kernel, dims), out_shape=(sds(...]
where the time goes in v3:
time: 41.5 us; the launch traced here: 41.4 us
  waiting for transfers between devices  20.6 us (50%)
  Pallas kernels  11.6 us (28%)
  starting transfers between devices  6.57 us (16%)
  other arithmetic  1.82 us (4%)
  between operations  0.71 us (2%)
    ppermute x2, waiting for transfers between devices, shifted(): lax.ppermute(value, axis, [(i, (i + steps) % count) for i in range(count)])  14.7 us
    ppermute x5, waiting for transfers between devices, swapped(): return lax.ppermute(value, axis, [(i, i ^ bit) for i in range(count)])  5.97 us
    pallas_call x1, Pallas kernels, per_device(): pl.pallas_call(functools.partial(own_grads_kernel, dims), out_shape=(sds(...  4.47 us
    ppermute x2, starting transfers between devices, shifted(): lax.ppermute(value, axis, [(i, (i + steps) % count) for i in range(count)])  4.2 us
    pallas_call x1, Pallas kernels, per_device(): pl.pallas_call(functools.partial(own_stats_kernel, dims), out_shape=(sds(...  3.73 us
    pallas_call x1, Pallas kernels, per_device(): pl.pallas_call(functools.partial(far_kernel, dims), out_shape=(sds((block...  3.41 us
    ppermute x5, starting transfers between devices, swapped(): return lax.ppermute(value, axis, [(i, i ^ bit) for i in range(count)])  2.37 us
    select_n x1, other arithmetic, per_device(): passed = jnp.where(first_core, key_own, value_own)  0.99 us
  transfers between devices with their start and end apart: 7, of which 5 were waited for; matrix products, arithmetic and copies ran while one was open for 0% of the time, Pallas kernels for 20%

profile of v3, /device:TPU:0, one launch (start us, length us, event | category | flops | bytes accessed | tf_op | source)
XLA Modules:
  0.0 41.4 jit_solution(15133329450890235025)
XLA Ops:
  0.6 1.0 %broadcast_select_fusion = bf16[512,128]{1,0:T(8,128)(2,1)S(1)} fusion(pred[]{:T(512)S(6)} %eq.5, bf16[512,1,128]{2,0,1:T(8,128)(2,1)} %param.8, bf16[512,1,128]{2,0,1:T(8,128)(2,1)} %param.7), kind=kLoop, calls=%fused_computation.5 | loop fusion | flops 65536 | bytes 393217 | tf_op jit(solution)/shard_map/jit(_where)/select_n | solution.py:376
  1.6 4.1 %collective-permute-start = (bf16[512,128]{1,0:T(8,128)(2,1)S(1)}, bf16[512,128]{1,0:T(8,128)(2,1)S(1)}, u32[]{:S(2)}, u32[]{:S(2)}) collective-permute-start(bf16[512,128]{1,0:T(8,128)(2,1)S(1)} %broadcast_select_fusion), channel_id=1, source_target_pairs={{0,16},{4,20},{8,24},{12,28},{16,0},{20,4},{24,8},{28,12},{1,17},{... | collective-permute-start | bytes 393224 | tf_op jit(solution)/shard_map/ppermute | solution.py:37
  5.8 6.3 %collective-permute-done.near_ref = bf16[512,128]{1,0:T(8,128)(2,1)S(1)} collective-permute-done((bf16[512,128]{1,0:T(8,128)(2,1)S(1)}, bf16[512,128]{1,0:T(8,128)(2,1)S(1)}, u32[]{:S(2)}, u32[]{:S(2)}) %collective-permute-start) | collective-permute-done | bytes 131104 | tf_op jit(solution)/shard_map/ppermute | solution.py:37
  12.1 0.0 collective-permute-start.1
  12.1 3.7 %own_stats.1 = (f32[4,3,8,512]{3,2,1,0:T(8,128)S(1)}, s32[8,128]{1,0:T(8,128)S(1)}, bf16[2048,128]{1,0:T(8,128)(2,1)S(1)}, bf16[2048,128]{1,0:T(8,128)(2,1)S(1)}...) custom-call(s32[4,8]{1,0:T(4,128)} %pos_hbm.1, s32[4,8,8]{2,1,0:T(8,128)} %mask_hbm.1, ...), custom_call_target="tpu_custom_call" | custom-call | flops 536870912 | bytes 1048576 | tf_op jit(solution)/shard_map/own_stats/pallas_call | solution.py:396
  15.8 0.0 collective-permute-done.1.swap_ref
  15.8 3.4 %far_part.1 = (f32[4,2,8,512]{3,2,1,0:T(8,128)S(1)}, bf16[18,128,512]{2,1,0:T(8,128)(2,1)S(1)}, f32[512,128]{1,0:T(8,128)S(1)}, bf16[512,128]{1,0:T(8,128)(2,1)S(1)}) custom-call(s32[8,128]{1,0:T(8,128)S(1)} %get-tuple-element.16.plan_hbm, bf16[2048,128]{1,0:T(8,128)(2,1)S(1)} %get-tuple-element.17.q_ref, bf16[2048,128]{1,0:T(8,128)(2,1)S(1)} %get-tuple-element.18.g_ref, ...), custom_call_target="tpu_custom_call" | custom-call | flops 1073741824 | bytes 1048576 | tf_op jit(solution)/shard_map/far_part/pallas_call | solution.py:428
  19.2 0.6 %collective-permute-start.2 = (bf16[512,128]{1,0:T(8,128)(2,1)S(1)}, bf16[512,128]{1,0:T(8,128)(2,1)S(1)}, u32[]{:S(2)}, u32[]{:S(2)}) collective-permute-start(bf16[512,128]{1,0:T(8,128)(2,1)S(1)} %get-tuple-element.26), channel_id=1, source_target_pairs={{0,1},{1,0},{2,3},{3,2},{4,5},{5,4},{6,7},{7,6},{8,9},{9,8},{10,11... | collective-permute-start | bytes 393224 | tf_op jit(solution)/shard_map/ppermute | solution.py:42
  19.8 4.5 %own_grads.1 = (bf16[2048,128]{1,0:T(8,128)(2,1)}, f32[512,128]{1,0:T(8,128)S(1)}, bf16[512,128]{1,0:T(8,128)(2,1)S(1)}) custom-call(s32[8,128]{1,0:T(8,128)S(1)} %get-tuple-element.16.plan_hbm, bf16[2048,128]{1,0:T(8,128)(2,1)S(1)} %get-tuple-element.17.q_ref, bf16[2048,128]{1,0:T(8,128)(2,1)S(1)} %get-tuple-element.18.g_ref, ...), custom_call_target="tpu_custom_call" | custom-call | flops 2684354560 | bytes 1048576 | tf_op jit(solution)/shard_map/own_grads/pallas_call | solution.py:454
  24.3 0.1 collective-permute-start.4
  24.4 0.0 collective-permute-done.2
  24.5 0.1 collective-permute-start.3
  24.5 1.2 %collective-permute-done.4 = bf16[512,128]{1,0:T(8,128)(2,1)S(1)} collective-permute-done((bf16[512,128]{1,0:T(8,128)(2,1)S(1)}, bf16[512,128]{1,0:T(8,128)(2,1)S(1)}, u32[]{:S(2)}, u32[]{:S(2)}) %collective-permute-start.4) | collective-permute-done | bytes 131104 | tf_op jit(solution)/shard_map/ppermute | solution.py:42
  25.7 8.4 %collective-permute-done.3 = bf16[512,128]{1,0:T(8,128)(2,1)S(1)} collective-permute-done((bf16[512,128]{1,0:T(8,128)(2,1)S(1)}, bf16[512,128]{1,0:T(8,128)(2,1)S(1)}, u32[]{:S(2)}, u32[]{:S(2)}) %collective-permute-start.3) | collective-permute-done | bytes 131104 | tf_op jit(solution)/shard_map/ppermute | solution.py:37
  34.1 1.6 %collective-permute-start.5 = (bf16[512,128]{1,0:T(8,128)(2,1)S(1)}, bf16[512,128]{1,0:T(8,128)(2,1)S(1)}, u32[]{:S(2)}, u32[]{:S(2)}) collective-permute-start(bf16[512,128]{1,0:T(8,128)(2,1)S(1)} %add_convert_fusion.1), channel_id=1, source_target_pairs={{0,2},{1,3},{2,0},{3,1},{4,6},{5,7},{6,4},{7,5},{8,10},{9,11},{10,... | collective-permute-start | bytes 393224 | tf_op jit(solution)/shard_map/ppermute | solution.py:42
  35.7 3.5 %collective-permute-done.5 = bf16[512,128]{1,0:T(8,128)(2,1)S(1)} collective-permute-done((bf16[512,128]{1,0:T(8,128)(2,1)S(1)}, bf16[512,128]{1,0:T(8,128)(2,1)S(1)}, u32[]{:S(2)}, u32[]{:S(2)}) %collective-permute-start.5) | collective-permute-done | bytes 131104 | tf_op jit(solution)/shard_map/ppermute | solution.py:42
  39.2 0.1 collective-permute-start.6
  39.3 1.3 %collective-permute-done.6 = bf16[512,128]{1,0:T(8,128)(2,1)S(1)} collective-permute-done((bf16[512,128]{1,0:T(8,128)(2,1)S(1)}, bf16[512,128]{1,0:T(8,128)(2,1)S(1)}, u32[]{:S(2)}, u32[]{:S(2)}) %collective-permute-start.6) | collective-permute-done | bytes 131104 | tf_op jit(solution)/shard_map/ppermute | solution.py:42
  40.6 0.7 %select_bitcast_fusion = (bf16[512,1,128]{2,0,1:T(8,128)(2,1)}, bf16[512,1,128]{2,0,1:T(8,128)(2,1)}) fusion(bf16[512,128]{1,0:T(8,128)(2,1)S(1)} %collective-permute-done.6, bf16[512,128]{1,0:T(8,128)(2,1)S(1)} %add_convert_fusion, pred[]{:T(512)S(6)} %eq.5), kind=kLoop, calls=%fused_computation.3 | loop fusion | flops 131072 | bytes 524289 | tf_op jit(solution)/shard_map/broadcast_in_dim | solution.py:501
  (3 shorter events, 0.1 us)
Async XLA Ops:
  1.6 10.4 %collective-permute-start = (bf16[512,128]{1,0:T(8,128)(2,1)S(1)}, bf16[512,128]{1,0:T(8,128)(2,1)S(1)}, u32[]{:S(2)}, u32[]{:S(2)}) collective-permute-start(bf16[512,128]{1,0:T(8,128)(2,1)S(1)} %broadcast_select_fusion), channel_id=1, source_target_pairs={{0,16},{4,20},{8,24},{12,28},{16,0},{20,4},{24,8},{28,12},{1,17},{... | collective-permute-start | bytes 393224 | tf_op jit(solution)/shard_map/ppermute | solution.py:37
  12.1 3.7 %collective-permute-start.1 = (bf16[512,128]{1,0:T(8,128)(2,1)S(1)}, bf16[512,128]{1,0:T(8,128)(2,1)S(1)}, u32[]{:S(2)}, u32[]{:S(2)}) collective-permute-start(bf16[512,128]{1,0:T(8,128)(2,1)S(1)} %collective-permute-done.near_ref), channel_id=1, source_target_pairs={{0,1},{1,0},{2,3},{3,2},{4,5},{5,4},{6,7},{7,6},{8,9},{9,8},{10,11... | collective-permute-start | bytes 393224 | tf_op jit(solution)/shard_map/ppermute | solution.py:42
  19.2 5.2 %collective-permute-start.2 = (bf16[512,128]{1,0:T(8,128)(2,1)S(1)}, bf16[512,128]{1,0:T(8,128)(2,1)S(1)}, u32[]{:S(2)}, u32[]{:S(2)}) collective-permute-start(bf16[512,128]{1,0:T(8,128)(2,1)S(1)} %get-tuple-element.26), channel_id=1, source_target_pairs={{0,1},{1,0},{2,3},{3,2},{4,5},{5,4},{6,7},{7,6},{8,9},{9,8},{10,11... | collective-permute-start | bytes 393224 | tf_op jit(solution)/shard_map/ppermute | solution.py:42
  24.3 1.4 %collective-permute-start.4 = (bf16[512,128]{1,0:T(8,128)(2,1)S(1)}, bf16[512,128]{1,0:T(8,128)(2,1)S(1)}, u32[]{:S(2)}, u32[]{:S(2)}) collective-permute-start(bf16[512,128]{1,0:T(8,128)(2,1)S(1)} %get-tuple-element.28), channel_id=1, source_target_pairs={{0,1},{1,0},{2,3},{3,2},{4,5},{5,4},{6,7},{7,6},{8,9},{9,8},{10,11... | collective-permute-start | bytes 393224 | tf_op jit(solution)/shard_map/ppermute | solution.py:42
  24.5 9.6 %collective-permute-start.3 = (bf16[512,128]{1,0:T(8,128)(2,1)S(1)}, bf16[512,128]{1,0:T(8,128)(2,1)S(1)}, u32[]{:S(2)}, u32[]{:S(2)}) collective-permute-start(bf16[512,128]{1,0:T(8,128)(2,1)S(1)} %add_convert_fusion.2), channel_id=1, source_target_pairs={{0,16},{4,20},{8,24},{12,28},{16,0},{20,4},{24,8},{28,12},{1,17},{... | collective-permute-start | bytes 393224 | tf_op jit(solution)/shard_map/ppermute | solution.py:37
  34.1 5.1 %collective-permute-start.5 = (bf16[512,128]{1,0:T(8,128)(2,1)S(1)}, bf16[512,128]{1,0:T(8,128)(2,1)S(1)}, u32[]{:S(2)}, u32[]{:S(2)}) collective-permute-start(bf16[512,128]{1,0:T(8,128)(2,1)S(1)} %add_convert_fusion.1), channel_id=1, source_target_pairs={{0,2},{1,3},{2,0},{3,1},{4,6},{5,7},{6,4},{7,5},{8,10},{9,11},{10,... | collective-permute-start | bytes 393224 | tf_op jit(solution)/shard_map/ppermute | solution.py:42
  39.2 1.4 %collective-permute-start.6 = (bf16[512,128]{1,0:T(8,128)(2,1)S(1)}, bf16[512,128]{1,0:T(8,128)(2,1)S(1)}, u32[]{:S(2)}, u32[]{:S(2)}) collective-permute-start(bf16[512,128]{1,0:T(8,128)(2,1)S(1)} %add_convert_fusion), channel_id=1, source_target_pairs={{0,1},{1,0},{2,3},{3,2},{4,5},{5,4},{6,7},{7,6},{8,9},{9,8},{10,11... | collective-permute-start | bytes 393224 | tf_op jit(solution)/shard_map/ppermute | solution.py:42

commit v4 on v3

v4 whole, which is shorter than its diff:
```python
import functools

import jax
import jax.numpy as jnp
from jax import lax
from jax.experimental import pallas as pl
from jax.experimental.pallas import tpu as pltpu
from jax.sharding import PartitionSpec as P


GROUP = 16
BLK = 128
SEQS = 4
LOG2E = 1.4426950408889634
MASKED = -1e30
SUB = 8
PIECE = 128
PIECES = 2


def dot_nt(left, right):
    return lax.dot_general(
        left, right, (((1,), (1,)), ((), ())), preferred_element_type=jnp.float32
    )


def dot_nn(left, right):
    return lax.dot_general(
        left, right, (((1,), (0,)), ((), ())), preferred_element_type=jnp.float32
    )


def by_sublane(value):
    return value.reshape(value.shape[0] // SUB, SUB, value.shape[1])


def shifted(value, axis, steps):
    count = lax.axis_size(axis)
    return lax.ppermute(value, axis, [(i, (i + steps) % count) for i in range(count)])


def swapped(value, axis, bit):
    count = lax.axis_size(axis)
    return lax.ppermute(value, axis, [(i, i ^ bit) for i in range(count)])


class Shape:
    def __init__(self, tokens, heads, depth, members):
        self.heads = heads
        self.members = members
        self.blocks = tokens // BLK
        self.far = (members - 1) * self.blocks
        self.rows = BLK * heads
        self.scale = depth**-0.5
        self.keep_tiles = self.blocks * self.far <= 32


FAR_Q, FAR_K, OWN_Q, OWN_K, COUNTS = range(5)
PLAN = (8, 128)


def causal_logits(dims, logits):
    key_token = lax.broadcasted_iota(jnp.int32, logits.shape, 0)
    query_token = lax.broadcasted_iota(jnp.int32, logits.shape, 1) // dims.heads
    return jnp.where(key_token <= query_token, logits, MASKED)


def stats_of(logits, dprob, factor):
    parts = by_sublane(logits)
    top = jnp.max(parts, axis=0)
    exps = jnp.exp2((parts - top[None]) * factor)
    return top * factor, jnp.sum(exps, axis=0), jnp.sum(exps * by_sublane(dprob), axis=0)


def merged(first, second):
    top = jnp.maximum(first[0], second[0])
    one, two = jnp.exp2(first[0] - top), jnp.exp2(second[0] - top)
    return top, first[1] * one + second[1] * two, first[2] * one + second[2] * two


def load_stats(ref, slot):
    return ref[slot, 0], ref[slot, 1], ref[slot, 2]


def store_stats(ref, slot, stats):
    for index in range(3):
        ref[slot, index] = stats[index]


def rows_of(ref, slot, count):
    return ref[pl.ds(pl.multiple_of(slot * count, count), count), :]


def build_plan(dims, pos_ref, mask_ref, plan_ref):
    ctx = lax.axis_index("ctx")
    seq, member = lax.rem(ctx, SEQS), lax.div(ctx, SEQS)
    query_ids = [pos_ref[seq, member * dims.blocks + slot] for slot in range(dims.blocks)]

    def append(rows, total, query_slot, key_slot, seen):
        plan_ref[rows[0], total] = query_slot
        plan_ref[rows[1], total] = key_slot
        return total + jnp.asarray(seen).astype(jnp.int32)

    def sees(query_slot, key_id):
        query_id = query_ids[query_slot]
        return jnp.logical_and(key_id < query_id, mask_ref[seq, query_id, key_id] == 1)

    own = jnp.int32(0)
    for query_slot in range(dims.blocks):
        for key_slot in range(dims.blocks):
            if key_slot != query_slot:
                own = append((OWN_Q, OWN_K), own, query_slot, key_slot, sees(query_slot, query_ids[key_slot]))
    append((OWN_Q, OWN_K), own, dims.blocks, dims.blocks, True)
    plan_ref[COUNTS, 1] = lax.div(own + 1, 2)

    owners = [member - hop for hop in range(1, dims.members)]
    owners = [jnp.where(owner < 0, owner + dims.members, owner) for owner in owners]
    far_ids = [pos_ref[seq, owner * dims.blocks + slot] for owner in owners for slot in range(dims.blocks)]
    far = jnp.int32(0)
    for query_slot in range(dims.blocks):
        for key_slot, key_id in enumerate(far_ids):
            far = append((FAR_Q, FAR_K), far, query_slot, key_slot, sees(query_slot, key_id))
        far = append((FAR_Q, FAR_K), far, dims.blocks, dims.far, lax.rem(far, 2) == 1)
    plan_ref[COUNTS, 0] = lax.div(far, 2)


def two_at_once(count, front, back):
    def trip(step, carry):
        first, second = 2 * step, 2 * step + 1
        one, two = front(first), front(second)
        back(first, one)
        back(second, two)
        return carry

    lax.fori_loop(0, count, trip, 0)


def doubled(count, trips):
    def both(index, carry):
        trips((2 * index, 2 * index + 1))
        return carry

    lax.fori_loop(0, lax.div(count, 2), both, 0)

    @pl.when(lax.rem(count, 2) == 1)
    def _():
        trips((count - 1,))


def own_stats_kernel(
    dims, pos_hbm, mask_hbm, q_hbm, g_hbm, k_hbm, v_hbm,
    stats_ref, plan_ref, q_ref, g_ref, k_ref, v_ref, qt_ref, gt_ref,
    logit_ref, dprob_ref,
    pos_ref, mask_ref, sums, whole_sems, slot_sems,
):
    factor = dims.scale * LOG2E
    whole = [
        pltpu.make_async_copy(source, target, whole_sems.at[index])
        for index, (source, target) in enumerate(
            ((pos_hbm, pos_ref), (mask_hbm, mask_ref), (k_hbm, k_ref), (v_hbm, v_ref))
        )
    ]
    slots = [
        [
            pltpu.make_async_copy(
                source.at[pl.ds(slot * dims.rows, dims.rows)],
                target.at[pl.ds(slot * dims.rows, dims.rows)],
                slot_sems.at[index, slot],
            )
            for index, (source, target) in enumerate(((q_hbm, q_ref), (g_hbm, g_ref)))
        ]
        for slot in range(dims.blocks)
    ]
    for copy in whole:
        copy.start()
    for pair in slots:
        for copy in pair:
            copy.start()
    whole[0].wait()
    whole[1].wait()
    build_plan(dims, pos_ref, mask_ref, plan_ref)
    whole[2].wait()
    whole[3].wait()

    def tile(index, query_slot, key_slot, mask):
        query_slot = jnp.minimum(query_slot, dims.blocks - 1)
        key_slot = jnp.minimum(key_slot, dims.blocks - 1)
        logits = dot_nt(rows_of(k_ref, key_slot, BLK), rows_of(q_ref, query_slot, dims.rows))
        dprob = dot_nt(rows_of(v_ref, key_slot, BLK), rows_of(g_ref, query_slot, dims.rows))
        logits = causal_logits(dims, logits) if mask else logits
        logit_ref[index], dprob_ref[index] = logits, dprob
        return stats_of(logits, dprob, factor)

    for slot in range(dims.blocks):
        slots[slot][0].wait()
        slots[slot][1].wait()
        qt_ref[slot] = rows_of(q_ref, slot, dims.rows).T
        gt_ref[slot] = rows_of(g_ref, slot, dims.rows).T
        store_stats(sums, slot, tile(slot, slot, slot, True))

    def front(pair):
        return tile(dims.blocks + pair, plan_ref[OWN_Q, pair], plan_ref[OWN_K, pair], False)

    def back(pair, stats):
        slot = plan_ref[OWN_Q, pair]
        store_stats(sums, slot, merged(load_stats(sums, slot), stats))

    two_at_once(plan_ref[COUNTS, 1], front, back)
    stats_ref[...] = sums[0:dims.blocks]


def far_kernel(
    dims, plan_hbm, q_ref, g_ref, qt_ref, gt_ref, near_ref, swap_ref, stats_ref,
    final_ref, ds_ref, keep_ref, send_ref,
    plan_ref, plan_sem, k_all, v_all, run, logit_all, dprob_all, dk_all, dv_all,
):
    factor = dims.scale * LOG2E
    first_core = lax.rem(lax.axis_index("head"), 2) == 0
    load_plan = pltpu.make_async_copy(plan_hbm, plan_ref, plan_sem)
    load_plan.start()

    @pl.when(first_core)
    def _():
        k_all[...] = near_ref[...]
        v_all[...] = swap_ref[...]

    @pl.when(jnp.logical_not(first_core))
    def _():
        k_all[...] = swap_ref[...]
        v_all[...] = near_ref[...]

    dk_all[...] = jnp.zeros_like(dk_all)
    dv_all[...] = jnp.zeros_like(dv_all)
    run[0:dims.blocks] = stats_ref[...]
    load_plan.wait()
    count = plan_ref[COUNTS, 0]

    def kept(step):
        return step if dims.keep_tiles else 0

    def query_of(step):
        return jnp.minimum(plan_ref[FAR_Q, 2 * step], dims.blocks - 1)

    def pair_rows(ref, step):
        return jnp.concatenate(
            [
                rows_of(ref, jnp.minimum(plan_ref[FAR_K, 2 * step + index], dims.far - 1), BLK)
                for index in range(2)
            ]
        )

    def products(step):
        slot = query_of(step)
        logit_all[kept(step)] = dot_nn(pair_rows(k_all, step), qt_ref[slot])
        dprob_all[kept(step)] = dot_nn(pair_rows(v_all, step), gt_ref[slot])

    def statistics(step):
        return [
            stats_of(
                logit_all[kept(step), index * BLK:(index + 1) * BLK],
                dprob_all[kept(step), index * BLK:(index + 1) * BLK],
                factor,
            )
            for index in range(2)
        ]

    def merge(step, halves):
        for index in range(2):
            slot = plan_ref[FAR_Q, 2 * step + index]
            store_stats(run, slot, merged(load_stats(run, slot), halves[index]))

    def stats_trips(steps):
        halves = []
        for step in steps:
            products(step)
            halves.append(statistics(step))
        for step, half in zip(steps, halves):
            merge(step, half)

    doubled(count, stats_trips)

    for slot in range(dims.blocks):
        tops, totals, weighted = load_stats(run, slot)
        top = jnp.max(tops, axis=0, keepdims=True)
        factors = jnp.exp2(tops - top)
        total = jnp.sum(totals * factors, axis=0, keepdims=True)
        log_sum = top + jnp.log2(total)
        delta = jnp.sum(weighted * factors, axis=0, keepdims=True) / total
        final_ref[slot, 0] = jnp.broadcast_to(log_sum, tops.shape)
        final_ref[slot, 1] = jnp.broadcast_to(delta, tops.shape)

    def gradients(step):
        slot = query_of(step)
        if not dims.keep_tiles:
            products(step)
        dk_part, dv_part = 0.0, 0.0
        for piece in range(dims.rows // PIECE):
            part = slice(piece * PIECE, (piece + 1) * PIECE)
            probs, dscore = gradient_tiles(
                logit_all[kept(step), :, part], dprob_all[kept(step), :, part], final_ref, slot, part, factor
            )
            ds_ref[step, :, part] = dscore
            dk_part += dot_nn(dscore, piece_of(dims, q_ref, slot, piece))
            dv_part += dot_nn(probs, piece_of(dims, g_ref, slot, piece))
        return dk_part, dv_part

    def grads_trips(steps):
        sums = [gradients(step) for step in steps]
        for step, (dk_part, dv_part) in zip(steps, sums):
            for index in range(2):
                key_slot = plan_ref[FAR_K, 2 * step + index]
                dk_all[key_slot] += dk_part[index * BLK:(index + 1) * BLK]
                dv_all[key_slot] += dv_part[index * BLK:(index + 1) * BLK]

    doubled(count, grads_trips)
    share_out(dims, dims.far, first_core, dk_all, dv_all, keep_ref, send_ref)


def piece_of(dims, ref, slot, piece):
    return ref[pl.ds(pl.multiple_of(slot * dims.rows + piece * PIECE, PIECE), PIECE), :]


def gradient_tiles(logits, dprob, final_ref, slot, part, factor):
    probs = jnp.exp2(by_sublane(logits) * factor - final_ref[slot, 0, :, part][None])
    dscore = probs * (by_sublane(dprob) - final_ref[slot, 1, :, part][None])
    return (
        probs.reshape(logits.shape).astype(jnp.bfloat16),
        dscore.reshape(logits.shape).astype(jnp.bfloat16),
    )


def share_out(dims, count, first_core, dk_all, dv_all, keep_ref, send_ref):
    shape = keep_ref.shape

    @pl.when(first_core)
    def _():
        keep_ref[...] = (dk_all[0:count] * dims.scale).reshape(shape)
        send_ref[...] = dv_all[0:count].reshape(shape).astype(send_ref.dtype)

    @pl.when(jnp.logical_not(first_core))
    def _():
        keep_ref[...] = dv_all[0:count].reshape(shape)
        send_ref[...] = (dk_all[0:count] * dims.scale).reshape(shape).astype(send_ref.dtype)


def own_sums_kernel(
    dims, plan_hbm, q_ref, g_ref, final_ref, logit_ref, dprob_ref,
    keep_ref, send_ref, ds_ref,
    plan_ref, plan_sem, dk_all, dv_all,
):
    factor = dims.scale * LOG2E
    first_core = lax.rem(lax.axis_index("head"), 2) == 0
    load_plan = pltpu.make_async_copy(plan_hbm, plan_ref, plan_sem)
    load_plan.start()

    def front(index, query_slot):
        probs, dscore = gradient_tiles(
            logit_ref[index], dprob_ref[index], final_ref, query_slot, slice(None), factor
        )
        ds_ref[index] = dscore
        return (
            dot_nn(dscore, rows_of(q_ref, query_slot, dims.rows)),
            dot_nn(probs, rows_of(g_ref, query_slot, dims.rows)),
        )

    for slot in range(dims.blocks):
        dk_all[slot], dv_all[slot] = front(slot, slot)
    load_plan.wait()

    def own_front(pair):
        return front(dims.blocks + pair, jnp.minimum(plan_ref[OWN_Q, pair], dims.blocks - 1))

    def own_back(pair, sums):
        dk_all[plan_ref[OWN_K, pair]] += sums[0]
        dv_all[plan_ref[OWN_K, pair]] += sums[1]

    two_at_once(plan_ref[COUNTS, 1], own_front, own_back)
    share_out(dims, dims.blocks, first_core, dk_all, dv_all, keep_ref, send_ref)


def queries_kernel(
    dims, plan_hbm, k_ref, near_ref, swap_ref, far_ds_ref, own_ds_ref,
    dq_ref,
    plan_ref, plan_sem, kt_own, kt_far, dq_all,
):
    first_core = lax.rem(lax.axis_index("head"), 2) == 0
    load_plan = pltpu.make_async_copy(plan_hbm, plan_ref, plan_sem)
    load_plan.start()
    for index in range(dims.blocks):
        kt_own[index] = k_ref[index * BLK:(index + 1) * BLK, :].T

    @pl.when(first_core)
    def _():
        for index in range(dims.far):
            kt_far[index] = near_ref[index * BLK:(index + 1) * BLK, :].T

    @pl.when(jnp.logical_not(first_core))
    def _():
        for index in range(dims.far):
            kt_far[index] = swap_ref[index * BLK:(index + 1) * BLK, :].T

    for slot in range(dims.blocks):
        dq_all[slot] = dot_nn(kt_own[slot], own_ds_ref[slot])
    load_plan.wait()

    def own_front(pair):
        key_slot = jnp.minimum(plan_ref[OWN_K, pair], dims.blocks - 1)
        return dot_nn(kt_own[key_slot], own_ds_ref[dims.blocks + pair])

    def own_back(pair, part):
        dq_all[plan_ref[OWN_Q, pair]] += part

    two_at_once(plan_ref[COUNTS, 1], own_front, own_back)

    def far_trip(step, carry):
        slot = jnp.minimum(plan_ref[FAR_Q, 2 * step], dims.blocks - 1)
        parts = [
            dot_nn(
                kt_far[jnp.minimum(plan_ref[FAR_K, 2 * step + index], dims.far - 1)],
                far_ds_ref[step, index * BLK:(index + 1) * BLK],
            )
            for index in range(2)
        ]
        real = plan_ref[FAR_Q, 2 * step + 1] < dims.blocks
        dq_all[slot] += parts[0] + jnp.where(real, parts[1], 0.0)
        return carry

    lax.fori_loop(0, plan_ref[COUNTS, 0], far_trip, 0)

    for slot in range(dims.blocks):
        start = slot * dims.rows
        dq_ref[start:start + dims.rows, :] = (dq_all[slot] * dims.scale).T.astype(dq_ref.dtype)


def pick_kernel(k_hbm, v_hbm, out_ref):
    first_core = lax.rem(lax.axis_index("head"), 2) == 0

    @pl.when(first_core)
    def _():
        pltpu.sync_copy(k_hbm, out_ref)

    @pl.when(jnp.logical_not(first_core))
    def _():
        pltpu.sync_copy(v_hbm, out_ref)


def place_kernel(*refs):
    own_refs, other_refs, (dk_hbm, dv_hbm, sems) = refs[:PIECES], refs[PIECES:2 * PIECES], refs[2 * PIECES:]
    first_core = lax.rem(lax.axis_index("head"), 2) == 0
    starts = [sum(ref.shape[0] for ref in own_refs[:index]) for index in range(PIECES)]

    def put(dk_refs, dv_refs):
        copies = [
            pltpu.make_async_copy(ref, target.at[pl.ds(starts[index], ref.shape[0])], sems.at[which, index])
            for which, (sources, target) in enumerate(((dk_refs, dk_hbm), (dv_refs, dv_hbm)))
            for index, ref in enumerate(sources)
        ]
        for copy in copies:
            copy.start()
        for copy in copies:
            copy.wait()

    @pl.when(first_core)
    def _():
        put(own_refs, other_refs)

    @pl.when(jnp.logical_not(first_core))
    def _():
        put(other_refs, own_refs)


VMEM = pl.BlockSpec(memory_space=pltpu.VMEM)
SMEM = pl.BlockSpec(memory_space=pltpu.SMEM)
HBM = pl.BlockSpec(memory_space=pltpu.HBM)


def per_device(queries, keys, values, d_out, block_pos, block_mask):
    tokens, heads, depth = queries.shape
    kv_count = keys.shape[1]
    members = lax.axis_size("ctx") // SEQS
    sharers = GROUP // heads
    dims = Shape(tokens, heads, depth, members)
    head_index = lax.axis_index("head")
    kv_index = head_index // sharers
    f32, bf16 = jnp.float32, jnp.bfloat16
    sds = jax.ShapeDtypeStruct

    key_own = lax.dynamic_index_in_dim(keys, kv_index, 1, keepdims=False) if kv_count > 1 else keys[:, 0]
    value_own = lax.dynamic_index_in_dim(values, kv_index, 1, keepdims=False) if kv_count > 1 else values[:, 0]
    query_rows = queries.reshape(tokens * heads, depth)
    grad_rows = d_out.reshape(tokens * heads, depth)

    passed = pl.pallas_call(
        pick_kernel,
        out_shape=sds((tokens, depth), bf16),
        in_specs=[HBM] * 2,
        out_specs=VMEM,
        compiler_params=pltpu.CompilerParams(vmem_limit_bytes=1 << 20),
        name="pick",
    )(*(pltpu.with_memory_space_constraint(operand, pltpu.HBM) for operand in (key_own, value_own)))
    near, swap = [], []
    for _ in range(members - 1):
        passed = shifted(passed, "ctx", SEQS)
        near.append(passed)
        swap.append(swapped(passed, "head", 1))
    near = near[0] if members == 2 else jnp.concatenate(near)
    swap = swap[0] if members == 2 else jnp.concatenate(swap)

    params = pltpu.CompilerParams(vmem_limit_bytes=16 << 20)
    blocks, rows = dims.blocks, dims.rows
    tile_flops = 2 * BLK * rows * depth

    def cost(tiles, dots):
        return pl.CostEstimate(
            flops=tiles * dots * tile_flops,
            bytes_accessed=4 * tokens * heads * depth,
            transcendentals=tiles * BLK * rows,
        )

    own_pairs = blocks + blocks * (blocks - 1) // 2 + 1
    (
        stats, plan, query_rows, grad_rows, key_own, value_own, query_cols, grad_cols, own_logits, own_dprobs,
    ) = pl.pallas_call(
        functools.partial(own_stats_kernel, dims),
        out_shape=(
            sds((blocks, 3, SUB, rows), f32),
            sds(PLAN, jnp.int32),
            sds((tokens * heads, depth), bf16),
            sds((tokens * heads, depth), bf16),
            sds((tokens, depth), bf16),
            sds((tokens, depth), bf16),
            sds((blocks, depth, rows), bf16),
            sds((blocks, depth, rows), bf16),
            sds((own_pairs, BLK, rows), f32),
            sds((own_pairs, BLK, rows), f32),
        ),
        in_specs=[HBM] * 6,
        out_specs=(VMEM, SMEM) + (VMEM,) * 8,
        scratch_shapes=[
            pltpu.SMEM(block_pos.shape, jnp.int32),
            pltpu.SMEM(block_mask.shape, jnp.int32),
            pltpu.VMEM((blocks + 1, 3, SUB, rows), f32),
            pltpu.SemaphoreType.DMA((4,)),
            pltpu.SemaphoreType.DMA((2, blocks)),
        ],
        compiler_params=params,
        cost_estimate=cost(blocks * blocks, 2),
        name="own_stats",
    )(
        *(
            pltpu.with_memory_space_constraint(operand, pltpu.HBM)
            for operand in (block_pos, block_mask, query_rows, grad_rows, key_own, value_own)
        )
    )

    far = dims.far
    trips = blocks * pl.cdiv(far, 2)
    kept = trips if dims.keep_tiles else 1
    final, far_scores, keep_far, send_far = pl.pallas_call(
        functools.partial(far_kernel, dims),
        out_shape=(
            sds((blocks, 2, SUB, rows), f32),
            sds((trips, 2 * BLK, rows), bf16),
            sds((far * BLK, depth), f32),
            sds((far * BLK, depth), bf16),
        ),
        in_specs=[VMEM] * 8,
        out_specs=(VMEM,) * 4,
        scratch_shapes=[
            pltpu.SMEM(PLAN, jnp.int32),
            pltpu.SemaphoreType.DMA,
            pltpu.VMEM((far * BLK, depth), bf16),
            pltpu.VMEM((far * BLK, depth), bf16),
            pltpu.VMEM((blocks + 1, 3, SUB, rows), f32),
            pltpu.VMEM((kept, 2 * BLK, rows), f32),
            pltpu.VMEM((kept, 2 * BLK, rows), f32),
            pltpu.VMEM((far + 1, BLK, depth), f32),
            pltpu.VMEM((far + 1, BLK, depth), f32),
        ],
        compiler_params=params,
        cost_estimate=cost(blocks * far, 4),
        name="far_part",
    )(plan, query_rows, grad_rows, query_cols, grad_cols, near, swap, stats)

    keep_own, send_own, own_scores = pl.pallas_call(
        functools.partial(own_sums_kernel, dims),
        out_shape=(
            sds((tokens, depth), f32),
            sds((tokens, depth), bf16),
            sds((own_pairs, BLK, rows), bf16),
        ),
        in_specs=[VMEM] * 6,
        out_specs=(VMEM,) * 3,
        scratch_shapes=[
            pltpu.SMEM(PLAN, jnp.int32),
            pltpu.SemaphoreType.DMA,
            pltpu.VMEM((blocks + 1, BLK, depth), f32),
            pltpu.VMEM((blocks + 1, BLK, depth), f32),
        ],
        compiler_params=params,
        cost_estimate=cost(blocks * blocks, 2),
        name="own_sums",
    )(plan, query_rows, grad_rows, final, own_logits, own_dprobs)

    dq = pl.pallas_call(
        functools.partial(queries_kernel, dims),
        out_shape=sds((tokens * heads, depth), bf16),
        in_specs=[VMEM] * 6,
        out_specs=VMEM,
        scratch_shapes=[
            pltpu.SMEM(PLAN, jnp.int32),
            pltpu.SemaphoreType.DMA,
            pltpu.VMEM((blocks, depth, BLK), bf16),
            pltpu.VMEM((far, depth, BLK), bf16),
            pltpu.VMEM((blocks + 1, depth, rows), f32),
        ],
        compiler_params=params,
        cost_estimate=cost(blocks * (blocks + far), 1),
        name="queries",
    )(plan, key_own, near, swap, far_scores, own_scores)

    cuts = (0, tokens // 2 + 16, tokens)
    travel = bf16 if members == 2 else f32
    pair_far = keep_far + swapped(send_far, "head", 1).astype(f32)

    def far_piece(hop, index):
        return pair_far[(hop - 1) * tokens + cuts[index]:(hop - 1) * tokens + cuts[index + 1]]

    totals = [far_piece(1, index) for index in range(PIECES)]
    for hop in range(1, members):
        for index in range(PIECES):
            totals[index] = shifted(totals[index].astype(travel), "ctx", SEQS)
            if hop < members - 1:
                totals[index] = totals[index].astype(f32) + far_piece(hop + 1, index)
    swapped_own = swapped(send_own, "head", 1)
    pair_own = keep_own + swapped_own.astype(f32)
    others = []
    for index in range(PIECES):
        total = (totals[index].astype(f32) + pair_own[cuts[index]:cuts[index + 1]]).astype(bf16)
        bit = 2
        while bit < sharers:
            moved = swapped(total, "head", bit)
            total = (total.astype(f32) + moved.astype(f32)).astype(bf16)
            bit *= 2
        totals[index] = total
        others.append(swapped(total, "head", 1))
    d_keys, d_values = pl.pallas_call(
        place_kernel,
        out_shape=(sds((tokens, depth), bf16),) * 2,
        in_specs=[VMEM] * (2 * PIECES),
        out_specs=(HBM,) * 2,
        scratch_shapes=[pltpu.SemaphoreType.DMA((2, PIECES))],
        compiler_params=pltpu.CompilerParams(vmem_limit_bytes=1 << 20),
        name="place",
    )(*totals, *others)
    if kv_count > 1:
        groups = [[p + sharers * g for g in range(kv_count)] for p in range(sharers)]
        both = lax.all_gather(
            jnp.stack([d_keys, d_values]), "head", axis=2, axis_index_groups=groups
        )
        d_keys, d_values = both[0], both[1]
    else:
        d_keys, d_values = d_keys[:, None], d_values[:, None]
    return dq.reshape(tokens, heads, depth), d_keys, d_values


def solution(mesh):
    placed = (
        P("ctx", "head", None),
        P("ctx", None, None),
        P("ctx", None, None),
        P("ctx", "head", None),
        P(),
        P(),
    )
    return jax.shard_map(
        per_device,
        mesh=mesh,
        in_specs=placed,
        out_specs=(P("ctx", "head", None), P("ctx", None, None), P("ctx", None, None)),
        check_vma=False,
    )
```

time: 41.5 us -> 40 us (0.964)
  waiting for transfers between devices: 20.6 us -> 16.6 us
  starting transfers between devices: 6.57 us -> 10 us
  other arithmetic: 1.82 us -> 0.14 us
  Pallas kernels: 11.6 us -> 12.3 us
    ppermute x2 -> x3, starting transfers between devices: 4.2 us -> 7.05 us  [shifted(): lax.ppermute(value, axis, [(i, (i + steps) % count) for i in range(count)])]
    ppermute x5 -> x7, waiting for transfers between devices: 5.97 us -> 3.66 us  [swapped(): return lax.ppermute(value, axis, [(i, i ^ bit) for i in range(count)])]
    ppermute x2 -> x3, waiting for transfers between devices: 14.7 us -> 13 us  [shifted(): lax.ppermute(value, axis, [(i, (i + steps) % count) for i in range(count)])]
    pallas_call x1 -> x4, Pallas kernels: 4.47 us -> 5.88 us  [the longest x1 2.94 us: per_device(): pl.pallas_call(functools.partial(queries_kernel, dims), out_shape=sds((to...]
    select_n x1 -> x0, other arithmetic: 0.99 us -> none  [per_device(): passed = jnp.where(first_core, key_own, value_own)]
    pallas_call x1, Pallas kernels: 3.41 us -> 2.64 us  [per_device(): pl.pallas_call(functools.partial(far_kernel, dims), out_shape=(sds((block...]
    broadcast_in_dim x1 -> x0, other arithmetic: 0.72 us -> none  [per_device(): d_keys, d_values = (d_keys[:, None], d_values[:, None])]
    ppermute x5 -> x7, starting transfers between devices: 2.37 us -> 2.95 us  [swapped(): return lax.ppermute(value, axis, [(i, i ^ bit) for i in range(count)])]
  transfers between devices with their start and end apart: 7 -> 10, of which waited for: 5 -> 4; matrix products, arithmetic and copies ran while one was open for 0% -> 0% of each run, Pallas kernels for 20% -> 20%
where the time goes in v4:
time: 40 us; the launch traced here: 39.8 us
  waiting for transfers between devices  16.6 us (42%)
  Pallas kernels  12.3 us (31%)
  starting transfers between devices  10 us (25%)
  between operations  0.75 us (2%)
    ppermute x3, waiting for transfers between devices, shifted(): lax.ppermute(value, axis, [(i, (i + steps) % count) for i in range(count)])  13 us
    ppermute x3, starting transfers between devices, shifted(): lax.ppermute(value, axis, [(i, (i + steps) % count) for i in range(count)])  7.05 us
    pallas_call x1, Pallas kernels, per_device(): pl.pallas_call(functools.partial(own_stats_kernel, dims), out_shape=(sds(...  3.78 us
    ppermute x7, waiting for transfers between devices, swapped(): return lax.ppermute(value, axis, [(i, i ^ bit) for i in range(count)])  3.66 us
    ppermute x7, starting transfers between devices, swapped(): return lax.ppermute(value, axis, [(i, i ^ bit) for i in range(count)])  2.95 us
    pallas_call x1, Pallas kernels, per_device(): pl.pallas_call(functools.partial(queries_kernel, dims), out_shape=sds((to...  2.94 us
    pallas_call x1, Pallas kernels, per_device(): pl.pallas_call(functools.partial(far_kernel, dims), out_shape=(sds((block...  2.64 us
    pallas_call x1, Pallas kernels, per_device(): pl.pallas_call(functools.partial(own_sums_kernel, dims), out_shape=(sds((...  1.29 us
  transfers between devices with their start and end apart: 10, of which 4 were waited for; matrix products, arithmetic and copies ran while one was open for 0% of the time, Pallas kernels for 20%

profile of v4, /device:TPU:0, one launch (start us, length us, event | category | flops | bytes accessed | tf_op | source)
XLA Modules:
  0.0 39.8 jit_solution(13112114590954468457)
XLA Ops:
  0.6 0.9 %pick.1 = bf16[512,128]{1,0:T(8,128)(2,1)S(1)} custom-call(bf16[512,128]{1,0:T(8,128)(2,1)} %bitcast.8, bf16[512,128]{1,0:T(8,128)(2,1)} %bitcast.10), custom_call_target="tpu_custom_call" | custom-call | tf_op jit(solution)/shard_map/pick/pallas_call | solution.py:493
  1.5 4.1 %collective-permute-start = (bf16[512,128]{1,0:T(8,128)(2,1)S(1)}, bf16[512,128]{1,0:T(8,128)(2,1)S(1)}, u32[]{:S(2)}, u32[]{:S(2)}) collective-permute-start(bf16[512,128]{1,0:T(8,128)(2,1)S(1)} %pick.1), channel_id=1, source_target_pairs={{0,16},{4,20},{8,24},{12,28},{16,0},{20,4},{24,8},{28,12},{1,17},{... | collective-permute-start | bytes 393224 | tf_op jit(solution)/shard_map/ppermute | solution.py:39
  5.6 6.3 %collective-permute-done.near_ref = bf16[512,128]{1,0:T(8,128)(2,1)S(1)} collective-permute-done((bf16[512,128]{1,0:T(8,128)(2,1)S(1)}, bf16[512,128]{1,0:T(8,128)(2,1)S(1)}, u32[]{:S(2)}, u32[]{:S(2)}) %collective-permute-start) | collective-permute-done | bytes 131104 | tf_op jit(solution)/shard_map/ppermute | solution.py:39
  11.9 0.0 collective-permute-start.1
  11.9 3.8 %own_stats.1 = (f32[4,3,8,512]{3,2,1,0:T(8,128)S(1)}, s32[8,128]{1,0:T(8,128)S(1)}, bf16[2048,128]{1,0:T(8,128)(2,1)S(1)}, bf16[2048,128]{1,0:T(8,128)(2,1)S(1)}...) custom-call(s32[4,8]{1,0:T(4,128)} %pos_hbm.1, ...), custom_call_target="tpu_custom_call" | custom-call | flops 536870912 | bytes 1048576 | tf_op jit(solution)/shard_map/own_stats/pallas_call | solution.py:523
  15.7 0.0 collective-permute-done.1.swap_ref
  15.7 2.6 %far_part.1 = (f32[4,2,8,512]{3,2,1,0:T(8,128)S(1)}, bf16[8,256,512]{2,1,0:T(8,128)(2,1)S(1)}, f32[512,128]{1,0:T(8,128)S(1)}, bf16[512,128]{1,0:T(8,128)(2,1)S(1)}) custom-call(s32[8,128]{1,0:T(8,128)S(1)} %get-tuple-element.21.plan_hbm, bf16[2048,128]{1,0:T(8,128)(2,1)S(1)} %get-tuple-element.23.q_ref, bf16[2048,128]{1,0:T(8,128)(2,1)S(1)} %get-tuple-element.24.g_ref, ...), custom_call_target="tpu_custom_call" | custom-call | flops 1073741824 | bytes 1048576 | tf_op jit(solution)/shard_map/far_part/pallas_call | solution.py:559
  18.4 0.6 %collective-permute-start.2 = (bf16[512,128]{1,0:T(8,128)(2,1)S(1)}, bf16[512,128]{1,0:T(8,128)(2,1)S(1)}, u32[]{:S(2)}, u32[]{:S(2)}) collective-permute-start(bf16[512,128]{1,0:T(8,128)(2,1)S(1)} %get-tuple-element.34), channel_id=1, source_target_pairs={{0,1},{1,0},{2,3},{3,2},{4,5},{5,4},{6,7},{7,6},{8,9},{9,8},{10,11... | collective-permute-start | bytes 393224 | tf_op jit(solution)/shard_map/ppermute | solution.py:44
  18.9 1.3 %own_sums.1 = (f32[512,128]{1,0:T(8,128)S(1)}, bf16[512,128]{1,0:T(8,128)(2,1)S(1)}, bf16[11,128,512]{2,1,0:T(8,128)(2,1)S(1)}) custom-call(s32[8,128]{1,0:T(8,128)S(1)} %get-tuple-element.21.plan_hbm, bf16[2048,128]{1,0:T(8,128)(2,1)S(1)} %get-tuple-element.23.q_ref, bf16[2048,128]{1,0:T(8,128)(2,1)S(1)} %get-tuple-element.24.g_ref, ...), custom_call_target="tpu_custom_call" | custom-call | flops 536870912 | bytes 1048576 | tf_op jit(solution)/shard_map/own_sums/pallas_call | solution.py:585
  20.2 0.1 collective-permute-start.4
  20.3 0.0 collective-permute-done.2
  20.4 0.1 collective-permute-start.6
  20.5 2.9 %collective-permute-start.3 = (bf16[272,128]{1,0:T(8,128)(2,1)S(1)}, bf16[272,128]{1,0:T(8,128)(2,1)S(1)}, u32[]{:S(2)}, u32[]{:S(2)}) collective-permute-start(bf16[272,128]{1,0:T(8,128)(2,1)S(1)} %slice.18), channel_id=1, source_target_pairs={{0,16},{4,20},{8,24},{12,28},{16,0},{20,4},{24,8},{28,12},{1,17},{... | collective-permute-start | bytes 208904 | tf_op jit(solution)/shard_map/ppermute | solution.py:39
  23.4 0.0 collective-permute-done.4
  23.4 6.6 %collective-permute-done.3 = bf16[272,128]{1,0:T(8,128)(2,1)S(1)} collective-permute-done((bf16[272,128]{1,0:T(8,128)(2,1)S(1)}, bf16[272,128]{1,0:T(8,128)(2,1)S(1)}, u32[]{:S(2)}, u32[]{:S(2)}) %collective-permute-start.3) | collective-permute-done | bytes 69664 | tf_op jit(solution)/shard_map/ppermute | solution.py:39
  30.1 1.6 %collective-permute-start.5 = (bf16[272,128]{1,0:T(8,128)(2,1)S(1)}, bf16[272,128]{1,0:T(8,128)(2,1)S(1)}, u32[]{:S(2)}, u32[]{:S(2)}) collective-permute-start(bf16[272,128]{1,0:T(8,128)(2,1)S(1)} %fusion), channel_id=1, source_target_pairs={{0,2},{1,3},{2,0},{3,1},{4,6},{5,7},{6,4},{7,5},{8,10},{9,11},{10,... | collective-permute-start | bytes 208904 | tf_op jit(solution)/shard_map/ppermute | solution.py:44
  31.7 0.0 collective-permute-done.6
  31.7 0.5 %collective-permute-start.7 = (bf16[240,128]{1,0:T(8,128)(2,1)S(1)}, bf16[240,128]{1,0:T(8,128)(2,1)S(1)}, u32[]{:S(2)}, u32[]{:S(2)}) collective-permute-start(bf16[240,128]{1,0:T(8,128)(2,1)S(1)} %fusion.1), channel_id=1, source_target_pairs={{0,2},{1,3},{2,0},{3,1},{4,6},{5,7},{6,4},{7,5},{8,10},{9,11},{10,... | collective-permute-start | bytes 184328 | tf_op jit(solution)/shard_map/ppermute | solution.py:44
  32.3 2.2 %collective-permute-done.5 = bf16[272,128]{1,0:T(8,128)(2,1)S(1)} collective-permute-done((bf16[272,128]{1,0:T(8,128)(2,1)S(1)}, bf16[272,128]{1,0:T(8,128)(2,1)S(1)}, u32[]{:S(2)}, u32[]{:S(2)}) %collective-permute-start.5) | collective-permute-done | bytes 69664 | tf_op jit(solution)/shard_map/ppermute | solution.py:44
  34.5 0.1 collective-permute-start.8
  34.6 1.5 %collective-permute-done.7 = bf16[240,128]{1,0:T(8,128)(2,1)S(1)} collective-permute-done((bf16[240,128]{1,0:T(8,128)(2,1)S(1)}, bf16[240,128]{1,0:T(8,128)(2,1)S(1)}, u32[]{:S(2)}, u32[]{:S(2)}) %collective-permute-start.7) | collective-permute-done | bytes 61472 | tf_op jit(solution)/shard_map/ppermute | solution.py:44
  36.0 0.1 collective-permute-start.9
  36.1 2.9 %queries.1 = bf16[2048,128]{1,0:T(8,128)(2,1)} custom-call(s32[8,128]{1,0:T(8,128)S(1)} %get-tuple-element.21.plan_hbm, bf16[512,128]{1,0:T(8,128)(2,1)S(1)} %get-tuple-element.22.k_ref, bf16[512,128]{1,0:T(8,128)(2,1)S(1)} %collective-permute-done.near_ref, bf16[512,128]{1,0:T(8,128)(2,1)S(1)} %collective-permute-done.1.swap_ref, ...), custom_call_target="tpu_custom_call" | custom-call | flops 536870912 | bytes 1048576 | tf_op jit(solution)/shard_map/queries/pallas_call | solution.py:605
  39.1 0.0 collective-permute-done.9.refs_3_
  39.1 0.0 collective-permute-done.8.refs_2_
  39.1 0.7 %place.1 = (bf16[512,128]{1,0:T(8,128)(2,1)}, bf16[512,128]{1,0:T(8,128)(2,1)}) custom-call(bf16[272,128]{1,0:T(8,128)(2,1)S(1)} %add_convert_fusion.1.refs_0_, bf16[240,128]{1,0:T(8,128)(2,1)S(1)} %add_convert_fusion.2.refs_1_, bf16[272,128]{1,0:T(8,128)(2,1)S(1)} %collective-permute-done.8.refs_2_, bf16[240,128]{1,0:T(8,128)(2,1)S(1)} %collective-permute-done.9.refs_3_), custom_call_target="tpu_custom_call" | custom-call | tf_op jit(solution)/shard_map/place/pallas_call | solution.py:647
  (8 shorter events, 0.2 us)
Async XLA Ops:
  1.5 10.4 %collective-permute-start = (bf16[512,128]{1,0:T(8,128)(2,1)S(1)}, bf16[512,128]{1,0:T(8,128)(2,1)S(1)}, u32[]{:S(2)}, u32[]{:S(2)}) collective-permute-start(bf16[512,128]{1,0:T(8,128)(2,1)S(1)} %pick.1), channel_id=1, source_target_pairs={{0,16},{4,20},{8,24},{12,28},{16,0},{20,4},{24,8},{28,12},{1,17},{... | collective-permute-start | bytes 393224 | tf_op jit(solution)/shard_map/ppermute | solution.py:39
  11.9 3.8 %collective-permute-start.1 = (bf16[512,128]{1,0:T(8,128)(2,1)S(1)}, bf16[512,128]{1,0:T(8,128)(2,1)S(1)}, u32[]{:S(2)}, u32[]{:S(2)}) collective-permute-start(bf16[512,128]{1,0:T(8,128)(2,1)S(1)} %collective-permute-done.near_ref), channel_id=1, source_target_pairs={{0,1},{1,0},{2,3},{3,2},{4,5},{5,4},{6,7},{7,6},{8,9},{9,8},{10,11... | collective-permute-start | bytes 393224 | tf_op jit(solution)/shard_map/ppermute | solution.py:44
  18.4 2.0 %collective-permute-start.2 = (bf16[512,128]{1,0:T(8,128)(2,1)S(1)}, bf16[512,128]{1,0:T(8,128)(2,1)S(1)}, u32[]{:S(2)}, u32[]{:S(2)}) collective-permute-start(bf16[512,128]{1,0:T(8,128)(2,1)S(1)} %get-tuple-element.34), channel_id=1, source_target_pairs={{0,1},{1,0},{2,3},{3,2},{4,5},{5,4},{6,7},{7,6},{8,9},{9,8},{10,11... | collective-permute-start | bytes 393224 | tf_op jit(solution)/shard_map/ppermute | solution.py:44
  20.2 3.2 %collective-permute-start.4 = (bf16[512,128]{1,0:T(8,128)(2,1)S(1)}, bf16[512,128]{1,0:T(8,128)(2,1)S(1)}, u32[]{:S(2)}, u32[]{:S(2)}) collective-permute-start(bf16[512,128]{1,0:T(8,128)(2,1)S(1)} %get-tuple-element.36), channel_id=1, source_target_pairs={{0,1},{1,0},{2,3},{3,2},{4,5},{5,4},{6,7},{7,6},{8,9},{9,8},{10,11... | collective-permute-start | bytes 393224 | tf_op jit(solution)/shard_map/ppermute | solution.py:44
  20.4 11.3 %collective-permute-start.6 = (bf16[240,128]{1,0:T(8,128)(2,1)S(1)}, bf16[240,128]{1,0:T(8,128)(2,1)S(1)}, u32[]{:S(2)}, u32[]{:S(2)}) collective-permute-start(bf16[240,128]{1,0:T(8,128)(2,1)S(1)} %slice.20), channel_id=1, source_target_pairs={{0,16},{4,20},{8,24},{12,28},{16,0},{20,4},{24,8},{28,12},{1,17},{... | collective-permute-start | bytes 184328 | tf_op jit(solution)/shard_map/ppermute | solution.py:39
  20.5 9.6 %collective-permute-start.3 = (bf16[272,128]{1,0:T(8,128)(2,1)S(1)}, bf16[272,128]{1,0:T(8,128)(2,1)S(1)}, u32[]{:S(2)}, u32[]{:S(2)}) collective-permute-start(bf16[272,128]{1,0:T(8,128)(2,1)S(1)} %slice.18), channel_id=1, source_target_pairs={{0,16},{4,20},{8,24},{12,28},{16,0},{20,4},{24,8},{28,12},{1,17},{... | collective-permute-start | bytes 208904 | tf_op jit(solution)/shard_map/ppermute | solution.py:39
  30.1 4.4 %collective-permute-start.5 = (bf16[272,128]{1,0:T(8,128)(2,1)S(1)}, bf16[272,128]{1,0:T(8,128)(2,1)S(1)}, u32[]{:S(2)}, u32[]{:S(2)}) collective-permute-start(bf16[272,128]{1,0:T(8,128)(2,1)S(1)} %fusion), channel_id=1, source_target_pairs={{0,2},{1,3},{2,0},{3,1},{4,6},{5,7},{6,4},{7,5},{8,10},{9,11},{10,... | collective-permute-start | bytes 208904 | tf_op jit(solution)/shard_map/ppermute | solution.py:44
  31.7 4.3 %collective-permute-start.7 = (bf16[240,128]{1,0:T(8,128)(2,1)S(1)}, bf16[240,128]{1,0:T(8,128)(2,1)S(1)}, u32[]{:S(2)}, u32[]{:S(2)}) collective-permute-start(bf16[240,128]{1,0:T(8,128)(2,1)S(1)} %fusion.1), channel_id=1, source_target_pairs={{0,2},{1,3},{2,0},{3,1},{4,6},{5,7},{6,4},{7,5},{8,10},{9,11},{10,... | collective-permute-start | bytes 184328 | tf_op jit(solution)/shard_map/ppermute | solution.py:44
  34.5 4.6 %collective-permute-start.8 = (bf16[272,128]{1,0:T(8,128)(2,1)S(1)}, bf16[272,128]{1,0:T(8,128)(2,1)S(1)}, u32[]{:S(2)}, u32[]{:S(2)}) collective-permute-start(bf16[272,128]{1,0:T(8,128)(2,1)S(1)} %add_convert_fusion.1.refs_0_), channel_id=1, source_target_pairs={{0,1},{1,0},{2,3},{3,2},{4,5},{5,4},{6,7},{7,6},{8,9},{9,8},{10,11... | collective-permute-start | bytes 208904 | tf_op jit(solution)/shard_map/ppermute | solution.py:44
  36.0 3.0 %collective-permute-start.9 = (bf16[240,128]{1,0:T(8,128)(2,1)S(1)}, bf16[240,128]{1,0:T(8,128)(2,1)S(1)}, u32[]{:S(2)}, u32[]{:S(2)}) collective-permute-start(bf16[240,128]{1,0:T(8,128)(2,1)S(1)} %add_convert_fusion.2.refs_1_), channel_id=1, source_target_pairs={{0,1},{1,0},{2,3},{3,2},{4,5},{5,4},{6,7},{7,6},{8,9},{9,8},{10,11... | collective-permute-start | bytes 184328 | tf_op jit(solution)/shard_map/ppermute | solution.py:44

commit v5 on v4

--- a/solution.py
+++ b/solution.py
@@ -16,6 +16,7 @@
 SUB = 8
 PIECE = 128
 PIECES = 2
+COPIES = 4
 
 
 def dot_nt(left, right):
@@ -378,10 +379,10 @@
     share_out(dims, dims.blocks, first_core, dk_all, dv_all, keep_ref, send_ref)
 
 
-def queries_kernel(
-    dims, plan_hbm, k_ref, near_ref, swap_ref, far_ds_ref, own_ds_ref,
-    dq_ref,
-    plan_ref, plan_sem, kt_own, kt_far, dq_all,
+def own_queries_kernel(
+    dims, plan_hbm, k_ref, near_ref, swap_ref, own_ds_ref,
+    dq_ref, kt_far,
+    plan_ref, plan_sem, kt_own,
 ):
     first_core = lax.rem(lax.axis_index("head"), 2) == 0
     load_plan = pltpu.make_async_copy(plan_hbm, plan_ref, plan_sem)
@@ -400,7 +401,7 @@
             kt_far[index] = swap_ref[index * BLK:(index + 1) * BLK, :].T
 
     for slot in range(dims.blocks):
-        dq_all[slot] = dot_nn(kt_own[slot], own_ds_ref[slot])
+        dq_ref[slot] = dot_nn(kt_own[slot], own_ds_ref[slot])
     load_plan.wait()
 
     def own_front(pair):
@@ -408,9 +409,20 @@
         return dot_nn(kt_own[key_slot], own_ds_ref[dims.blocks + pair])
 
     def own_back(pair, part):
-        dq_all[plan_ref[OWN_Q, pair]] += part
+        dq_ref[plan_ref[OWN_Q, pair]] += part
 
     two_at_once(plan_ref[COUNTS, 1], own_front, own_back)
+
+
+def queries_kernel(
+    dims, plan_hbm, kt_far, far_ds_ref, dq_own_ref,
+    dq_hbm,
+    plan_ref, plan_sem, dq_all, dq_out, dq_sems,
+):
+    load_plan = pltpu.make_async_copy(plan_hbm, plan_ref, plan_sem)
+    load_plan.start()
+    dq_all[...] = dq_own_ref[0:dims.blocks]
+    load_plan.wait()
 
     def far_trip(step, carry):
         slot = jnp.minimum(plan_ref[FAR_Q, 2 * step], dims.blocks - 1)
@@ -427,21 +439,39 @@
 
     lax.fori_loop(0, plan_ref[COUNTS, 0], far_trip, 0)
 
+    copies = []
     for slot in range(dims.blocks):
-        start = slot * dims.rows
-        dq_ref[start:start + dims.rows, :] = (dq_all[slot] * dims.scale).T.astype(dq_ref.dtype)
-
-
-def pick_kernel(k_hbm, v_hbm, out_ref):
+        part = pl.ds(slot * dims.rows, dims.rows)
+        dq_out[part, :] = (dq_all[slot] * dims.scale).T.astype(dq_out.dtype)
+        copies.append(pltpu.make_async_copy(dq_out.at[part], dq_hbm.at[part], dq_sems.at[slot]))
+        copies[-1].start()
+    for copy in copies:
+        copy.wait()
+
+
+def pick_kernel(k_hbm, v_hbm, out_ref, sems):
     first_core = lax.rem(lax.axis_index("head"), 2) == 0
+    rows = out_ref.shape[0] // COPIES
+
+    def take(source):
+        copies = [
+            pltpu.make_async_copy(
+                source.at[pl.ds(index * rows, rows)], out_ref.at[pl.ds(index * rows, rows)], sems.at[index]
+            )
+            for index in range(COPIES)
+        ]
+        for copy in copies:
+            copy.start()
+        for copy in copies:
+            copy.wait()
 
     @pl.when(first_core)
     def _():
-        pltpu.sync_copy(k_hbm, out_ref)
+        take(k_hbm)
 
     @pl.when(jnp.logical_not(first_core))
     def _():
-        pltpu.sync_copy(v_hbm, out_ref)
+        take(v_hbm)
 
 
 def place_kernel(*refs):
@@ -495,6 +525,7 @@
         out_shape=sds((tokens, depth), bf16),
         in_specs=[HBM] * 2,
         out_specs=VMEM,
+        scratch_shapes=[pltpu.SemaphoreType.DMA((COPIES,))],
         compiler_params=pltpu.CompilerParams(vmem_limit_bytes=1 << 20),
         name="pick",
     )(*(pltpu.with_memory_space_constraint(operand, pltpu.HBM) for operand in (key_own, value_own)))
@@ -602,24 +633,39 @@
         name="own_sums",
     )(plan, query_rows, grad_rows, final, own_logits, own_dprobs)
 
-    dq = pl.pallas_call(
-        functools.partial(queries_kernel, dims),
-        out_shape=sds((tokens * heads, depth), bf16),
-        in_specs=[VMEM] * 6,
-        out_specs=VMEM,
+    dq_own, far_cols = pl.pallas_call(
+        functools.partial(own_queries_kernel, dims),
+        out_shape=(sds((blocks + 1, depth, rows), f32), sds((far, depth, BLK), bf16)),
+        in_specs=[VMEM] * 5,
+        out_specs=(VMEM,) * 2,
         scratch_shapes=[
             pltpu.SMEM(PLAN, jnp.int32),
             pltpu.SemaphoreType.DMA,
             pltpu.VMEM((blocks, depth, BLK), bf16),
-            pltpu.VMEM((far, depth, BLK), bf16),
-            pltpu.VMEM((blocks + 1, depth, rows), f32),
         ],
         compiler_params=params,
-        cost_estimate=cost(blocks * (blocks + far), 1),
+        cost_estimate=cost(blocks * blocks, 1),
+        name="own_queries",
+    )(plan, key_own, near, swap, own_scores)
+
+    dq = pl.pallas_call(
+        functools.partial(queries_kernel, dims),
+        out_shape=sds((tokens * heads, depth), bf16),
+        in_specs=[VMEM] * 4,
+        out_specs=HBM,
+        scratch_shapes=[
+            pltpu.SMEM(PLAN, jnp.int32),
+            pltpu.SemaphoreType.DMA,
+            pltpu.VMEM((blocks, depth, rows), f32),
+            pltpu.VMEM((tokens * heads, depth), bf16),
+            pltpu.SemaphoreType.DMA((blocks,)),
+        ],
+        compiler_params=params,
+        cost_estimate=cost(blocks * far, 1),
         name="queries",
-    )(plan, key_own, near, swap, far_scores, own_scores)
-
-    cuts = (0, tokens // 2 + 16, tokens)
+    )(plan, far_cols, far_scores, dq_own)
+
+    cuts = (0, tokens * 5 // 8, tokens)
     travel = bf16 if members == 2 else f32
     pair_far = keep_far + swapped(send_far, "head", 1).astype(f32)
 

time: 40 us -> 38.7 us (0.968)
  waiting for transfers between devices: 16.6 us -> 14.7 us
    ppermute x3, waiting for transfers between devices: 13 us -> 11.2 us  [shifted(): lax.ppermute(value, axis, [(i, (i + steps) % count) for i in range(count)])]
    pallas_call x0 -> x1, Pallas kernels: none -> 1.05 us  [per_device(): pl.pallas_call(functools.partial(own_queries_kernel, dims), out_shape=(sd...]
    pallas_call x1, Pallas kernels: 2.94 us -> 2.4 us  [per_device(): pl.pallas_call(functools.partial(queries_kernel, dims), out_shape=sds((to...]
  transfers between devices with their start and end apart: 10 -> 10, of which waited for: 4 -> 4; matrix products, arithmetic and copies ran while one was open for 0% -> 0% of each run, Pallas kernels for 20% -> 22%
where the time goes in v5:
time: 38.7 us; the launch traced here: 38.5 us
  waiting for transfers between devices  14.7 us (38%)
  Pallas kernels  12.7 us (33%)
  starting transfers between devices  10.1 us (26%)
  between operations  0.77 us (2%)
    ppermute x3, waiting for transfers between devices, shifted(): lax.ppermute(value, axis, [(i, (i + steps) % count) for i in range(count)])  11.2 us
    ppermute x3, starting transfers between devices, shifted(): lax.ppermute(value, axis, [(i, (i + steps) % count) for i in range(count)])  7.11 us
    pallas_call x1, Pallas kernels, per_device(): pl.pallas_call(functools.partial(own_stats_kernel, dims), out_shape=(sds(...  3.78 us
    ppermute x7, waiting for transfers between devices, swapped(): return lax.ppermute(value, axis, [(i, i ^ bit) for i in range(count)])  3.53 us
    ppermute x7, starting transfers between devices, swapped(): return lax.ppermute(value, axis, [(i, i ^ bit) for i in range(count)])  2.95 us
    pallas_call x1, Pallas kernels, per_device(): pl.pallas_call(functools.partial(far_kernel, dims), out_shape=(sds((block...  2.63 us
    pallas_call x1, Pallas kernels, per_device(): pl.pallas_call(functools.partial(queries_kernel, dims), out_shape=sds((to...  2.4 us
    pallas_call x1, Pallas kernels, per_device(): pl.pallas_call(functools.partial(own_sums_kernel, dims), out_shape=(sds((...  1.29 us
  transfers between devices with their start and end apart: 10, of which 4 were waited for; matrix products, arithmetic and copies ran while one was open for 0% of the time, Pallas kernels for 22%

profile of v5, /device:TPU:0, one launch (start us, length us, event | category | flops | bytes accessed | tf_op | source)
XLA Modules:
  0.0 38.5 jit_solution(10274200270363847295)
XLA Ops:
  0.6 0.9 %pick.1 = bf16[512,128]{1,0:T(8,128)(2,1)S(1)} custom-call(bf16[512,128]{1,0:T(8,128)(2,1)} %bitcast.8, bf16[512,128]{1,0:T(8,128)(2,1)} %bitcast.10), custom_call_target="tpu_custom_call" | custom-call | tf_op jit(solution)/shard_map/pick/pallas_call | solution.py:523
  1.5 4.1 %collective-permute-start = (bf16[512,128]{1,0:T(8,128)(2,1)S(1)}, bf16[512,128]{1,0:T(8,128)(2,1)S(1)}, u32[]{:S(2)}, u32[]{:S(2)}) collective-permute-start(bf16[512,128]{1,0:T(8,128)(2,1)S(1)} %pick.1), channel_id=1, source_target_pairs={{0,16},{4,20},{8,24},{12,28},{16,0},{20,4},{24,8},{28,12},{1,17},{... | collective-permute-start | bytes 393224 | tf_op jit(solution)/shard_map/ppermute | solution.py:40
  5.6 6.3 %collective-permute-done.near_ref = bf16[512,128]{1,0:T(8,128)(2,1)S(1)} collective-permute-done((bf16[512,128]{1,0:T(8,128)(2,1)S(1)}, bf16[512,128]{1,0:T(8,128)(2,1)S(1)}, u32[]{:S(2)}, u32[]{:S(2)}) %collective-permute-start) | collective-permute-done | bytes 131104 | tf_op jit(solution)/shard_map/ppermute | solution.py:40
  11.9 0.0 collective-permute-start.1
  11.9 3.8 %own_stats.1 = (f32[4,3,8,512]{3,2,1,0:T(8,128)S(1)}, s32[8,128]{1,0:T(8,128)S(1)}, bf16[2048,128]{1,0:T(8,128)(2,1)S(1)}, bf16[2048,128]{1,0:T(8,128)(2,1)S(1)}...) custom-call(s32[4,8]{1,0:T(4,128)} %pos_hbm.1, ...), custom_call_target="tpu_custom_call" | custom-call | flops 536870912 | bytes 1048576 | tf_op jit(solution)/shard_map/own_stats/pallas_call | solution.py:554
  15.7 0.0 collective-permute-done.1.swap_ref
  15.7 2.6 %far_part.1 = (f32[4,2,8,512]{3,2,1,0:T(8,128)S(1)}, bf16[8,256,512]{2,1,0:T(8,128)(2,1)S(1)}, f32[512,128]{1,0:T(8,128)S(1)}, bf16[512,128]{1,0:T(8,128)(2,1)S(1)}) custom-call(s32[8,128]{1,0:T(8,128)S(1)} %get-tuple-element.23.plan_hbm, bf16[2048,128]{1,0:T(8,128)(2,1)S(1)} %get-tuple-element.25.q_ref, bf16[2048,128]{1,0:T(8,128)(2,1)S(1)} %get-tuple-element.26.g_ref, ...), custom_call_target="tpu_custom_call" | custom-call | flops 1073741824 | bytes 1048576 | tf_op jit(solution)/shard_map/far_part/pallas_call | solution.py:590
  18.4 0.6 %collective-permute-start.2 = (bf16[512,128]{1,0:T(8,128)(2,1)S(1)}, bf16[512,128]{1,0:T(8,128)(2,1)S(1)}, u32[]{:S(2)}, u32[]{:S(2)}) collective-permute-start(bf16[512,128]{1,0:T(8,128)(2,1)S(1)} %get-tuple-element.38), channel_id=1, source_target_pairs={{0,1},{1,0},{2,3},{3,2},{4,5},{5,4},{6,7},{7,6},{8,9},{9,8},{10,11... | collective-permute-start | bytes 393224 | tf_op jit(solution)/shard_map/ppermute | solution.py:45
  18.9 1.3 %own_sums.1 = (f32[512,128]{1,0:T(8,128)S(1)}, bf16[512,128]{1,0:T(8,128)(2,1)S(1)}, bf16[11,128,512]{2,1,0:T(8,128)(2,1)S(1)}) custom-call(s32[8,128]{1,0:T(8,128)S(1)} %get-tuple-element.23.plan_hbm, bf16[2048,128]{1,0:T(8,128)(2,1)S(1)} %get-tuple-element.25.q_ref, bf16[2048,128]{1,0:T(8,128)(2,1)S(1)} %get-tuple-element.26.g_ref, ...), custom_call_target="tpu_custom_call" | custom-call | flops 536870912 | bytes 1048576 | tf_op jit(solution)/shard_map/own_sums/pallas_call | solution.py:616
  20.2 0.1 collective-permute-start.4
  20.3 0.0 collective-permute-done.2
  20.4 0.1 collective-permute-start.6
  20.5 2.9 %collective-permute-start.3 = (bf16[320,128]{1,0:T(8,128)(2,1)S(1)}, bf16[320,128]{1,0:T(8,128)(2,1)S(1)}, u32[]{:S(2)}, u32[]{:S(2)}) collective-permute-start(bf16[320,128]{1,0:T(8,128)(2,1)S(1)} %slice.18), channel_id=1, source_target_pairs={{0,16},{4,20},{8,24},{12,28},{16,0},{20,4},{24,8},{28,12},{1,17},{... | collective-permute-start | bytes 245768 | tf_op jit(solution)/shard_map/ppermute | solution.py:40
  23.4 0.0 collective-permute-done.4
  23.4 4.9 %collective-permute-done.3 = bf16[320,128]{1,0:T(8,128)(2,1)S(1)} collective-permute-done((bf16[320,128]{1,0:T(8,128)(2,1)S(1)}, bf16[320,128]{1,0:T(8,128)(2,1)S(1)}, u32[]{:S(2)}, u32[]{:S(2)}) %collective-permute-start.3) | collective-permute-done | bytes 81952 | tf_op jit(solution)/shard_map/ppermute | solution.py:40
  28.3 1.6 %collective-permute-start.5 = (bf16[320,128]{1,0:T(8,128)(2,1)S(1)}, bf16[320,128]{1,0:T(8,128)(2,1)S(1)}, u32[]{:S(2)}, u32[]{:S(2)}) collective-permute-start(bf16[320,128]{1,0:T(8,128)(2,1)S(1)} %fusion), channel_id=1, source_target_pairs={{0,2},{1,3},{2,0},{3,1},{4,6},{5,7},{6,4},{7,5},{8,10},{9,11},{10,... | collective-permute-start | bytes 245768 | tf_op jit(solution)/shard_map/ppermute | solution.py:45
  30.0 0.0 collective-permute-done.6
  30.0 0.5 %collective-permute-start.7 = (bf16[192,128]{1,0:T(8,128)(2,1)S(1)}, bf16[192,128]{1,0:T(8,128)(2,1)S(1)}, u32[]{:S(2)}, u32[]{:S(2)}) collective-permute-start(bf16[192,128]{1,0:T(8,128)(2,1)S(1)} %fusion.1), channel_id=1, source_target_pairs={{0,2},{1,3},{2,0},{3,1},{4,6},{5,7},{6,4},{7,5},{8,10},{9,11},{10,... | collective-permute-start | bytes 147464 | tf_op jit(solution)/shard_map/ppermute | solution.py:45
  30.5 2.9 %collective-permute-done.5 = bf16[320,128]{1,0:T(8,128)(2,1)S(1)} collective-permute-done((bf16[320,128]{1,0:T(8,128)(2,1)S(1)}, bf16[320,128]{1,0:T(8,128)(2,1)S(1)}, u32[]{:S(2)}, u32[]{:S(2)}) %collective-permute-start.5) | collective-permute-done | bytes 81952 | tf_op jit(solution)/shard_map/ppermute | solution.py:45
  33.4 0.1 collective-permute-start.8
  33.5 0.7 %collective-permute-done.7 = bf16[192,128]{1,0:T(8,128)(2,1)S(1)} collective-permute-done((bf16[192,128]{1,0:T(8,128)(2,1)S(1)}, bf16[192,128]{1,0:T(8,128)(2,1)S(1)}, u32[]{:S(2)}, u32[]{:S(2)}) %collective-permute-start.7) | collective-permute-done | bytes 49184 | tf_op jit(solution)/shard_map/ppermute | solution.py:45
  34.2 0.1 collective-permute-start.9
  34.2 1.1 %own_queries.1 = (f32[5,128,512]{2,1,0:T(8,128)S(1)}, bf16[4,128,128]{2,1,0:T(8,128)(2,1)S(1)}) custom-call(s32[8,128]{1,0:T(8,128)S(1)} %get-tuple-element.23.plan_hbm, bf16[512,128]{1,0:T(8,128)(2,1)S(1)} %get-tuple-element.24.k_ref, bf16[512,128]{1,0:T(8,128)(2,1)S(1)} %collective-permute-done.near_ref, ...), custom_call_target="tpu_custom_call" | custom-call | flops 268435456 | bytes 1048576 | tf_op jit(solution)/shard_map/own_queries/pallas_call | solution.py:636
  35.3 2.4 %queries.1 = bf16[2048,128]{1,0:T(8,128)(2,1)} custom-call(s32[8,128]{1,0:T(8,128)S(1)} %get-tuple-element.23.plan_hbm, bf16[4,128,128]{2,1,0:T(8,128)(2,1)S(1)} %get-tuple-element.34.kt_far, bf16[8,256,512]{2,1,0:T(8,128)(2,1)S(1)} %get-tuple-element.35.far_ds_ref, f32[5,128,512]{2,1,0:T(8,128)S(1)} %get-tuple-element.36.dq_own_ref), custom_call_target="tpu_custom_call" | custom-call | flops 268435456 | bytes 1048576 | tf_op jit(solution)/shard_map/queries/pallas_call | solution.py:651
  37.7 0.0 collective-permute-done.9.refs_3_
  37.7 0.0 collective-permute-done.8.refs_2_
  37.7 0.7 %place.1 = (bf16[512,128]{1,0:T(8,128)(2,1)}, bf16[512,128]{1,0:T(8,128)(2,1)}) custom-call(bf16[320,128]{1,0:T(8,128)(2,1)S(1)} %add_convert_fusion.1.refs_0_, bf16[192,128]{1,0:T(8,128)(2,1)S(1)} %add_convert_fusion.2.refs_1_, bf16[320,128]{1,0:T(8,128)(2,1)S(1)} %collective-permute-done.8.refs_2_, bf16[192,128]{1,0:T(8,128)(2,1)S(1)} %collective-permute-done.9.refs_3_), custom_call_target="tpu_custom_call" | custom-call | tf_op jit(solution)/shard_map/place/pallas_call | solution.py:693
  (8 shorter events, 0.2 us)
Async XLA Ops:
  1.5 10.4 %collective-permute-start = (bf16[512,128]{1,0:T(8,128)(2,1)S(1)}, bf16[512,128]{1,0:T(8,128)(2,1)S(1)}, u32[]{:S(2)}, u32[]{:S(2)}) collective-permute-start(bf16[512,128]{1,0:T(8,128)(2,1)S(1)} %pick.1), channel_id=1, source_target_pairs={{0,16},{4,20},{8,24},{12,28},{16,0},{20,4},{24,8},{28,12},{1,17},{... | collective-permute-start | bytes 393224 | tf_op jit(solution)/shard_map/ppermute | solution.py:40
  11.9 3.8 %collective-permute-start.1 = (bf16[512,128]{1,0:T(8,128)(2,1)S(1)}, bf16[512,128]{1,0:T(8,128)(2,1)S(1)}, u32[]{:S(2)}, u32[]{:S(2)}) collective-permute-start(bf16[512,128]{1,0:T(8,128)(2,1)S(1)} %collective-permute-done.near_ref), channel_id=1, source_target_pairs={{0,1},{1,0},{2,3},{3,2},{4,5},{5,4},{6,7},{7,6},{8,9},{9,8},{10,11... | collective-permute-start | bytes 393224 | tf_op jit(solution)/shard_map/ppermute | solution.py:45
  18.4 2.0 %collective-permute-start.2 = (bf16[512,128]{1,0:T(8,128)(2,1)S(1)}, bf16[512,128]{1,0:T(8,128)(2,1)S(1)}, u32[]{:S(2)}, u32[]{:S(2)}) collective-permute-start(bf16[512,128]{1,0:T(8,128)(2,1)S(1)} %get-tuple-element.38), channel_id=1, source_target_pairs={{0,1},{1,0},{2,3},{3,2},{4,5},{5,4},{6,7},{7,6},{8,9},{9,8},{10,11... | collective-permute-start | bytes 393224 | tf_op jit(solution)/shard_map/ppermute | solution.py:45
  20.2 3.1 %collective-permute-start.4 = (bf16[512,128]{1,0:T(8,128)(2,1)S(1)}, bf16[512,128]{1,0:T(8,128)(2,1)S(1)}, u32[]{:S(2)}, u32[]{:S(2)}) collective-permute-start(bf16[512,128]{1,0:T(8,128)(2,1)S(1)} %get-tuple-element.40), channel_id=1, source_target_pairs={{0,1},{1,0},{2,3},{3,2},{4,5},{5,4},{6,7},{7,6},{8,9},{9,8},{10,11... | collective-permute-start | bytes 393224 | tf_op jit(solution)/shard_map/ppermute | solution.py:45
  20.4 9.6 %collective-permute-start.6 = (bf16[192,128]{1,0:T(8,128)(2,1)S(1)}, bf16[192,128]{1,0:T(8,128)(2,1)S(1)}, u32[]{:S(2)}, u32[]{:S(2)}) collective-permute-start(bf16[192,128]{1,0:T(8,128)(2,1)S(1)} %slice.20), channel_id=1, source_target_pairs={{0,16},{4,20},{8,24},{12,28},{16,0},{20,4},{24,8},{28,12},{1,17},{... | collective-permute-start | bytes 147464 | tf_op jit(solution)/shard_map/ppermute | solution.py:40
  20.5 7.8 %collective-permute-start.3 = (bf16[320,128]{1,0:T(8,128)(2,1)S(1)}, bf16[320,128]{1,0:T(8,128)(2,1)S(1)}, u32[]{:S(2)}, u32[]{:S(2)}) collective-permute-start(bf16[320,128]{1,0:T(8,128)(2,1)S(1)} %slice.18), channel_id=1, source_target_pairs={{0,16},{4,20},{8,24},{12,28},{16,0},{20,4},{24,8},{28,12},{1,17},{... | collective-permute-start | bytes 245768 | tf_op jit(solution)/shard_map/ppermute | solution.py:40
  28.3 5.0 %collective-permute-start.5 = (bf16[320,128]{1,0:T(8,128)(2,1)S(1)}, bf16[320,128]{1,0:T(8,128)(2,1)S(1)}, u32[]{:S(2)}, u32[]{:S(2)}) collective-permute-start(bf16[320,128]{1,0:T(8,128)(2,1)S(1)} %fusion), channel_id=1, source_target_pairs={{0,2},{1,3},{2,0},{3,1},{4,6},{5,7},{6,4},{7,5},{8,10},{9,11},{10,... | collective-permute-start | bytes 245768 | tf_op jit(solution)/shard_map/ppermute | solution.py:45
  30.0 4.2 %collective-permute-start.7 = (bf16[192,128]{1,0:T(8,128)(2,1)S(1)}, bf16[192,128]{1,0:T(8,128)(2,1)S(1)}, u32[]{:S(2)}, u32[]{:S(2)}) collective-permute-start(bf16[192,128]{1,0:T(8,128)(2,1)S(1)} %fusion.1), channel_id=1, source_target_pairs={{0,2},{1,3},{2,0},{3,1},{4,6},{5,7},{6,4},{7,5},{8,10},{9,11},{10,... | collective-permute-start | bytes 147464 | tf_op jit(solution)/shard_map/ppermute | solution.py:45
  33.4 4.3 %collective-permute-start.8 = (bf16[320,128]{1,0:T(8,128)(2,1)S(1)}, bf16[320,128]{1,0:T(8,128)(2,1)S(1)}, u32[]{:S(2)}, u32[]{:S(2)}) collective-permute-start(bf16[320,128]{1,0:T(8,128)(2,1)S(1)} %add_convert_fusion.1.refs_0_), channel_id=1, source_target_pairs={{0,1},{1,0},{2,3},{3,2},{4,5},{5,4},{6,7},{7,6},{8,9},{9,8},{10,11... | collective-permute-start | bytes 245768 | tf_op jit(solution)/shard_map/ppermute | solution.py:45
  34.2 3.6 %collective-permute-start.9 = (bf16[192,128]{1,0:T(8,128)(2,1)S(1)}, bf16[192,128]{1,0:T(8,128)(2,1)S(1)}, u32[]{:S(2)}, u32[]{:S(2)}) collective-permute-start(bf16[192,128]{1,0:T(8,128)(2,1)S(1)} %add_convert_fusion.2.refs_1_), channel_id=1, source_target_pairs={{0,1},{1,0},{2,3},{3,2},{4,5},{5,4},{6,7},{7,6},{8,9},{9,8},{10,11... | collective-permute-start | bytes 147464 | tf_op jit(solution)/shard_map/ppermute | solution.py:45

commit v6 on v5

--- a/solution.py
+++ b/solution.py
@@ -16,7 +16,7 @@
 SUB = 8
 PIECE = 128
 PIECES = 2
-COPIES = 4
+COPIES = 8
 
 
 def dot_nt(left, right):
@@ -56,7 +56,7 @@
         self.keep_tiles = self.blocks * self.far <= 32
 
 
-FAR_Q, FAR_K, OWN_Q, OWN_K, COUNTS = range(5)
+FAR_Q, FAR_K, OWN_Q, OWN_K = range(4)
 PLAN = (8, 128)
 
 
@@ -92,37 +92,55 @@
     return ref[pl.ds(pl.multiple_of(slot * count, count), count), :]
 
 
-def build_plan(dims, pos_ref, mask_ref, plan_ref):
+def seen_words(dims, pos_ref, mask_ref, bits_ref):
     ctx = lax.axis_index("ctx")
     seq, member = lax.rem(ctx, SEQS), lax.div(ctx, SEQS)
-    query_ids = [pos_ref[seq, member * dims.blocks + slot] for slot in range(dims.blocks)]
-
-    def append(rows, total, query_slot, key_slot, seen):
-        plan_ref[rows[0], total] = query_slot
-        plan_ref[rows[1], total] = key_slot
-        return total + jnp.asarray(seen).astype(jnp.int32)
-
-    def sees(query_slot, key_id):
-        query_id = query_ids[query_slot]
-        return jnp.logical_and(key_id < query_id, mask_ref[seq, query_id, key_id] == 1)
-
-    own = jnp.int32(0)
-    for query_slot in range(dims.blocks):
-        for key_slot in range(dims.blocks):
-            if key_slot != query_slot:
-                own = append((OWN_Q, OWN_K), own, query_slot, key_slot, sees(query_slot, query_ids[key_slot]))
-    append((OWN_Q, OWN_K), own, dims.blocks, dims.blocks, True)
-    plan_ref[COUNTS, 1] = lax.div(own + 1, 2)
-
+    own_ids = [pos_ref[seq, member * dims.blocks + slot] for slot in range(dims.blocks)]
     owners = [member - hop for hop in range(1, dims.members)]
     owners = [jnp.where(owner < 0, owner + dims.members, owner) for owner in owners]
     far_ids = [pos_ref[seq, owner * dims.blocks + slot] for owner in owners for slot in range(dims.blocks)]
-    far = jnp.int32(0)
-    for query_slot in range(dims.blocks):
-        for key_slot, key_id in enumerate(far_ids):
-            far = append((FAR_Q, FAR_K), far, query_slot, key_slot, sees(query_slot, key_id))
-        far = append((FAR_Q, FAR_K), far, dims.blocks, dims.far, lax.rem(far, 2) == 1)
-    plan_ref[COUNTS, 0] = lax.div(far, 2)
+    words = []
+    for key_ids in (far_ids, own_ids):
+        for query_id in own_ids:
+            word = jnp.int32(0)
+            for index, key_id in enumerate(key_ids):
+                seen = jnp.logical_and(key_id < query_id, mask_ref[seq, query_id, key_id] == 1)
+                word += jnp.where(seen, 1 << index, 0)
+            words.append(word)
+    for row, word in enumerate(words):
+        bits_ref[row:row + 1, :] = jnp.full((1, bits_ref.shape[1]), word, jnp.int32)
+    return words
+
+
+def append(plan_ref, rows, total, query_slot, key_slot, seen):
+    plan_ref[rows[0], total] = query_slot
+    plan_ref[rows[1], total] = key_slot
+    return total + jnp.asarray(seen).astype(jnp.int32)
+
+
+def list_own(dims, words, plan_ref):
+    total = jnp.int32(0)
+    for query_slot, word in enumerate(words[dims.blocks:]):
+        for key_slot in range(dims.blocks):
+            if key_slot != query_slot:
+                seen = lax.rem(lax.shift_right_logical(word, key_slot), 2) == 1
+                total = append(plan_ref, (OWN_Q, OWN_K), total, query_slot, key_slot, seen)
+    append(plan_ref, (OWN_Q, OWN_K), total, dims.blocks, dims.blocks, True)
+    return lax.div(total + 1, 2)
+
+
+def list_far(dims, words, plan_ref):
+    total = jnp.int32(0)
+    for query_slot, word in enumerate(words[:dims.blocks]):
+        for key_slot in range(dims.far):
+            seen = lax.rem(lax.shift_right_logical(word, key_slot), 2) == 1
+            total = append(plan_ref, (FAR_Q, FAR_K), total, query_slot, key_slot, seen)
+        total = append(plan_ref, (FAR_Q, FAR_K), total, dims.blocks, dims.far, lax.rem(total, 2) == 1)
+    return lax.div(total, 2)
+
+
+def read_words(dims, bits_ref):
+    return [bits_ref[row, 0] for row in range(2 * dims.blocks)]
 
 
 def two_at_once(count, front, back):
@@ -150,9 +168,9 @@
 
 def own_stats_kernel(
     dims, pos_hbm, mask_hbm, q_hbm, g_hbm, k_hbm, v_hbm,
-    stats_ref, plan_ref, q_ref, g_ref, k_ref, v_ref, qt_ref, gt_ref,
+    stats_ref, bits_ref, q_ref, g_ref, k_ref, v_ref, qt_ref, gt_ref,
     logit_ref, dprob_ref,
-    pos_ref, mask_ref, sums, whole_sems, slot_sems,
+    plan_ref, pos_ref, mask_ref, sums, whole_sems, slot_sems,
 ):
     factor = dims.scale * LOG2E
     whole = [
@@ -179,7 +197,7 @@
             copy.start()
     whole[0].wait()
     whole[1].wait()
-    build_plan(dims, pos_ref, mask_ref, plan_ref)
+    count = list_own(dims, seen_words(dims, pos_ref, mask_ref, bits_ref), plan_ref)
     whole[2].wait()
     whole[3].wait()
 
@@ -206,19 +224,18 @@
         slot = plan_ref[OWN_Q, pair]
         store_stats(sums, slot, merged(load_stats(sums, slot), stats))
 
-    two_at_once(plan_ref[COUNTS, 1], front, back)
+    two_at_once(count, front, back)
     stats_ref[...] = sums[0:dims.blocks]
 
 
 def far_kernel(
-    dims, plan_hbm, q_ref, g_ref, qt_ref, gt_ref, near_ref, swap_ref, stats_ref,
+    dims, bits_ref, q_ref, g_ref, qt_ref, gt_ref, near_ref, swap_ref, stats_ref,
     final_ref, ds_ref, keep_ref, send_ref,
-    plan_ref, plan_sem, k_all, v_all, run, logit_all, dprob_all, dk_all, dv_all,
+    plan_ref, k_all, v_all, run, logit_all, dprob_all, dk_all, dv_all,
 ):
     factor = dims.scale * LOG2E
     first_core = lax.rem(lax.axis_index("head"), 2) == 0
-    load_plan = pltpu.make_async_copy(plan_hbm, plan_ref, plan_sem)
-    load_plan.start()
+    words = read_words(dims, bits_ref)
 
     @pl.when(first_core)
     def _():
@@ -233,8 +250,7 @@
     dk_all[...] = jnp.zeros_like(dk_all)
     dv_all[...] = jnp.zeros_like(dv_all)
     run[0:dims.blocks] = stats_ref[...]
-    load_plan.wait()
-    count = plan_ref[COUNTS, 0]
+    count = list_far(dims, words, plan_ref)
 
     def kept(step):
         return step if dims.keep_tiles else 0
@@ -345,14 +361,13 @@
 
 
 def own_sums_kernel(
-    dims, plan_hbm, q_ref, g_ref, final_ref, logit_ref, dprob_ref,
+    dims, bits_ref, q_ref, g_ref, final_ref, logit_ref, dprob_ref,
     keep_ref, send_ref, ds_ref,
-    plan_ref, plan_sem, dk_all, dv_all,
+    plan_ref, dk_all, dv_all,
 ):
     factor = dims.scale * LOG2E
     first_core = lax.rem(lax.axis_index("head"), 2) == 0
-    load_plan = pltpu.make_async_copy(plan_hbm, plan_ref, plan_sem)
-    load_plan.start()
+    words = read_words(dims, bits_ref)
 
     def front(index, query_slot):
         probs, dscore = gradient_tiles(
@@ -366,7 +381,7 @@
 
     for slot in range(dims.blocks):
         dk_all[slot], dv_all[slot] = front(slot, slot)
-    load_plan.wait()
+    count = list_own(dims, words, plan_ref)
 
     def own_front(pair):
         return front(dims.blocks + pair, jnp.minimum(plan_ref[OWN_Q, pair], dims.blocks - 1))
@@ -375,18 +390,17 @@
         dk_all[plan_ref[OWN_K, pair]] += sums[0]
         dv_all[plan_ref[OWN_K, pair]] += sums[1]
 
-    two_at_once(plan_ref[COUNTS, 1], own_front, own_back)
+    two_at_once(count, own_front, own_back)
     share_out(dims, dims.blocks, first_core, dk_all, dv_all, keep_ref, send_ref)
 
 
 def own_queries_kernel(
-    dims, plan_hbm, k_ref, near_ref, swap_ref, own_ds_ref,
+    dims, bits_ref, k_ref, near_ref, swap_ref, own_ds_ref,
     dq_ref, kt_far,
-    plan_ref, plan_sem, kt_own,
+    plan_ref, kt_own,
 ):
     first_core = lax.rem(lax.axis_index("head"), 2) == 0
-    load_plan = pltpu.make_async_copy(plan_hbm, plan_ref, plan_sem)
-    load_plan.start()
+    words = read_words(dims, bits_ref)
     for index in range(dims.blocks):
         kt_own[index] = k_ref[index * BLK:(index + 1) * BLK, :].T
 
@@ -402,7 +416,7 @@
 
     for slot in range(dims.blocks):
         dq_ref[slot] = dot_nn(kt_own[slot], own_ds_ref[slot])
-    load_plan.wait()
+    count = list_own(dims, words, plan_ref)
 
     def own_front(pair):
         key_slot = jnp.minimum(plan_ref[OWN_K, pair], dims.blocks - 1)
@@ -411,18 +425,17 @@
     def own_back(pair, part):
         dq_ref[plan_ref[OWN_Q, pair]] += part
 
-    two_at_once(plan_ref[COUNTS, 1], own_front, own_back)
+    two_at_once(count, own_front, own_back)
 
 
 def queries_kernel(
-    dims, plan_hbm, kt_far, far_ds_ref, dq_own_ref,
+    dims, bits_ref, kt_far, far_ds_ref, dq_own_ref,
     dq_hbm,
-    plan_ref, plan_sem, dq_all, dq_out, dq_sems,
+    plan_ref, dq_all, dq_out, dq_sems,
 ):
-    load_plan = pltpu.make_async_copy(plan_hbm, plan_ref, plan_sem)
-    load_plan.start()
+    words = read_words(dims, bits_ref)
     dq_all[...] = dq_own_ref[0:dims.blocks]
-    load_plan.wait()
+    count = list_far(dims, words, plan_ref)
 
     def far_trip(step, carry):
         slot = jnp.minimum(plan_ref[FAR_Q, 2 * step], dims.blocks - 1)
@@ -437,7 +450,7 @@
         dq_all[slot] += parts[0] + jnp.where(real, parts[1], 0.0)
         return carry
 
-    lax.fori_loop(0, plan_ref[COUNTS, 0], far_trip, 0)
+    lax.fori_loop(0, count, far_trip, 0)
 
     copies = []
     for slot in range(dims.blocks):
@@ -550,12 +563,12 @@
 
     own_pairs = blocks + blocks * (blocks - 1) // 2 + 1
     (
-        stats, plan, query_rows, grad_rows, key_own, value_own, query_cols, grad_cols, own_logits, own_dprobs,
+        stats, bits, query_rows, grad_rows, key_own, value_own, query_cols, grad_cols, own_logits, own_dprobs,
     ) = pl.pallas_call(
         functools.partial(own_stats_kernel, dims),
         out_shape=(
             sds((blocks, 3, SUB, rows), f32),
-            sds(PLAN, jnp.int32),
+            sds((2 * blocks, 128), jnp.int32),
             sds((tokens * heads, depth), bf16),
             sds((tokens * heads, depth), bf16),
             sds((tokens, depth), bf16),
@@ -566,8 +579,9 @@
             sds((own_pairs, BLK, rows), f32),
         ),
         in_specs=[HBM] * 6,
-        out_specs=(VMEM, SMEM) + (VMEM,) * 8,
+        out_specs=(VMEM,) * 10,
         scratch_shapes=[
+            pltpu.SMEM(PLAN, jnp.int32),
             pltpu.SMEM(block_pos.shape, jnp.int32),
             pltpu.SMEM(block_mask.shape, jnp.int32),
             pltpu.VMEM((blocks + 1, 3, SUB, rows), f32),
@@ -599,7 +613,6 @@
         out_specs=(VMEM,) * 4,
         scratch_shapes=[
             pltpu.SMEM(PLAN, jnp.int32),
-            pltpu.SemaphoreType.DMA,
             pltpu.VMEM((far * BLK, depth), bf16),
             pltpu.VMEM((far * BLK, depth), bf16),
             pltpu.VMEM((blocks + 1, 3, SUB, rows), f32),
@@ -611,7 +624,7 @@
         compiler_params=params,
         cost_estimate=cost(blocks * far, 4),
         name="far_part",
-    )(plan, query_rows, grad_rows, query_cols, grad_cols, near, swap, stats)
+    )(bits, query_rows, grad_rows, query_cols, grad_cols, near, swap, stats)
 
     keep_own, send_own, own_scores = pl.pallas_call(
         functools.partial(own_sums_kernel, dims),
@@ -624,14 +637,13 @@
         out_specs=(VMEM,) * 3,
         scratch_shapes=[
             pltpu.SMEM(PLAN, jnp.int32),
-            pltpu.SemaphoreType.DMA,
             pltpu.VMEM((blocks + 1, BLK, depth), f32),
             pltpu.VMEM((blocks + 1, BLK, depth), f32),
         ],
         compiler_params=params,
         cost_estimate=cost(blocks * blocks, 2),
         name="own_sums",
-    )(plan, query_rows, grad_rows, final, own_logits, own_dprobs)
+    )(bits, query_rows, grad_rows, final, own_logits, own_dprobs)
 
     dq_own, far_cols = pl.pallas_call(
         functools.partial(own_queries_kernel, dims),
@@ -640,13 +652,12 @@
         out_specs=(VMEM,) * 2,
         scratch_shapes=[
             pltpu.SMEM(PLAN, jnp.int32),
-            pltpu.SemaphoreType.DMA,
             pltpu.VMEM((blocks, depth, BLK), bf16),
         ],
         compiler_params=params,
         cost_estimate=cost(blocks * blocks, 1),
         name="own_queries",
-    )(plan, key_own, near, swap, own_scores)
+    )(bits, key_own, near, swap, own_scores)
 
     dq = pl.pallas_call(
         functools.partial(queries_kernel, dims),
@@ -655,7 +666,6 @@
         out_specs=HBM,
         scratch_shapes=[
             pltpu.SMEM(PLAN, jnp.int32),
-            pltpu.SemaphoreType.DMA,
             pltpu.VMEM((blocks, depth, rows), f32),
             pltpu.VMEM((tokens * heads, depth), bf16),
             pltpu.SemaphoreType.DMA((blocks,)),
@@ -663,7 +673,7 @@
         compiler_params=params,
         cost_estimate=cost(blocks * far, 1),
         name="queries",
-    )(plan, far_cols, far_scores, dq_own)
+    )(bits, far_cols, far_scores, dq_own)
 
     cuts = (0, tokens * 5 // 8, tokens)
     travel = bf16 if members == 2 else f32

time: 38.7 us -> 37.7 us (0.974)
  Pallas kernels: 12.7 us -> 11.5 us
    pallas_call x1, Pallas kernels: 2.63 us -> 2.14 us  [per_device(): pl.pallas_call(functools.partial(far_kernel, dims), out_shape=(sds((block...]
    pallas_call x1, Pallas kernels: 2.4 us -> 1.92 us  [per_device(): pl.pallas_call(functools.partial(queries_kernel, dims), out_shape=sds((to...]
  transfers between devices with their start and end apart: 10 -> 10, of which waited for: 4 -> 4; matrix products, arithmetic and copies ran while one was open for 0% -> 0% of each run, Pallas kernels for 22% -> 21%
where the time goes in v6:
time: 37.7 us; the launch traced here: 37.2 us
  waiting for transfers between devices  14.7 us (39%)
  Pallas kernels  11.5 us (31%)
  starting transfers between devices  10.1 us (27%)
  between operations  0.77 us (2%)
    ppermute x3, waiting for transfers between devices, shifted(): lax.ppermute(value, axis, [(i, (i + steps) % count) for i in range(count)])  11.2 us
    ppermute x3, starting transfers between devices, shifted(): lax.ppermute(value, axis, [(i, (i + steps) % count) for i in range(count)])  7.11 us
    pallas_call x1, Pallas kernels, per_device(): pl.pallas_call(functools.partial(own_stats_kernel, dims), out_shape=(sds(...  3.77 us
    ppermute x7, waiting for transfers between devices, swapped(): return lax.ppermute(value, axis, [(i, i ^ bit) for i in range(count)])  3.5 us
    ppermute x7, starting transfers between devices, swapped(): return lax.ppermute(value, axis, [(i, i ^ bit) for i in range(count)])  2.97 us
    pallas_call x1, Pallas kernels, per_device(): pl.pallas_call(functools.partial(far_kernel, dims), out_shape=(sds((block...  2.14 us
    pallas_call x1, Pallas kernels, per_device(): pl.pallas_call(functools.partial(queries_kernel, dims), out_shape=sds((to...  1.92 us
    pallas_call x1, Pallas kernels, per_device(): pl.pallas_call(functools.partial(own_sums_kernel, dims), out_shape=(sds((...  1.16 us
  transfers between devices with their start and end apart: 10, of which 4 were waited for; matrix products, arithmetic and copies ran while one was open for 0% of the time, Pallas kernels for 21%

profile of v6, /device:TPU:0, one launch (start us, length us, event | category | flops | bytes accessed | tf_op | source)
XLA Modules:
  0.0 37.2 jit_solution(3742932116782250758)
XLA Ops:
  0.6 0.9 %pick.1 = bf16[512,128]{1,0:T(8,128)(2,1)S(1)} custom-call(bf16[512,128]{1,0:T(8,128)(2,1)} %bitcast.8, bf16[512,128]{1,0:T(8,128)(2,1)} %bitcast.10), custom_call_target="tpu_custom_call" | custom-call | tf_op jit(solution)/shard_map/pick/pallas_call | solution.py:536
  1.6 4.1 %collective-permute-start = (bf16[512,128]{1,0:T(8,128)(2,1)S(1)}, bf16[512,128]{1,0:T(8,128)(2,1)S(1)}, u32[]{:S(2)}, u32[]{:S(2)}) collective-permute-start(bf16[512,128]{1,0:T(8,128)(2,1)S(1)} %pick.1), channel_id=1, source_target_pairs={{0,16},{4,20},{8,24},{12,28},{16,0},{20,4},{24,8},{28,12},{1,17},{... | collective-permute-start | bytes 393224 | tf_op jit(solution)/shard_map/ppermute | solution.py:40
  5.7 6.3 %collective-permute-done.near_ref = bf16[512,128]{1,0:T(8,128)(2,1)S(1)} collective-permute-done((bf16[512,128]{1,0:T(8,128)(2,1)S(1)}, bf16[512,128]{1,0:T(8,128)(2,1)S(1)}, u32[]{:S(2)}, u32[]{:S(2)}) %collective-permute-start) | collective-permute-done | bytes 131104 | tf_op jit(solution)/shard_map/ppermute | solution.py:40
  12.0 0.0 collective-permute-start.1
  12.0 3.8 %own_stats.1 = (f32[4,3,8,512]{3,2,1,0:T(8,128)S(1)}, s32[8,128]{1,0:T(8,128)S(1)}, bf16[2048,128]{1,0:T(8,128)(2,1)S(1)}, bf16[2048,128]{1,0:T(8,128)(2,1)S(1)}...) custom-call(s32[4,8]{1,0:T(4,128)} %pos_hbm.1, ...), custom_call_target="tpu_custom_call" | custom-call | flops 536870912 | bytes 1048576 | tf_op jit(solution)/shard_map/own_stats/pallas_call | solution.py:567
  15.8 0.0 collective-permute-done.1.swap_ref
  15.8 2.1 %far_part.1 = (f32[4,2,8,512]{3,2,1,0:T(8,128)S(1)}, bf16[8,256,512]{2,1,0:T(8,128)(2,1)S(1)}, f32[512,128]{1,0:T(8,128)S(1)}, bf16[512,128]{1,0:T(8,128)(2,1)S(1)}) custom-call(s32[8,128]{1,0:T(8,128)S(1)} %get-tuple-element.23.bits_ref, bf16[2048,128]{1,0:T(8,128)(2,1)S(1)} %get-tuple-element.25.q_ref, bf16[2048,128]{1,0:T(8,128)(2,1)S(1)} %get-tuple-element.26.g_ref, ...), custom_call_target="tpu_custom_call" | custom-call | flops 1073741824 | bytes 1048576 | tf_op jit(solution)/shard_map/far_part/pallas_call | solution.py:604
  17.9 0.6 %collective-permute-start.2 = (bf16[512,128]{1,0:T(8,128)(2,1)S(1)}, bf16[512,128]{1,0:T(8,128)(2,1)S(1)}, u32[]{:S(2)}, u32[]{:S(2)}) collective-permute-start(bf16[512,128]{1,0:T(8,128)(2,1)S(1)} %get-tuple-element.38), channel_id=1, source_target_pairs={{0,1},{1,0},{2,3},{3,2},{4,5},{5,4},{6,7},{7,6},{8,9},{9,8},{10,11... | collective-permute-start | bytes 393224 | tf_op jit(solution)/shard_map/ppermute | solution.py:45
  18.5 1.2 %own_sums.1 = (f32[512,128]{1,0:T(8,128)S(1)}, bf16[512,128]{1,0:T(8,128)(2,1)S(1)}, bf16[11,128,512]{2,1,0:T(8,128)(2,1)S(1)}) custom-call(s32[8,128]{1,0:T(8,128)S(1)} %get-tuple-element.23.bits_ref, bf16[2048,128]{1,0:T(8,128)(2,1)S(1)} %get-tuple-element.25.q_ref, bf16[2048,128]{1,0:T(8,128)(2,1)S(1)} %get-tuple-element.26.g_ref, ...), custom_call_target="tpu_custom_call" | custom-call | flops 536870912 | bytes 1048576 | tf_op jit(solution)/shard_map/own_sums/pallas_call | solution.py:629
  19.7 0.1 collective-permute-start.4
  19.8 0.0 collective-permute-done.2
  19.9 0.1 collective-permute-start.6
  19.9 2.9 %collective-permute-start.3 = (bf16[320,128]{1,0:T(8,128)(2,1)S(1)}, bf16[320,128]{1,0:T(8,128)(2,1)S(1)}, u32[]{:S(2)}, u32[]{:S(2)}) collective-permute-start(bf16[320,128]{1,0:T(8,128)(2,1)S(1)} %slice.18), channel_id=1, source_target_pairs={{0,16},{4,20},{8,24},{12,28},{16,0},{20,4},{24,8},{28,12},{1,17},{... | collective-permute-start | bytes 245768 | tf_op jit(solution)/shard_map/ppermute | solution.py:40
  22.8 0.0 collective-permute-done.4
  22.9 4.9 %collective-permute-done.3 = bf16[320,128]{1,0:T(8,128)(2,1)S(1)} collective-permute-done((bf16[320,128]{1,0:T(8,128)(2,1)S(1)}, bf16[320,128]{1,0:T(8,128)(2,1)S(1)}, u32[]{:S(2)}, u32[]{:S(2)}) %collective-permute-start.3) | collective-permute-done | bytes 81952 | tf_op jit(solution)/shard_map/ppermute | solution.py:40
  27.8 1.6 %collective-permute-start.5 = (bf16[320,128]{1,0:T(8,128)(2,1)S(1)}, bf16[320,128]{1,0:T(8,128)(2,1)S(1)}, u32[]{:S(2)}, u32[]{:S(2)}) collective-permute-start(bf16[320,128]{1,0:T(8,128)(2,1)S(1)} %fusion), channel_id=1, source_target_pairs={{0,2},{1,3},{2,0},{3,1},{4,6},{5,7},{6,4},{7,5},{8,10},{9,11},{10,... | collective-permute-start | bytes 245768 | tf_op jit(solution)/shard_map/ppermute | solution.py:45
  29.4 0.0 collective-permute-done.6
  29.4 0.6 %collective-permute-start.7 = (bf16[192,128]{1,0:T(8,128)(2,1)S(1)}, bf16[192,128]{1,0:T(8,128)(2,1)S(1)}, u32[]{:S(2)}, u32[]{:S(2)}) collective-permute-start(bf16[192,128]{1,0:T(8,128)(2,1)S(1)} %fusion.1), channel_id=1, source_target_pairs={{0,2},{1,3},{2,0},{3,1},{4,6},{5,7},{6,4},{7,5},{8,10},{9,11},{10,... | collective-permute-start | bytes 147464 | tf_op jit(solution)/shard_map/ppermute | solution.py:45
  30.0 2.9 %collective-permute-done.5 = bf16[320,128]{1,0:T(8,128)(2,1)S(1)} collective-permute-done((bf16[320,128]{1,0:T(8,128)(2,1)S(1)}, bf16[320,128]{1,0:T(8,128)(2,1)S(1)}, u32[]{:S(2)}, u32[]{:S(2)}) %collective-permute-start.5) | collective-permute-done | bytes 81952 | tf_op jit(solution)/shard_map/ppermute | solution.py:45
  32.8 0.1 collective-permute-start.8
  32.9 0.6 %collective-permute-done.7 = bf16[192,128]{1,0:T(8,128)(2,1)S(1)} collective-permute-done((bf16[192,128]{1,0:T(8,128)(2,1)S(1)}, bf16[192,128]{1,0:T(8,128)(2,1)S(1)}, u32[]{:S(2)}, u32[]{:S(2)}) %collective-permute-start.7) | collective-permute-done | bytes 49184 | tf_op jit(solution)/shard_map/ppermute | solution.py:45
  33.6 0.1 collective-permute-start.9
  33.7 0.9 %own_queries.1 = (f32[5,128,512]{2,1,0:T(8,128)S(1)}, bf16[4,128,128]{2,1,0:T(8,128)(2,1)S(1)}) custom-call(s32[8,128]{1,0:T(8,128)S(1)} %get-tuple-element.23.bits_ref, bf16[512,128]{1,0:T(8,128)(2,1)S(1)} %get-tuple-element.24.k_ref, bf16[512,128]{1,0:T(8,128)(2,1)S(1)} %collective-permute-done.near_ref, ...), custom_call_target="tpu_custom_call" | custom-call | flops 268435456 | bytes 1048576 | tf_op jit(solution)/shard_map/own_queries/pallas_call | solution.py:648
  34.6 1.9 %queries.1 = bf16[2048,128]{1,0:T(8,128)(2,1)} custom-call(s32[8,128]{1,0:T(8,128)S(1)} %get-tuple-element.23.bits_ref, bf16[4,128,128]{2,1,0:T(8,128)(2,1)S(1)} %get-tuple-element.34.kt_far, bf16[8,256,512]{2,1,0:T(8,128)(2,1)S(1)} %get-tuple-element.35.far_ds_ref, f32[5,128,512]{2,1,0:T(8,128)S(1)} %get-tuple-element.36.dq_own_ref), custom_call_target="tpu_custom_call" | custom-call | flops 268435456 | bytes 1048576 | tf_op jit(solution)/shard_map/queries/pallas_call | solution.py:662
  36.5 0.0 collective-permute-done.9.refs_3_
  36.5 0.0 collective-permute-done.8.refs_2_
  36.5 0.7 %place.1 = (bf16[512,128]{1,0:T(8,128)(2,1)}, bf16[512,128]{1,0:T(8,128)(2,1)}) custom-call(bf16[320,128]{1,0:T(8,128)(2,1)S(1)} %add_convert_fusion.1.refs_0_, bf16[192,128]{1,0:T(8,128)(2,1)S(1)} %add_convert_fusion.2.refs_1_, bf16[320,128]{1,0:T(8,128)(2,1)S(1)} %collective-permute-done.8.refs_2_, bf16[192,128]{1,0:T(8,128)(2,1)S(1)} %collective-permute-done.9.refs_3_), custom_call_target="tpu_custom_call" | custom-call | tf_op jit(solution)/shard_map/place/pallas_call | solution.py:703
  (8 shorter events, 0.2 us)
Async XLA Ops:
  1.6 10.4 %collective-permute-start = (bf16[512,128]{1,0:T(8,128)(2,1)S(1)}, bf16[512,128]{1,0:T(8,128)(2,1)S(1)}, u32[]{:S(2)}, u32[]{:S(2)}) collective-permute-start(bf16[512,128]{1,0:T(8,128)(2,1)S(1)} %pick.1), channel_id=1, source_target_pairs={{0,16},{4,20},{8,24},{12,28},{16,0},{20,4},{24,8},{28,12},{1,17},{... | collective-permute-start | bytes 393224 | tf_op jit(solution)/shard_map/ppermute | solution.py:40
  12.0 3.8 %collective-permute-start.1 = (bf16[512,128]{1,0:T(8,128)(2,1)S(1)}, bf16[512,128]{1,0:T(8,128)(2,1)S(1)}, u32[]{:S(2)}, u32[]{:S(2)}) collective-permute-start(bf16[512,128]{1,0:T(8,128)(2,1)S(1)} %collective-permute-done.near_ref), channel_id=1, source_target_pairs={{0,1},{1,0},{2,3},{3,2},{4,5},{5,4},{6,7},{7,6},{8,9},{9,8},{10,11... | collective-permute-start | bytes 393224 | tf_op jit(solution)/shard_map/ppermute | solution.py:45
  17.9 1.8 %collective-permute-start.2 = (bf16[512,128]{1,0:T(8,128)(2,1)S(1)}, bf16[512,128]{1,0:T(8,128)(2,1)S(1)}, u32[]{:S(2)}, u32[]{:S(2)}) collective-permute-start(bf16[512,128]{1,0:T(8,128)(2,1)S(1)} %get-tuple-element.38), channel_id=1, source_target_pairs={{0,1},{1,0},{2,3},{3,2},{4,5},{5,4},{6,7},{7,6},{8,9},{9,8},{10,11... | collective-permute-start | bytes 393224 | tf_op jit(solution)/shard_map/ppermute | solution.py:45
  19.7 3.1 %collective-permute-start.4 = (bf16[512,128]{1,0:T(8,128)(2,1)S(1)}, bf16[512,128]{1,0:T(8,128)(2,1)S(1)}, u32[]{:S(2)}, u32[]{:S(2)}) collective-permute-start(bf16[512,128]{1,0:T(8,128)(2,1)S(1)} %get-tuple-element.40), channel_id=1, source_target_pairs={{0,1},{1,0},{2,3},{3,2},{4,5},{5,4},{6,7},{7,6},{8,9},{9,8},{10,11... | collective-permute-start | bytes 393224 | tf_op jit(solution)/shard_map/ppermute | solution.py:45
  19.9 9.5 %collective-permute-start.6 = (bf16[192,128]{1,0:T(8,128)(2,1)S(1)}, bf16[192,128]{1,0:T(8,128)(2,1)S(1)}, u32[]{:S(2)}, u32[]{:S(2)}) collective-permute-start(bf16[192,128]{1,0:T(8,128)(2,1)S(1)} %slice.20), channel_id=1, source_target_pairs={{0,16},{4,20},{8,24},{12,28},{16,0},{20,4},{24,8},{28,12},{1,17},{... | collective-permute-start | bytes 147464 | tf_op jit(solution)/shard_map/ppermute | solution.py:40
  19.9 7.8 %collective-permute-start.3 = (bf16[320,128]{1,0:T(8,128)(2,1)S(1)}, bf16[320,128]{1,0:T(8,128)(2,1)S(1)}, u32[]{:S(2)}, u32[]{:S(2)}) collective-permute-start(bf16[320,128]{1,0:T(8,128)(2,1)S(1)} %slice.18), channel_id=1, source_target_pairs={{0,16},{4,20},{8,24},{12,28},{16,0},{20,4},{24,8},{28,12},{1,17},{... | collective-permute-start | bytes 245768 | tf_op jit(solution)/shard_map/ppermute | solution.py:40
  27.8 5.0 %collective-permute-start.5 = (bf16[320,128]{1,0:T(8,128)(2,1)S(1)}, bf16[320,128]{1,0:T(8,128)(2,1)S(1)}, u32[]{:S(2)}, u32[]{:S(2)}) collective-permute-start(bf16[320,128]{1,0:T(8,128)(2,1)S(1)} %fusion), channel_id=1, source_target_pairs={{0,2},{1,3},{2,0},{3,1},{4,6},{5,7},{6,4},{7,5},{8,10},{9,11},{10,... | collective-permute-start | bytes 245768 | tf_op jit(solution)/shard_map/ppermute | solution.py:45
  29.4 4.2 %collective-permute-start.7 = (bf16[192,128]{1,0:T(8,128)(2,1)S(1)}, bf16[192,128]{1,0:T(8,128)(2,1)S(1)}, u32[]{:S(2)}, u32[]{:S(2)}) collective-permute-start(bf16[192,128]{1,0:T(8,128)(2,1)S(1)} %fusion.1), channel_id=1, source_target_pairs={{0,2},{1,3},{2,0},{3,1},{4,6},{5,7},{6,4},{7,5},{8,10},{9,11},{10,... | collective-permute-start | bytes 147464 | tf_op jit(solution)/shard_map/ppermute | solution.py:45
  32.8 3.6 %collective-permute-start.8 = (bf16[320,128]{1,0:T(8,128)(2,1)S(1)}, bf16[320,128]{1,0:T(8,128)(2,1)S(1)}, u32[]{:S(2)}, u32[]{:S(2)}) collective-permute-start(bf16[320,128]{1,0:T(8,128)(2,1)S(1)} %add_convert_fusion.1.refs_0_), channel_id=1, source_target_pairs={{0,1},{1,0},{2,3},{3,2},{4,5},{5,4},{6,7},{7,6},{8,9},{9,8},{10,11... | collective-permute-start | bytes 245768 | tf_op jit(solution)/shard_map/ppermute | solution.py:45
  33.6 2.9 %collective-permute-start.9 = (bf16[192,128]{1,0:T(8,128)(2,1)S(1)}, bf16[192,128]{1,0:T(8,128)(2,1)S(1)}, u32[]{:S(2)}, u32[]{:S(2)}) collective-permute-start(bf16[192,128]{1,0:T(8,128)(2,1)S(1)} %add_convert_fusion.2.refs_1_), channel_id=1, source_target_pairs={{0,1},{1,0},{2,3},{3,2},{4,5},{5,4},{6,7},{7,6},{8,9},{9,8},{10,11... | collective-permute-start | bytes 147464 | tf_op jit(solution)/shard_map/ppermute | solution.py:45
